TPU v7x, 256 devices: a whole 4x4x8 slice. The times are simulated.
256 devices in a mesh: seq: 16 (over z, core), head: 16 (over x, y).
Axes of the slice: x: 4, y: 4, z: 8, core: 2. Of those that a mesh axis runs over, the one named last changes fastest.
Arguments:
- queries: bfloat16 [12288, 2048], P('seq', 'head'), may hold values from -8 to 8
- enc_keys: bfloat16 [32768, 2048], P('seq', 'head'), may hold values from -8 to 8
- enc_values: bfloat16 [32768, 2048], P('seq', 'head'), may hold values from -6 to 6
- out_proj: bfloat16 [2048, 2048], P('head'), may hold values from -0.125 to 0.125
- out_grad: bfloat16 [12288, 2048], P(('seq', 'head')), may hold values from -24 to 24
- block_doc: int32 [256], replicated, may hold values from 0 to 127, as said below
- query_doc: int32 [12288], replicated, may hold values from 0 to 127, as said below
Outputs:
- mixed: bfloat16 [12288, 2048], P(('seq', 'head'))
- grad_q: bfloat16 [12288, 2048], P('seq', 'head')
- grad_k: bfloat16 [32768, 2048], P('seq', 'head')
- grad_v: bfloat16 [32768, 2048], P('seq', 'head')
- grad_wo: float32 [2048, 2048], P('head', 'seq')
Inputs may be any that keep to these rules, and one draw needn't show every extreme that they name: `block_doc`: never falls; each document's blocks are consecutive, lie on one sequence shard and number 1 to 3; each shard holds the blocks of exactly 8 documents. `query_doc`: every row belongs to a document; each document has 1 to 144 rows, all consecutive and on one sequence shard of 768 rows; each shard holds the rows of exactly 8 documents, and no two documents whose blocks lie on one shard have their rows on one shard.
All inputs are finite; a program needn't handle non-finite values.
Results may differ from a plain program's by a relative error of at most 0.023.
Values may be sent and summed in bfloat16 or wider, within the bound.
No kernel may reach another device: no remote copies, remote signals or barrier semaphores. Data moves between devices by JAX's collectives and lax.ppermute only.
A program may use at most 64 MiB of HBM per device.

v0:
```python
import jax
import jax.numpy as jnp
from jax import lax
from jax.sharding import PartitionSpec as P

HD = 64
BLOCK = 128
BLK = 16
DPS = 8
CAP = 3


score_scale = 0.125
masked_score = -1e30


def lookup(table, index):
    positions = jnp.arange(table.shape[0], dtype=jnp.int32)
    return jnp.sum(jnp.where(index[:, None] == positions[None, :], table[None, :], 0), axis=1)


def first_true(flags, wanted_count):
    order = jnp.cumsum(flags.astype(jnp.int32)) - 1
    wanted = jnp.arange(wanted_count, dtype=jnp.int32)
    matches = flags[None, :] & (order[None, :] == wanted[:, None])
    positions = jnp.arange(flags.shape[0], dtype=jnp.int32)
    return jnp.sum(jnp.where(matches, positions[None, :], 0), axis=1)


def rank_within(targets, shard_count):
    onehot = (targets[:, None] == jnp.arange(shard_count, dtype=jnp.int32)[None, :]).astype(
        jnp.int32
    )
    before = jnp.cumsum(onehot, axis=0) - onehot
    return jnp.sum(before * onehot, axis=1)


def attend(query_rows, grad_rows, query_docs, key_rows, value_rows, key_docs):
    row_count = query_rows.shape[0]
    heads_here = query_rows.shape[1] // HD
    key_total = key_rows.shape[0]
    key_width = min(256, key_total)
    blocks = key_total // key_width
    query_heads = query_rows.reshape(row_count, heads_here, HD)
    grad_heads = grad_rows.reshape(row_count, heads_here, HD)
    key_heads = key_rows.reshape(blocks, key_width, heads_here, HD)
    value_heads = value_rows.reshape(blocks, key_width, heads_here, HD)
    block_docs = key_docs.reshape(blocks, key_width)

    def scores_of(key_block, doc_block):
        raw_scores = (
            jnp.einsum("rhd,khd->rhk", query_heads, key_block, preferred_element_type=jnp.float32)
            * score_scale
        )
        admitted = (query_docs[:, None] == doc_block[None, :])[:, None, :]
        return (jnp.where(admitted, raw_scores, masked_score), admitted)

    def stats_step(carry, block_item):
        running_max, running_sum = carry
        key_block, doc_block = block_item
        scores, admitted = scores_of(key_block, doc_block)
        new_max = jnp.maximum(running_max, jnp.max(scores, axis=2))
        terms = jnp.where(admitted, jnp.exp(scores - new_max[:, :, None]), 0.0)
        running_sum = running_sum * jnp.exp(running_max - new_max) + jnp.sum(terms, axis=2)
        return ((new_max, running_sum), None)

    start_state = (
        jnp.full((row_count, heads_here), masked_score, jnp.float32),
        jnp.zeros((row_count, heads_here), jnp.float32),
    )
    (running_max, running_sum), _ = lax.scan(stats_step, start_state, (key_heads, block_docs))
    running_sum = jnp.where(running_sum > 0.0, running_sum, 1.0)
    logsum = running_max + jnp.log(running_sum)

    def probs_of(key_block, doc_block):
        scores, admitted = scores_of(key_block, doc_block)
        return jnp.where(admitted, jnp.exp(scores - logsum[:, :, None]), 0.0)

    def output_step(accumulated, block_item):
        key_block, value_block, doc_block = block_item
        weights = probs_of(key_block, doc_block).astype(jnp.bfloat16)
        return (
            accumulated
            + jnp.einsum("rhk,khd->rhd", weights, value_block, preferred_element_type=jnp.float32),
            None,
        )

    accumulated, _ = lax.scan(
        output_step,
        jnp.zeros((row_count, heads_here, HD), jnp.float32),
        (key_heads, value_heads, block_docs),
    )
    attended = accumulated.astype(jnp.bfloat16)
    row_delta = jnp.sum(grad_heads.astype(jnp.float32) * attended.astype(jnp.float32), axis=2)

    def grad_step(accumulated, block_item):
        key_block, value_block, doc_block = block_item
        probabilities = probs_of(key_block, doc_block)
        weights = probabilities.astype(jnp.bfloat16)
        dprobs = jnp.einsum(
            "rhd,khd->rhk", grad_heads, value_block, preferred_element_type=jnp.float32
        )
        dscores = (probabilities * (dprobs - row_delta[:, :, None])).astype(jnp.bfloat16)
        accumulated = accumulated + jnp.einsum(
            "rhk,khd->rhd", dscores, key_block, preferred_element_type=jnp.float32
        )
        key_grads = (
            jnp.einsum("rhk,rhd->khd", dscores, query_heads, preferred_element_type=jnp.float32)
            * score_scale
        ).astype(jnp.bfloat16)
        value_grads = jnp.einsum(
            "rhk,rhd->khd", weights, grad_heads, preferred_element_type=jnp.float32
        ).astype(jnp.bfloat16)
        return (accumulated, (key_grads, value_grads))

    accumulated, (key_grads, value_grads) = lax.scan(
        grad_step,
        jnp.zeros((row_count, heads_here, HD), jnp.float32),
        (key_heads, value_heads, block_docs),
    )
    query_grads = (accumulated * score_scale).astype(jnp.bfloat16)
    return (
        attended.reshape(row_count, -1),
        query_grads.reshape(row_count, -1),
        key_grads.reshape(key_total, -1),
        value_grads.reshape(key_total, -1),
    )


def shards(queries, enc_keys, enc_values, out_proj, out_grad, block_doc, query_doc):
    shard_count = lax.axis_size("seq")
    my_shard = lax.axis_index("seq")
    inner_here = queries.shape[1]
    query_total = queries.shape[0]
    key_total = enc_keys.shape[0]
    local_blocks = key_total // BLOCK
    doc_count = block_doc.shape[0] // BLK * DPS
    full_grad = lax.all_gather(out_grad, "head", axis=0, tiled=True)
    attn_grad = lax.dot_general(
        full_grad, out_proj, (((1,), (1,)), ((), ())), preferred_element_type=jnp.float32
    ).astype(jnp.bfloat16)
    doc_ids = jnp.arange(doc_count, dtype=jnp.int32)
    row_ids = jnp.arange(query_doc.shape[0], dtype=jnp.int32)
    doc_shard = jnp.max(
        jnp.where(query_doc[None, :] == doc_ids[:, None], row_ids[None, :] // query_total, -1),
        axis=1,
    )
    local_query_doc = lax.dynamic_slice_in_dim(query_doc, my_shard * query_total, query_total)
    block_ids = jnp.arange(block_doc.shape[0], dtype=jnp.int32)
    member = block_doc[None, :] == doc_ids[:, None]
    key_shard = jnp.max(jnp.where(member, block_ids[None, :] // local_blocks, -1), axis=1)
    block_counts = jnp.sum(member.astype(jnp.int32), axis=1)
    my_docs = lax.dynamic_slice_in_dim(block_doc, my_shard * local_blocks, local_blocks)
    block_dest = lookup(doc_shard, my_docs)
    send_slot = block_dest * CAP + rank_within(block_dest, shard_count)
    slot_total = shard_count * CAP
    send_keys = (
        jnp.zeros((slot_total, BLOCK, inner_here), jnp.bfloat16)
        .at[send_slot]
        .set(enc_keys.reshape(local_blocks, BLOCK, inner_here))
    )
    send_values = (
        jnp.zeros((slot_total, BLOCK, inner_here), jnp.bfloat16)
        .at[send_slot]
        .set(enc_values.reshape(local_blocks, BLOCK, inner_here))
    )
    got_keys, got_values = (
        lax.all_to_all(send_keys, "seq", split_axis=0, concat_axis=0, tiled=True),
        lax.all_to_all(send_values, "seq", split_axis=0, concat_axis=0, tiled=True),
    )
    owned_docs = first_true(doc_shard == my_shard, DPS)
    cap_range = jnp.arange(CAP, dtype=jnp.int32)
    source_slot = (lookup(key_shard, owned_docs)[:, None] * CAP + cap_range[None, :]).reshape(-1)
    live_slot = (cap_range[None, :] < lookup(block_counts, owned_docs)[:, None]).reshape(-1)
    slot_docs = jnp.where(live_slot, jnp.repeat(owned_docs, CAP), -2)
    token_docs = jnp.repeat(slot_docs, BLOCK)
    near_keys = got_keys[source_slot].reshape(-1, inner_here)
    near_values = got_values[source_slot].reshape(-1, inner_here)
    attended, grad_q, key_grads, value_grads = attend(
        queries, attn_grad, local_query_doc, near_keys, near_values, token_docs
    )
    back_keys = (
        jnp.zeros((slot_total, BLOCK, inner_here), jnp.bfloat16)
        .at[source_slot]
        .set(key_grads.reshape(-1, BLOCK, inner_here))
    )
    back_values = (
        jnp.zeros((slot_total, BLOCK, inner_here), jnp.bfloat16)
        .at[source_slot]
        .set(value_grads.reshape(-1, BLOCK, inner_here))
    )
    returned_keys, returned_values = (
        lax.all_to_all(back_keys, "seq", split_axis=0, concat_axis=0, tiled=True),
        lax.all_to_all(back_values, "seq", split_axis=0, concat_axis=0, tiled=True),
    )
    grad_k = returned_keys[send_slot].reshape(key_total, inner_here)
    grad_v = returned_values[send_slot].reshape(key_total, inner_here)
    mixed_out = lax.psum_scatter(
        jnp.dot(attended, out_proj, preferred_element_type=jnp.float32).astype(jnp.bfloat16),
        "head",
        scatter_dimension=0,
        tiled=True,
    )
    weight_part = lax.dot_general(
        attended, full_grad, (((0,), (0,)), ((), ())), preferred_element_type=jnp.float32
    )
    grad_wo = lax.psum_scatter(
        weight_part.astype(jnp.bfloat16), "seq", scatter_dimension=1, tiled=True
    ).astype(jnp.float32)
    return (mixed_out, grad_q, grad_k, grad_v, grad_wo)


def solution(mesh):
    placed = (
        P("seq", "head"),
        P("seq", "head"),
        P("seq", "head"),
        P("head", None),
        P(("seq", "head"), None),
        P(),
        P(),
    )
    return jax.shard_map(
        shards,
        mesh=mesh,
        in_specs=placed,
        out_specs=(
            P(("seq", "head"), None),
            P("seq", "head"),
            P("seq", "head"),
            P("seq", "head"),
            P("head", "seq"),
        ),
        check_vma=False,
    )
```

profile of v0, /device:TPU:1, one launch (start us, length us, event | category | flops | bytes accessed | tf_op | source)
XLA Modules:
  0.0 329.2 jit_solution(9185713792149519369)
XLA Ops:
  11.8 2.6 scatter_fusion.1
  14.3 10.1 %all-to-all-start.1 = ((bf16[48,128,128]{2,1,0:T(8,128)(2,1)}), bf16[48,128,128]{2,1,0:T(8,128)(2,1)S(1)}, u32[]{:S(2)}, u32[]{:S(2)}) async-start(bf16[48,128,128]{2,1,0:T(8,128)(2,1)} %scatter_fusion.1), calls=%async_computation.1 | async-start | bytes 3145728 | tf_op jit(solution)/shard_map/all_to_all | solution.py:168
  29.0 2.6 scatter_fusion
  31.5 31.4 %all-to-all-done.1 = bf16[48,128,128]{2,1,0:T(8,128)(2,1)S(1)} async-done(((bf16[48,128,128]{2,1,0:T(8,128)(2,1)}), bf16[48,128,128]{2,1,0:T(8,128)(2,1)S(1)}, u32[]{:S(2)}, u32[]{:S(2)}) %all-to-all-start.1) | async-done | bytes 1572896 | tf_op jit(solution)/shard_map/all_to_all | solution.py:168
  63.0 4.3 %all-to-all-start = ((bf16[48,128,128]{2,1,0:T(8,128)(2,1)}), bf16[48,128,128]{2,1,0:T(8,128)(2,1)}, u32[]{:S(2)}, u32[]{:S(2)}) async-start(bf16[48,128,128]{2,1,0:T(8,128)(2,1)} %scatter_fusion), calls=%async_computation | async-start | bytes 3145728 | tf_op jit(solution)/shard_map/all_to_all | solution.py:169
  69.7 13.4 %while.39 = (s32[]{:T(128)}, f32[768,2]{0,1:T(2,128)S(1)}, f32[768,2]{0,1:T(2,128)S(1)}, s32[768]{0:T(1024)S(1)}, s32[12,256]{1,0:T(8,128)S(1)}, /*index=5*/bf16...) while((s32[]{:T(128)}, f32[768,2]{0,1:T(2,128)S(1)}, ...), condition=%wide.region_15.16_spmd.clone, body=%wide.region_12.15_spmd.clone.sunk | while | flops 52895232 | bytes 4083824 | solution.py:71
  84.0 21.7 %all-to-all-done = bf16[48,128,128]{2,1,0:T(8,128)(2,1)} async-done(((bf16[48,128,128]{2,1,0:T(8,128)(2,1)}), bf16[48,128,128]{2,1,0:T(8,128)(2,1)}, u32[]{:S(2)}, u32[]{:S(2)}) %all-to-all-start) | async-done | bytes 1572896 | tf_op jit(solution)/shard_map/all_to_all | solution.py:169
  105.7 2.1 gather_fusion
  108.6 2.6 copy.79
  111.2 23.1 %while.40 = (s32[]{:T(128)}, f32[768,2,64]{0,2,1:T(8,128)S(1)}, bf16[12,256,2,64]{1,3,2,0:T(8,128)(2,1)}, s32[768]{0:T(1024)S(1)}, s32[12,256]{1,0:T(8,128)S(1)}...) while((s32[]{:T(128)}, f32[768,2,64]{0,2,1:T(8,128)S(1)}, ...), condition=%wide.region_17.18_spmd.clone, body=%wide.region_16.17_spmd.clone.sunk | while | flops 103022592 | bytes 1520755 | solution.py:88
  134.4 3.2 multiply_reduce_fusion
  139.3 2.7 convolution_convert_fusion.1
  142.0 83.4 %while.41 = (s32[]{:T(128)}, f32[768,2,64]{0,2,1:T(8,128)}, bf16[12,256,2,64]{1,3,2,0:T(8,128)(2,1)}, bf16[12,256,2,64]{1,3,2,0:T(8,128)(2,1)}, bf16[12,256,2,64...) while((s32[]{:T(128)}, f32[768,2,64]{0,2,1:T(8,128)}, ...), condition=%wide.region_21.22_spmd.clone, body=%wide.region_20.21_spmd.clone.sunk | while | flops 255295488 | bytes 9392787 | solution.py:116
  173.6 2.0 fusion.117
  222.4 2.0 fusion.117
  225.4 3.4 %copy.93 = bf16[12,256,2,64]{3,2,1,0:T(2,128)(2,1)S(1)} copy(bf16[12,256,2,64]{1,3,2,0:T(8,128)(2,1)} %get-tuple-element.154) | data formatting | bytes 1572864 | tf_op jit(solution)/shard_map/reshape;reshape | solution.py:190
  231.1 4.6 %scatter_fusion.3 = bf16[48,128,128]{2,1,0:T(8,128)(2,1)} fusion(bf16[48,128,128]{2,1,0:T(8,128)(2,1)} %broadcast.249.clone.3, s32[24]{0:T(128)S(1)} %fusion.58, bf16[24,128,128]{2,1,0:T(8,128)(2,1)S(1)} %reshape.365), kind=kCustom, calls=%fused_computation.7 | custom fusion | bytes 2359392 | tf_op jit(solution)/shard_map/scatter | solution.py:190
  235.7 4.3 %all-to-all-start.3 = ((bf16[48,128,128]{2,1,0:T(8,128)(2,1)}), bf16[48,128,128]{2,1,0:T(8,128)(2,1)}, u32[]{:S(2)}, u32[]{:S(2)}) async-start(bf16[48,128,128]{2,1,0:T(8,128)(2,1)} %scatter_fusion.3), calls=%async_computation.4 | async-start | bytes 3145728 | tf_op jit(solution)/shard_map/all_to_all | solution.py:194
  240.0 3.5 %copy.92 = bf16[12,256,2,64]{3,2,1,0:T(2,128)(2,1)S(1)} copy(bf16[12,256,2,64]{1,3,2,0:T(8,128)(2,1)} %get-tuple-element.153) | data formatting | bytes 1572864 | tf_op jit(solution)/shard_map/reshape;reshape | solution.py:185
  245.8 4.5 %scatter_fusion.2 = bf16[48,128,128]{2,1,0:T(8,128)(2,1)} fusion(bf16[48,128,128]{2,1,0:T(8,128)(2,1)} %broadcast.249.clone.2, s32[24]{0:T(128)S(1)} %fusion.58, bf16[24,128,128]{2,1,0:T(8,128)(2,1)S(1)} %reshape.364), kind=kCustom, calls=%fused_computation.6 | custom fusion | bytes 2359392 | tf_op jit(solution)/shard_map/scatter | solution.py:185
  250.3 28.2 %all-to-all-done.3 = bf16[48,128,128]{2,1,0:T(8,128)(2,1)} async-done(((bf16[48,128,128]{2,1,0:T(8,128)(2,1)}), bf16[48,128,128]{2,1,0:T(8,128)(2,1)}, u32[]{:S(2)}, u32[]{:S(2)}) %all-to-all-start.3) | async-done | bytes 1572896 | tf_op jit(solution)/shard_map/all_to_all | solution.py:194
  278.6 4.1 %all-to-all-start.2 = ((bf16[48,128,128]{2,1,0:T(8,128)(2,1)}), bf16[48,128,128]{2,1,0:T(8,128)(2,1)S(1)}, u32[]{:S(2)}, u32[]{:S(2)}) async-start(bf16[48,128,128]{2,1,0:T(8,128)(2,1)} %scatter_fusion.2), calls=%async_computation.3 | async-start | bytes 3145728 | tf_op jit(solution)/shard_map/all_to_all | solution.py:193
  285.1 2.8 gather_fusion.3
  287.9 33.3 %all-to-all-done.2 = bf16[48,128,128]{2,1,0:T(8,128)(2,1)S(1)} async-done(((bf16[48,128,128]{2,1,0:T(8,128)(2,1)}), bf16[48,128,128]{2,1,0:T(8,128)(2,1)S(1)}, u32[]{:S(2)}, u32[]{:S(2)}) %all-to-all-start.2) | async-done | bytes 1572896 | tf_op jit(solution)/shard_map/all_to_all | solution.py:193
  (282 shorter events, 137.3 us)
Async XLA Ops:
  7.2 127.2 %copy-start = (bf16[128,2048]{1,0:T(8,128)(2,1)S(1)}, bf16[128,2048]{1,0:T(8,128)(2,1)}, u32[]{:S(2)}) copy-start(bf16[128,2048]{1,0:T(8,128)(2,1)} %param.16) | copy-start | bytes 1572868
  7.2 4.6 %copy-start.5 = (bf16[2048,128]{1,0:T(8,128)(2,1)S(1)}, bf16[2048,128]{1,0:T(8,128)(2,1)}, u32[]{:S(2)}) copy-start(bf16[2048,128]{1,0:T(8,128)(2,1)} %param.14) | copy-start | bytes 1572868
  14.3 11.4 %copy-start.8 = (s32[256]{0:T(256)S(1)}, s32[256]{0:T(256)}, u32[]{:S(2)}) copy-start(s32[256]{0:T(256)} %param.18) | copy-start | bytes 3076
  14.3 12.9 %copy-start.7 = (bf16[768,128]{1,0:T(8,128)(2,1)S(1)}, bf16[768,128]{1,0:T(8,128)(2,1)}, u32[]{:S(2)}) copy-start(bf16[768,128]{1,0:T(8,128)(2,1)} %param.13) | copy-start | bytes 589828
  14.3 48.6 %all-to-all-start.1 = ((bf16[48,128,128]{2,1,0:T(8,128)(2,1)}), bf16[48,128,128]{2,1,0:T(8,128)(2,1)S(1)}, u32[]{:S(2)}, u32[]{:S(2)}) async-start(bf16[48,128,128]{2,1,0:T(8,128)(2,1)} %scatter_fusion.1), calls=%async_computation.1 | async-start | bytes 3145728 | tf_op jit(solution)/shard_map/all_to_all | solution.py:168
  24.4 4.5 %copy-start.6 = (bf16[2048,128]{1,0:T(8,128)(2,1)S(1)}, bf16[2048,128]{1,0:T(8,128)(2,1)}, u32[]{:S(2)}) copy-start(bf16[2048,128]{1,0:T(8,128)(2,1)} %param.15) | copy-start | bytes 1572868
  24.4 109.9 %all-gather.2.cloned.1.call-start = ((), (), s32[]{:S(2)}) async-start(), calls=%async_computation.7 | async-start | bytes 3342336 | tf_op jit(solution)/shard_map/all_gather | solution.py:138
  63.0 42.8 %all-to-all-start = ((bf16[48,128,128]{2,1,0:T(8,128)(2,1)}), bf16[48,128,128]{2,1,0:T(8,128)(2,1)}, u32[]{:S(2)}, u32[]{:S(2)}) async-start(bf16[48,128,128]{2,1,0:T(8,128)(2,1)} %scatter_fusion), calls=%async_computation | async-start | bytes 3145728 | tf_op jit(solution)/shard_map/all_to_all | solution.py:169
  67.3 216.3 %reduce-scatter.7.cloned.1.call-start = ((), (), s32[]{:S(2)}) async-start(), calls=%async_computation.8 | async-start | bytes 557056
  83.1 0.9 copy-start.3
  108.6 2.6 copy-start.4
  134.4 3.3 copy-start.1
  139.2 183.4 %reduce-scatter.5.cloned.1.call-start = ((), (), s32[]{:S(2)}) async-start(), calls=%async_computation.6 | async-start | bytes 3342336 | tf_op jit(solution)/shard_map/reduce_scatter | solution.py:198
  235.7 42.9 %all-to-all-start.3 = ((bf16[48,128,128]{2,1,0:T(8,128)(2,1)}), bf16[48,128,128]{2,1,0:T(8,128)(2,1)}, u32[]{:S(2)}, u32[]{:S(2)}) async-start(bf16[48,128,128]{2,1,0:T(8,128)(2,1)} %scatter_fusion.3), calls=%async_computation.4 | async-start | bytes 3145728 | tf_op jit(solution)/shard_map/all_to_all | solution.py:194
  250.3 32.4 %copy-start.2 = (f32[768,2,64]{0,2,1:T(8,128)S(1)}, f32[768,2,64]{0,2,1:T(8,128)}, u32[]{:S(2)}) copy-start(f32[768,2,64]{0,2,1:T(8,128)} %get-tuple-element.152) | copy-start | bytes 1179652
  278.6 42.7 %all-to-all-start.2 = ((bf16[48,128,128]{2,1,0:T(8,128)(2,1)}), bf16[48,128,128]{2,1,0:T(8,128)(2,1)S(1)}, u32[]{:S(2)}, u32[]{:S(2)}) async-start(bf16[48,128,128]{2,1,0:T(8,128)(2,1)} %scatter_fusion.2), calls=%async_computation.3 | async-start | bytes 3145728 | tf_op jit(solution)/shard_map/all_to_all | solution.py:193
Sparse Core Ops, SparseCore 0:
  27.7 53.2 all-gather.1
  139.3 52.5 reduce-scatter.6
  196.2 81.7 reduce-scatter.4
where the time goes:
time: 332 us; the launch traced here: 329 us
  waiting for transfers between devices  115 us (35%)
  matrix products  114 us (34%)
  local copies, waits for them, and re-layouts  46.8 us (14%)
  starting transfers between devices  23 us (7%)
  other arithmetic  14.4 us (4%)
  between operations  14.1 us (4%)
    all_to_all x1, waiting for transfers between devices, shards(): lax.all_to_all(back_keys, 'seq', split_axis=0, concat_axis=0, tiled=True)  33.3 us
    all_to_all x1, waiting for transfers between devices, shards(): lax.all_to_all(send_keys, 'seq', split_axis=0, concat_axis=0, tiled=True)  31.4 us
    all_to_all x1, waiting for transfers between devices, shards(): lax.all_to_all(back_values, 'seq', split_axis=0, concat_axis=0, tiled=True)  28.2 us
    dot_general x12, matrix products, grad_step(): jnp.einsum('rhk,khd->rhd', dscores, key_block, preferred_element_type=jnp...  24.2 us
    dot_general x24, matrix products, scores_of(): jnp.einsum('rhd,khd->rhk', query_heads, key_block, preferred_element_type...  24.1 us
    all_to_all x1, waiting for transfers between devices, shards(): lax.all_to_all(send_values, 'seq', split_axis=0, concat_axis=0, tiled=True)  21.7 us
    dot_general x12, matrix products, output_step(): jnp.einsum('rhk,khd->rhd', weights, value_block, preferred_element_type=j...  20.4 us
    dot_general x12, matrix products, grad_step(): jnp.einsum('rhd,khd->rhk', grad_heads, value_block, preferred_element_typ...  15 us
  transfers between devices with their start and end apart: 7, of which 4 were waited for; matrix products, arithmetic and copies ran while one was open for 49% of the time, Pallas kernels for 0%

commit v1 on v0

v1 whole, which is shorter than its diff:
```python
import jax
import jax.numpy as jnp
from jax import lax
from jax.experimental import pallas as pl
from jax.experimental.pallas import tpu as pltpu
from jax.sharding import PartitionSpec as P

BLOCK = 128
DPS = 8
SLOT = 144
N_SEQ = 16
SIDE = 4
LANE_SPLIT = 64
SCALE = 0.125

VMEM = pltpu.MemorySpace.VMEM
SMEM = pltpu.MemorySpace.SMEM


def vmem_specs(count):
    return [pl.BlockSpec(memory_space=VMEM)] * count


def smem_specs(count):
    return [pl.BlockSpec(memory_space=SMEM)] * count


def dot(a, b, dims):
    return lax.dot_general(a, b, (dims, ((), ())), preferred_element_type=jnp.float32)


def select(equal):
    return jnp.where(equal, 1.0, 0.0).astype(jnp.bfloat16)


def pack_rows(slot_row, rows, out_ref):
    for slot in range(N_SEQ):
        place = lax.broadcasted_iota(jnp.int32, (SLOT, slot_row.shape[1]), 0) + slot * SLOT
        out_ref[slot] = dot(select(place == slot_row), rows, ((1,), (0,))).astype(jnp.bfloat16)


def unpack_rows(slot_col, packed):
    place = lax.broadcasted_iota(jnp.int32, (slot_col.shape[0], packed.shape[0]), 1)
    return dot(select(place == slot_col), packed, ((1,), (0,))).astype(jnp.bfloat16)


def pack_kernel(slot_ref, rows_ref, out_ref):
    pack_rows(slot_ref[...], rows_ref[...], out_ref)


def pack_queries(slot_row, queries):
    return pl.pallas_call(
        pack_kernel,
        out_shape=jax.ShapeDtypeStruct((N_SEQ, SLOT, queries.shape[1]), jnp.bfloat16),
        in_specs=vmem_specs(2),
        out_specs=pl.BlockSpec(memory_space=VMEM),
        name="pack_queries",
    )(slot_row, queries)


def unpack_kernel(slot_ref, packed_ref, out_ref):
    packed = packed_ref[...].reshape(N_SEQ * SLOT, -1)
    step = out_ref.shape[0] // SIDE
    for part in range(SIDE):
        span = slice(part * step, (part + 1) * step)
        out_ref[span, :] = unpack_rows(slot_ref[span, :], packed)


def unpack_grads(slot_col, packed):
    return pl.pallas_call(
        unpack_kernel,
        out_shape=jax.ShapeDtypeStruct((slot_col.shape[0], packed.shape[2]), jnp.bfloat16),
        in_specs=vmem_specs(2),
        out_specs=pl.BlockSpec(memory_space=VMEM),
        name="unpack_grads",
    )(slot_col, packed)


def swap_order(rows):
    unit = rows.shape[0] // (SIDE * SIDE)
    return jnp.concatenate(
        [
            rows[(a * SIDE + b) * unit : (a * SIDE + b + 1) * unit]
            for b in range(SIDE)
            for a in range(SIDE)
        ],
        axis=0,
    )


def grad_kernel(slot_ref, proj_ref, *refs):
    first, second, out_ref = refs[:SIDE], refs[SIDE : 2 * SIDE], refs[2 * SIDE]
    half = proj_ref.shape[1] // 2
    low = proj_ref[:, :half]
    high = proj_ref[:, half:]
    one = jnp.concatenate([dot(r[...], low, ((1,), (1,))) for r in first], axis=0)
    two = jnp.concatenate([dot(r[...], high, ((1,), (1,))) for r in second], axis=0)
    grads = (one + swap_order(two)).astype(jnp.bfloat16)
    pack_rows(slot_ref[...], grads, out_ref)


def attention_grads(slot_row, out_proj, first, second):
    return pl.pallas_call(
        grad_kernel,
        out_shape=jax.ShapeDtypeStruct((N_SEQ, SLOT, out_proj.shape[0]), jnp.bfloat16),
        in_specs=vmem_specs(2 + 2 * SIDE),
        out_specs=pl.BlockSpec(memory_space=VMEM),
        name="attention_grads",
    )(slot_row, out_proj, *first, *second)


def two_heads(rows):
    low = lax.broadcasted_iota(jnp.int32, rows.shape, 1) < LANE_SPLIT
    zero = jnp.zeros_like(rows)
    return jnp.concatenate([jnp.where(low, rows, zero), jnp.where(low, zero, rows)], axis=0)


def one_row(stacked):
    half = stacked.shape[0] // 2
    low = lax.broadcasted_iota(jnp.int32, (half, stacked.shape[1]), 1) < LANE_SPLIT
    return jnp.where(low, stacked[:half], stacked[half:])


def for_documents(source_ref, start_ref, count_ref, body):
    def step(doc, carry):
        source = source_ref[doc]
        first = pl.multiple_of(start_ref[doc] * BLOCK, BLOCK)
        for blocks in range(1, 4):

            @pl.when(count_ref[doc] == blocks)
            def _():
                body(doc, source, pl.ds(first, blocks * BLOCK), blocks * BLOCK)

        return carry

    lax.fori_loop(0, DPS, step, 0)


def forward_kernel(source_ref, start_ref, count_ref, q_ref, k_ref, v_ref, att_ref, w_ref):
    att_ref[...] = jnp.zeros(att_ref.shape, att_ref.dtype)

    def body(doc, source, tokens, width):
        queries = two_heads(q_ref[source])
        scores = dot(queries, k_ref[tokens, :], ((1,), (1,))) * SCALE
        top = jnp.max(scores, axis=1, keepdims=True)
        terms = jnp.exp(scores - top)
        weights = (terms / jnp.sum(terms, axis=1, keepdims=True)).astype(jnp.bfloat16)
        w_ref[doc, :, :width] = weights
        mixed = dot(weights, v_ref[tokens, :], ((1,), (0,)))
        att_ref[source] = one_row(mixed).astype(jnp.bfloat16)

    for_documents(source_ref, start_ref, count_ref, body)


def forward(source, start, count, got_q, keys, values):
    return pl.pallas_call(
        forward_kernel,
        out_shape=(
            jax.ShapeDtypeStruct(got_q.shape, jnp.bfloat16),
            jax.ShapeDtypeStruct((DPS, 2 * SLOT, 3 * BLOCK), jnp.bfloat16),
        ),
        in_specs=smem_specs(3) + vmem_specs(3),
        out_specs=tuple(vmem_specs(2)),
        name="forward",
    )(source, start, count, got_q, keys, values)


def backward_kernel(
    source_ref, start_ref, count_ref, q_ref, g_ref, att_ref, w_ref, k_ref, v_ref, dq_ref, dk_ref, dv_ref
):
    dq_ref[...] = jnp.zeros(dq_ref.shape, dq_ref.dtype)

    def body(doc, source, tokens, width):
        queries = two_heads(q_ref[source])
        grads = two_heads(g_ref[source])
        attended = att_ref[source].astype(jnp.float32)
        both = jnp.concatenate([attended, attended], axis=0)
        delta = jnp.sum(grads.astype(jnp.float32) * both, axis=1, keepdims=True)
        weights = w_ref[doc, :, :width]
        dprobs = dot(grads, v_ref[tokens, :], ((1,), (1,)))
        dscores = (weights.astype(jnp.float32) * (dprobs - delta)).astype(jnp.bfloat16)
        dq = dot(dscores, k_ref[tokens, :], ((1,), (0,)))
        dq_ref[source] = (one_row(dq) * SCALE).astype(jnp.bfloat16)
        dk_ref[tokens, :] = (dot(dscores, queries, ((0,), (0,))) * SCALE).astype(jnp.bfloat16)
        dv_ref[tokens, :] = dot(weights, grads, ((0,), (0,))).astype(jnp.bfloat16)

    for_documents(source_ref, start_ref, count_ref, body)


def backward(source, start, count, got_q, got_g, attended, weights, keys, values):
    return pl.pallas_call(
        backward_kernel,
        out_shape=(
            jax.ShapeDtypeStruct(got_q.shape, jnp.bfloat16),
            jax.ShapeDtypeStruct(keys.shape, jnp.bfloat16),
            jax.ShapeDtypeStruct(values.shape, jnp.bfloat16),
        ),
        in_specs=smem_specs(3) + vmem_specs(6),
        out_specs=tuple(vmem_specs(3)),
        name="backward",
    )(source, start, count, got_q, got_g, attended, weights, keys, values)


def mixed_kernel(slot_ref, packed_ref, proj_ref, *refs):
    first, second = refs[:SIDE], refs[SIDE : 2 * SIDE]
    m_first, m_second = refs[2 * SIDE : 3 * SIDE], refs[3 * SIDE : 4 * SIDE]
    even_ref, odd_ref = refs[4 * SIDE :]
    packed = packed_ref[...].reshape(N_SEQ * SLOT, -1)
    step = slot_ref.shape[0] // SIDE
    half = proj_ref.shape[1] // 2
    rows = [unpack_rows(slot_ref[p * step : (p + 1) * step, :], packed) for p in range(SIDE)]
    other = swap_order(jnp.concatenate(rows, axis=0))
    rows_two = [other[p * step : (p + 1) * step] for p in range(SIDE)]
    sums = []
    for part, ins, outs, cols in (
        (rows, first, m_first, slice(0, half)),
        (rows_two, second, m_second, slice(half, 2 * half)),
    ):
        total = None
        for p in range(SIDE):
            outs[p][...] = dot(part[p], proj_ref[:, cols], ((1,), (0,))).astype(jnp.bfloat16)
            term = dot(part[p], ins[p][...], ((0,), (0,)))
            total = term if total is None else total + term
        sums.append(total)
    per_half = half // BLOCK
    for h in range(2):
        for c in range(per_half):
            chunk = h * per_half + c
            target = even_ref if chunk % 2 == 0 else odd_ref
            target[chunk // 2] = sums[h][:, c * BLOCK : (c + 1) * BLOCK]


def mixed_parts(slot_col, packed, out_proj, first, second):
    inner, width = out_proj.shape
    part = jax.ShapeDtypeStruct(first[0].shape, jnp.bfloat16)
    sums = jax.ShapeDtypeStruct((width // BLOCK // 2, inner, BLOCK), jnp.float32)
    outs = pl.pallas_call(
        mixed_kernel,
        out_shape=(part,) * (2 * SIDE) + (sums,) * 2,
        in_specs=vmem_specs(3 + 2 * SIDE),
        out_specs=tuple(vmem_specs(2 * SIDE + 2)),
        name="mixed_parts",
    )(slot_col, packed, out_proj, *first, *second)
    return outs[:SIDE], outs[SIDE : 2 * SIDE], outs[2 * SIDE], outs[2 * SIDE + 1]


def along_x(value, k):
    perm = [(x * SIDE + y, (x + k) % SIDE * SIDE + y) for x in range(SIDE) for y in range(SIDE)]
    return lax.ppermute(value, "head", perm)


def along_y(value, k):
    perm = [(x * SIDE + y, x * SIDE + (y + k) % SIDE) for x in range(SIDE) for y in range(SIDE)]
    return lax.ppermute(value, "head", perm)


def gather(value, one, two):
    rows = jnp.concatenate([value] + [one(value, k) for k in range(1, SIDE)], axis=0)
    return [rows] + [two(rows, k) for k in range(1, SIDE)]


def total(parts):
    out = parts[0].astype(jnp.float32)
    for part in parts[1:]:
        out = out + part.astype(jnp.float32)
    return out.astype(jnp.bfloat16)


def scatter_sum(parts, one, two):
    rows = total([parts[0]] + [one(parts[k], SIDE - k) for k in range(1, SIDE)])
    unit = rows.shape[0] // SIDE
    return total(
        [rows[:unit]]
        + [two(rows[k * unit : (k + 1) * unit], SIDE - k) for k in range(1, SIDE)]
    )


def to_all(value):
    return lax.all_to_all(value, "seq", split_axis=0, concat_axis=0, tiled=True)


def shards(queries, enc_keys, enc_values, out_proj, out_grad, block_doc, query_doc):
    shard = lax.axis_index("seq")
    head = lax.axis_index("head")
    row_count = queries.shape[0]
    half = out_grad.shape[1] // 2
    rows = jnp.arange(row_count, dtype=jnp.int32)

    docs_here = lax.dynamic_slice_in_dim(query_doc, shard * row_count, row_count)
    same = docs_here[:, None] == docs_here[None, :]
    slot_row = docs_here // DPS * SLOT + rows - jnp.min(jnp.where(same, rows[:, None], row_count), axis=0)
    got_q = to_all(pack_queries(slot_row[None, :], queries))

    first = gather(out_grad[:, :half], along_x, along_y)
    second = gather(out_grad[:, half:], along_y, along_x)

    unit = out_grad.shape[0]
    block = rows // unit
    behind_y, behind_x = block // SIDE, block % SIDE
    source_block = (head // SIDE - behind_x) % SIDE * SIDE + (head % SIDE - behind_y) % SIDE
    source_row = source_block * unit + rows % unit
    slot_rel = jnp.sum(jnp.where(source_row[None, :] == rows[:, None], slot_row[:, None], 0), axis=0)
    slot_rel_col = jnp.sum(jnp.where(source_row[:, None] == rows[None, :], slot_row[None, :], 0), axis=1)

    my_docs = shard * DPS + jnp.arange(DPS, dtype=jnp.int32)
    all_rows = jnp.arange(query_doc.shape[0], dtype=jnp.int32)
    source = jnp.max(jnp.where(query_doc[None, :] == my_docs[:, None], all_rows[None, :], 0), axis=1) // row_count
    local_blocks = enc_keys.shape[0] // BLOCK
    blocks_here = lax.dynamic_slice_in_dim(block_doc, shard * local_blocks, local_blocks)
    start = jnp.sum((blocks_here[None, :] < my_docs[:, None]).astype(jnp.int32), axis=1)
    count = jnp.sum((blocks_here[None, :] == my_docs[:, None]).astype(jnp.int32), axis=1)

    attended, weights = forward(source, start, count, got_q, enc_keys, enc_values)
    home = to_all(attended)
    got_g = to_all(attention_grads(slot_rel[None, :], out_proj, first, second))

    m_first, m_second, even, odd = mixed_parts(slot_rel_col[:, None], home, out_proj, first, second)
    mixed = jnp.concatenate(
        [scatter_sum(m_first, along_y, along_x), scatter_sum(m_second, along_x, along_y)], axis=1
    )

    core = shard % 2
    swap = [(s, s ^ 1) for s in range(N_SEQ)]
    other = lax.ppermute(jnp.where(core == 0, odd, even).astype(jnp.bfloat16), "seq", swap)
    pair = (jnp.where(core == 0, even, odd) + other.astype(jnp.float32)).astype(jnp.bfloat16)
    groups = [[z * 2 + c for z in range(N_SEQ // 2)] for c in range(2)]
    terms = lax.all_to_all(pair, "seq", split_axis=0, concat_axis=0, axis_index_groups=groups, tiled=True)
    grad_wo = jnp.sum(terms.astype(jnp.float32), axis=0)

    grads_q, grad_k, grad_v = backward(
        source, start, count, got_q, got_g, attended, weights, enc_keys, enc_values
    )
    grad_q = unpack_grads(slot_row[:, None], to_all(grads_q))
    return (mixed, grad_q, grad_k, grad_v, grad_wo)


def solution(mesh):
    placed = (
        P("seq", "head"),
        P("seq", "head"),
        P("seq", "head"),
        P("head", None),
        P(("seq", "head"), None),
        P(),
        P(),
    )
    return jax.shard_map(
        shards,
        mesh=mesh,
        in_specs=placed,
        out_specs=(
            P(("seq", "head"), None),
            P("seq", "head"),
            P("seq", "head"),
            P("seq", "head"),
            P("head", "seq"),
        ),
        check_vma=False,
    )
```

time: 332 us -> 193 us (0.58)
  matrix products: 114 us -> 0 us
  local copies, waits for them, and re-layouts: 46.8 us -> 5.69 us
  starting transfers between devices: 23 us -> 62.8 us
  waiting for transfers between devices: 115 us -> 79.6 us
  Pallas kernels: 0 us -> 32.6 us
  between operations: 14.1 us -> 0.94 us
  other arithmetic: 14.4 us -> 9.12 us
    dot_general x87 -> x0, matrix products: 114 us -> none  [the longest x12 24.2 us: grad_step(): jnp.einsum('rhk,khd->rhd', dscores, key_block, preferred_element_type=jnp...]
    all_to_all x4 -> x5, waiting for transfers between devices: 115 us -> 23.8 us  [the longest x4 17.8 us: to_all(): return lax.all_to_all(value, 'seq', split_axis=0, concat_axis=0, tiled=True)]
    ppermute x0 -> x25, waiting for transfers between devices: none -> 55.7 us  [the longest x12 31.6 us: along_x(): return lax.ppermute(value, 'head', perm)]
    pallas_call x0 -> x6, Pallas kernels: none -> 32.6 us  [the longest x1 7.88 us: backward(): pl.pallas_call(backward_kernel, out_shape=(jax.ShapeDtypeStruct(got_q.sha...]
    ppermute x0 -> x25, starting transfers between devices: none -> 32.1 us  [the longest x12 20.9 us: along_y(): return lax.ppermute(value, 'head', perm)]
    another operation x10 -> x0, local copies, waits for them, and re-layouts: 15.9 us -> none
    scatter x4 -> x0, local copies, waits for them, and re-layouts: 14.3 us -> none  [the longest x1 4.59 us: shards(): back_values = jnp.zeros((slot_total, BLOCK, inner_here), jnp.bfloat16).at...]
    all_to_all x4 -> x5, starting transfers between devices: 22.8 us -> 30.7 us  [the longest x4 24.7 us: to_all(): return lax.all_to_all(value, 'seq', split_axis=0, concat_axis=0, tiled=True)]
  transfers between devices with their start and end apart: 7 -> 30, of which waited for: 4 -> 12; matrix products, arithmetic and copies ran while one was open for 49% -> 5% of each run, Pallas kernels for 0% -> 12%
where the time goes in v1:
time: 193 us; the launch traced here: 191 us
  waiting for transfers between devices  79.6 us (41%)
  starting transfers between devices  62.8 us (33%)
  Pallas kernels  32.6 us (17%)
  other arithmetic  9.12 us (5%)
  local copies, waits for them, and re-layouts  5.69 us (3%)
    ppermute x12, waiting for transfers between devices, along_x(): return lax.ppermute(value, 'head', perm)  31.6 us
    all_to_all x4, starting transfers between devices, to_all(): return lax.all_to_all(value, 'seq', split_axis=0, concat_axis=0, tiled=True)  24.7 us
    ppermute x12, waiting for transfers between devices, along_y(): return lax.ppermute(value, 'head', perm)  24.1 us
    ppermute x12, starting transfers between devices, along_y(): return lax.ppermute(value, 'head', perm)  20.9 us
    all_to_all x4, waiting for transfers between devices, to_all(): return lax.all_to_all(value, 'seq', split_axis=0, concat_axis=0, tiled=True)  17.8 us
    ppermute x12, starting transfers between devices, along_x(): return lax.ppermute(value, 'head', perm)  11 us
    pallas_call x1, Pallas kernels, backward(): pl.pallas_call(backward_kernel, out_shape=(jax.ShapeDtypeStruct(got_q.sha...  7.88 us
    pallas_call x1, Pallas kernels, forward(): pl.pallas_call(forward_kernel, out_shape=(jax.ShapeDtypeStruct(got_q.shap...  7.35 us
  transfers between devices with their start and end apart: 30, of which 12 were waited for; matrix products, arithmetic and copies ran while one was open for 5% of the time, Pallas kernels for 12%

profile of v1, /device:TPU:1, one launch (start us, length us, event | category | flops | bytes accessed | tf_op | source)
XLA Modules:
  0.0 190.8 jit_solution(13236160154358301406)
XLA Ops:
  3.3 2.8 %pack_queries.1 = bf16[16,144,128]{2,1,0:T(8,128)(2,1)} custom-call(s32[1,768]{1,0:T(1,128)} %broadcast_in_dim.79.slot_ref, bf16[768,128]{1,0:T(8,128)(2,1)} %rows_ref.1), custom_call_target="tpu_custom_call" | custom-call | tf_op jit(solution)/shard_map/pack_queries/pallas_call | solution.py:52
  6.1 10.1 %all-to-all-start = ((bf16[16,144,128]{2,1,0:T(8,128)(2,1)}), bf16[16,144,128]{2,1,0:T(8,128)(2,1)S(1)}, u32[]{:S(2)}, u32[]{:S(2)}) async-start(bf16[16,144,128]{2,1,0:T(8,128)(2,1)} %pack_queries.1), calls=%async_computation | async-start | bytes 1179648 | tf_op jit(solution)/shard_map/all_to_all | solution.py:279
  17.9 16.9 %all-to-all-done.q_ref = bf16[16,144,128]{2,1,0:T(8,128)(2,1)S(1)} async-done(((bf16[16,144,128]{2,1,0:T(8,128)(2,1)}), bf16[16,144,128]{2,1,0:T(8,128)(2,1)S(1)}, u32[]{:S(2)}, u32[]{:S(2)}) %all-to-all-start) | async-done | bytes 589856 | tf_op jit(solution)/shard_map/all_to_all | solution.py:279
  35.6 7.4 %forward.1 = (bf16[16,144,128]{2,1,0:T(8,128)(2,1)}, bf16[8,288,384]{2,1,0:T(8,128)(2,1)}) custom-call(s32[8]{0:T(128)} %and_select_fusion.source_ref, s32[8]{0:T(128)} %get-tuple-element.38.start_ref, s32[8]{0:T(128)} %get-tuple-element.37.count_ref, bf16[16,144,128]{2,1,0:T(8,128)(2,1)} %copy-done, bf16[2048,128]{1,0:T(8,128)(2,1)} %k_ref.3, ...), custom_call_target="tpu_custom_call" | custom-call | tf_op jit(solution)/shard_map/forward/pallas_call | solution.py:156
  42.9 3.5 %all-to-all-start.1 = ((bf16[16,144,128]{2,1,0:T(8,128)(2,1)}), bf16[16,144,128]{2,1,0:T(8,128)(2,1)S(1)}, u32[]{:S(2)}, u32[]{:S(2)}) async-start(bf16[16,144,128]{2,1,0:T(8,128)(2,1)} %get-tuple-element.20.att_ref), calls=%async_computation.1 | async-start | bytes 1179648 | tf_op jit(solution)/shard_map/all_to_all | solution.py:279
  46.4 2.5 %collective-permute-start.2 = (bf16[48,1024]{1,0:T(8,128)(2,1)S(1)}, bf16[48,1024]{1,0:T(8,128)(2,1)S(1)}, u32[]{:S(2)}, u32[]{:S(2)}) collective-permute-start(bf16[48,1024]{1,0:T(8,128)(2,1)S(1)} %get-tuple-element.46), channel_id=1, source_target_pairs={{0,12},{1,13},{2,14},{3,15},{4,0},{5,1},{6,2},{7,3},{8,4},{9,5},{1... | collective-permute-start | bytes 294920 | tf_op jit(solution)/shard_map/ppermute | solution.py:249
  50.1 3.3 %collective-permute-done.2 = bf16[48,1024]{1,0:T(8,128)(2,1)S(1)} collective-permute-done((bf16[48,1024]{1,0:T(8,128)(2,1)S(1)}, bf16[48,1024]{1,0:T(8,128)(2,1)S(1)}, u32[]{:S(2)}, u32[]{:S(2)}) %collective-permute-start.2) | collective-permute-done | bytes 98336 | tf_op jit(solution)/shard_map/ppermute | solution.py:249
  57.4 2.8 %collective-permute-start.5 = (bf16[192,1024]{1,0:T(8,128)(2,1)S(1)}, bf16[192,1024]{1,0:T(8,128)(2,1)S(1)}, u32[]{:S(2)}, u32[]{:S(2)}) collective-permute-start(bf16[192,1024]{1,0:T(8,128)(2,1)S(1)} %pad_maximum_fusion.refs_0_), channel_id=1, source_target_pairs={{0,3},{1,0},{2,1},{3,2},{4,7},{5,4},{6,5},{7,6},{8,11},{9,8},{10,9... | collective-permute-start | bytes 1179656 | tf_op jit(solution)/shard_map/ppermute | solution.py:254
  61.7 3.6 %collective-permute-start.4 = (bf16[192,1024]{1,0:T(8,128)(2,1)S(1)}, bf16[192,1024]{1,0:T(8,128)(2,1)S(1)}, u32[]{:S(2)}, u32[]{:S(2)}) collective-permute-start(bf16[192,1024]{1,0:T(8,128)(2,1)S(1)} %pad_maximum_fusion.refs_0_), channel_id=1, source_target_pairs={{0,2},{1,3},{2,0},{3,1},{4,6},{5,7},{6,4},{7,5},{8,10},{9,11},{10,... | collective-permute-start | bytes 1179656 | tf_op jit(solution)/shard_map/ppermute | solution.py:254
  65.2 15.5 %collective-permute-done.8 = bf16[48,1024]{1,0:T(8,128)(2,1)S(1)} collective-permute-done((bf16[48,1024]{1,0:T(8,128)(2,1)S(1)}, bf16[48,1024]{1,0:T(8,128)(2,1)S(1)}, u32[]{:S(2)}, u32[]{:S(2)}) %collective-permute-start.8) | collective-permute-done | bytes 98336 | tf_op jit(solution)/shard_map/ppermute | solution.py:254
  83.9 8.6 %collective-permute-done.3.refs_1_ = bf16[192,1024]{1,0:T(8,128)(2,1)S(1)} collective-permute-done((bf16[192,1024]{1,0:T(8,128)(2,1)S(1)}, bf16[192,1024]{1,0:T(8,128)(2,1)S(1)}, u32[]{:S(2)}, u32[]{:S(2)}) %collective-permute-start.3) | collective-permute-done | bytes 393248 | tf_op jit(solution)/shard_map/ppermute | solution.py:254
  92.6 9.5 %collective-permute-done.9.refs_5_ = bf16[192,1024]{1,0:T(8,128)(2,1)} collective-permute-done((bf16[192,1024]{1,0:T(8,128)(2,1)S(1)}, bf16[192,1024]{1,0:T(8,128)(2,1)}, u32[]{:S(2)}, u32[]{:S(2)}) %collective-permute-start.9) | collective-permute-done | bytes 393248 | tf_op jit(solution)/shard_map/ppermute | solution.py:249
  102.1 5.6 %attention_grads.1 = bf16[16,144,128]{2,1,0:T(8,128)(2,1)} custom-call(s32[1,768]{1,0:T(1,128)} %broadcast_in_dim.83.slot_ref, bf16[128,2048]{1,0:T(8,128)(2,1)} %proj_ref.3, bf16[192,1024]{1,0:T(8,128)(2,1)} %copy-done.1, bf16[192,1024]{1,0:T(8,128)(2,1)} %copy-done.10, bf16[192,1024]{1,0:T(8,128)(2,1)} %copy-done.9, bf16[192,1024]{1,0:T(8,128)(2,1)} %copy-done.8, ...), custom_call_target="tpu_custom_call" | custom-call | tf_op jit(solution)/shard_map/attention_grads/pallas_call | solution.py:103
  107.7 3.9 %all-to-all-start.2 = ((bf16[16,144,128]{2,1,0:T(8,128)(2,1)}), bf16[16,144,128]{2,1,0:T(8,128)(2,1)S(1)}, u32[]{:S(2)}, u32[]{:S(2)}) async-start(bf16[16,144,128]{2,1,0:T(8,128)(2,1)} %attention_grads.1), calls=%async_computation.2 | async-start | bytes 1179648 | tf_op jit(solution)/shard_map/all_to_all | solution.py:279
  112.5 5.9 %mixed_parts.1 = (bf16[192,1024]{1,0:T(8,128)(2,1)}, bf16[192,1024]{1,0:T(8,128)(2,1)}, bf16[192,1024]{1,0:T(8,128)(2,1)}, bf16[192,1024]{1,0:T(8,128)(2,1)}, bf...) custom-call(s32[768,1]{1,0:T(8,128)} %broadcast_in_dim.84.slot_ref, ...), custom_call_target="tpu_custom_call" | custom-call | tf_op jit(solution)/shard_map/mixed_parts/pallas_call | solution.py:237
  120.5 5.9 %collective-permute-start.12 = (bf16[192,1024]{1,0:T(8,128)(2,1)}, bf16[192,1024]{1,0:T(8,128)(2,1)S(1)}, u32[]{:S(2)}, u32[]{:S(2)}) collective-permute-start(bf16[192,1024]{1,0:T(8,128)(2,1)} %get-tuple-element.22), channel_id=1, source_target_pairs={{0,3},{1,0},{2,1},{3,2},{4,7},{5,4},{6,5},{7,6},{8,11},{9,8},{10,9... | collective-permute-start | bytes 1179656 | tf_op jit(solution)/shard_map/ppermute | solution.py:254
  131.2 7.9 %backward.1 = (bf16[16,144,128]{2,1,0:T(8,128)(2,1)}, bf16[2048,128]{1,0:T(8,128)(2,1)}, bf16[2048,128]{1,0:T(8,128)(2,1)}) custom-call(s32[8]{0:T(128)} %and_select_fusion.source_ref, s32[8]{0:T(128)} %get-tuple-element.38.start_ref, s32[8]{0:T(128)} %get-tuple-element.37.count_ref, bf16[16,144,128]{2,1,0:T(8,128)(2,1)} %copy-done, ...), custom_call_target="tpu_custom_call" | custom-call | tf_op jit(solution)/shard_map/backward/pallas_call | solution.py:191
  139.0 7.3 %all-to-all-start.3 = ((bf16[16,144,128]{2,1,0:T(8,128)(2,1)}), bf16[16,144,128]{2,1,0:T(8,128)(2,1)S(1)}, u32[]{:S(2)}, u32[]{:S(2)}) async-start(bf16[16,144,128]{2,1,0:T(8,128)(2,1)} %get-tuple-element.30), calls=%async_computation.3 | async-start | bytes 1179648 | tf_op jit(solution)/shard_map/all_to_all | solution.py:279
  152.6 4.4 %collective-permute-done.18 = bf16[192,1024]{1,0:T(8,128)(2,1)S(1)} collective-permute-done((bf16[192,1024]{1,0:T(8,128)(2,1)}, bf16[192,1024]{1,0:T(8,128)(2,1)S(1)}, u32[]{:S(2)}, u32[]{:S(2)}) %collective-permute-start.18) | collective-permute-done | bytes 393248 | tf_op jit(solution)/shard_map/ppermute | solution.py:249
  159.7 9.2 %collective-permute-done.20 = bf16[192,1024]{1,0:T(8,128)(2,1)S(1)} collective-permute-done((bf16[192,1024]{1,0:T(8,128)(2,1)}, bf16[192,1024]{1,0:T(8,128)(2,1)S(1)}, u32[]{:S(2)}, u32[]{:S(2)}) %collective-permute-start.20) | collective-permute-done | bytes 393248 | tf_op jit(solution)/shard_map/ppermute | solution.py:249
  171.6 2.6 %collective-permute-start.22 = (bf16[48,1024]{1,0:T(8,128)(2,1)S(1)}, bf16[48,1024]{1,0:T(8,128)(2,1)S(1)}, u32[]{:S(2)}, u32[]{:S(2)}) collective-permute-start(bf16[48,1024]{1,0:T(8,128)(2,1)S(1)} %get-tuple-element.44), channel_id=1, source_target_pairs={{0,2},{1,3},{2,0},{3,1},{4,6},{5,7},{6,4},{7,5},{8,10},{9,11},{10,... | collective-permute-start | bytes 294920 | tf_op jit(solution)/shard_map/ppermute | solution.py:254
  174.3 6.0 %all-to-all-start.4 = ((bf16[8,128,128]{2,1,0:T(8,128)(2,1)}), bf16[8,128,128]{2,1,0:T(8,128)(2,1)S(1)}, u32[]{:S(2)}, u32[]{:S(2)}) async-start(bf16[8,128,128]{2,1,0:T(8,128)(2,1)} %add_convert_fusion.2), calls=%async_computation.4 | async-start | bytes 524288 | tf_op jit(solution)/shard_map/all_to_all | solution.py:327
  180.3 3.0 %unpack_grads.1 = bf16[768,128]{1,0:T(8,128)(2,1)} custom-call(s32[768,1]{1,0:T(8,128)} %broadcast_in_dim.85.slot_ref, bf16[16,144,128]{2,1,0:T(8,128)(2,1)} %copy-done.4), custom_call_target="tpu_custom_call" | custom-call | tf_op jit(solution)/shard_map/unpack_grads/pallas_call | solution.py:70
  184.1 6.0 %all-to-all-done.4 = bf16[8,128,128]{2,1,0:T(8,128)(2,1)S(1)} async-done(((bf16[8,128,128]{2,1,0:T(8,128)(2,1)}), bf16[8,128,128]{2,1,0:T(8,128)(2,1)S(1)}, u32[]{:S(2)}, u32[]{:S(2)}) %all-to-all-start.4) | async-done | bytes 262176 | tf_op jit(solution)/shard_map/all_to_all | solution.py:327
  (104 shorter events, 35.6 us)
Async XLA Ops:
  6.1 28.6 %all-to-all-start = ((bf16[16,144,128]{2,1,0:T(8,128)(2,1)}), bf16[16,144,128]{2,1,0:T(8,128)(2,1)S(1)}, u32[]{:S(2)}, u32[]{:S(2)}) async-start(bf16[16,144,128]{2,1,0:T(8,128)(2,1)} %pack_queries.1), calls=%async_computation | async-start | bytes 1179648 | tf_op jit(solution)/shard_map/all_to_all | solution.py:279
  42.9 64.8 %all-to-all-start.1 = ((bf16[16,144,128]{2,1,0:T(8,128)(2,1)}), bf16[16,144,128]{2,1,0:T(8,128)(2,1)S(1)}, u32[]{:S(2)}, u32[]{:S(2)}) async-start(bf16[16,144,128]{2,1,0:T(8,128)(2,1)} %get-tuple-element.20.att_ref), calls=%async_computation.1 | async-start | bytes 1179648 | tf_op jit(solution)/shard_map/all_to_all | solution.py:279
  57.4 24.1 %collective-permute-start.5 = (bf16[192,1024]{1,0:T(8,128)(2,1)S(1)}, bf16[192,1024]{1,0:T(8,128)(2,1)S(1)}, u32[]{:S(2)}, u32[]{:S(2)}) collective-permute-start(bf16[192,1024]{1,0:T(8,128)(2,1)S(1)} %pad_maximum_fusion.refs_0_), channel_id=1, source_target_pairs={{0,3},{1,0},{2,1},{3,2},{4,7},{5,4},{6,5},{7,6},{8,11},{9,8},{10,9... | collective-permute-start | bytes 1179656 | tf_op jit(solution)/shard_map/ppermute | solution.py:254
  60.2 20.5 %collective-permute-start.8 = (bf16[48,1024]{1,0:T(8,128)(2,1)S(1)}, bf16[48,1024]{1,0:T(8,128)(2,1)S(1)}, u32[]{:S(2)}, u32[]{:S(2)}) collective-permute-start(bf16[48,1024]{1,0:T(8,128)(2,1)S(1)} %get-tuple-element.45), channel_id=1, source_target_pairs={{0,3},{1,0},{2,1},{3,2},{4,7},{5,4},{6,5},{7,6},{8,11},{9,8},{10,9... | collective-permute-start | bytes 294920 | tf_op jit(solution)/shard_map/ppermute | solution.py:254
  60.7 20.1 %collective-permute-start.7 = (bf16[48,1024]{1,0:T(8,128)(2,1)S(1)}, bf16[48,1024]{1,0:T(8,128)(2,1)S(1)}, u32[]{:S(2)}, u32[]{:S(2)}) collective-permute-start(bf16[48,1024]{1,0:T(8,128)(2,1)S(1)} %get-tuple-element.45), channel_id=1, source_target_pairs={{0,2},{1,3},{2,0},{3,1},{4,6},{5,7},{6,4},{7,5},{8,10},{9,11},{10,... | collective-permute-start | bytes 294920 | tf_op jit(solution)/shard_map/ppermute | solution.py:254
  60.7 20.0 %collective-permute-start.6 = (bf16[48,1024]{1,0:T(8,128)(2,1)S(1)}, bf16[48,1024]{1,0:T(8,128)(2,1)S(1)}, u32[]{:S(2)}, u32[]{:S(2)}) collective-permute-start(bf16[48,1024]{1,0:T(8,128)(2,1)S(1)} %get-tuple-element.45), channel_id=1, source_target_pairs={{0,1},{1,2},{2,3},{3,0},{4,5},{5,6},{6,7},{7,4},{8,9},{9,10},{10,1... | collective-permute-start | bytes 294920 | tf_op jit(solution)/shard_map/ppermute | solution.py:254
  61.7 22.3 %collective-permute-start.4 = (bf16[192,1024]{1,0:T(8,128)(2,1)S(1)}, bf16[192,1024]{1,0:T(8,128)(2,1)S(1)}, u32[]{:S(2)}, u32[]{:S(2)}) collective-permute-start(bf16[192,1024]{1,0:T(8,128)(2,1)S(1)} %pad_maximum_fusion.refs_0_), channel_id=1, source_target_pairs={{0,2},{1,3},{2,0},{3,1},{4,6},{5,7},{6,4},{7,5},{8,10},{9,11},{10,... | collective-permute-start | bytes 1179656 | tf_op jit(solution)/shard_map/ppermute | solution.py:254
  80.7 11.8 %collective-permute-start.3 = (bf16[192,1024]{1,0:T(8,128)(2,1)S(1)}, bf16[192,1024]{1,0:T(8,128)(2,1)S(1)}, u32[]{:S(2)}, u32[]{:S(2)}) collective-permute-start(bf16[192,1024]{1,0:T(8,128)(2,1)S(1)} %pad_maximum_fusion.refs_0_), channel_id=1, source_target_pairs={{0,1},{1,2},{2,3},{3,0},{4,5},{5,6},{6,7},{7,4},{8,9},{9,10},{10,1... | collective-permute-start | bytes 1179656 | tf_op jit(solution)/shard_map/ppermute | solution.py:254
  80.8 11.8 %collective-permute-start.11 = (bf16[192,1024]{1,0:T(8,128)(2,1)S(1)}, bf16[192,1024]{1,0:T(8,128)(2,1)S(1)}, u32[]{:S(2)}, u32[]{:S(2)}) collective-permute-start(bf16[192,1024]{1,0:T(8,128)(2,1)S(1)} %pad_maximum_fusion.1.refs_4_), channel_id=1, source_target_pairs={{0,12},{1,13},{2,14},{3,15},{4,0},{5,1},{6,2},{7,3},{8,4},{9,5},{1... | collective-permute-start | bytes 1179656 | tf_op jit(solution)/shard_map/ppermute | solution.py:249
  81.5 20.5 %collective-permute-start.9 = (bf16[192,1024]{1,0:T(8,128)(2,1)S(1)}, bf16[192,1024]{1,0:T(8,128)(2,1)}, u32[]{:S(2)}, u32[]{:S(2)}) collective-permute-start(bf16[192,1024]{1,0:T(8,128)(2,1)S(1)} %pad_maximum_fusion.1.refs_4_), channel_id=1, source_target_pairs={{0,4},{1,5},{2,6},{3,7},{4,8},{5,9},{6,10},{7,11},{8,12},{9,13},{1... | collective-permute-start | bytes 1179656 | tf_op jit(solution)/shard_map/ppermute | solution.py:249
  107.7 22.6 %all-to-all-start.2 = ((bf16[16,144,128]{2,1,0:T(8,128)(2,1)}), bf16[16,144,128]{2,1,0:T(8,128)(2,1)S(1)}, u32[]{:S(2)}, u32[]{:S(2)}) async-start(bf16[16,144,128]{2,1,0:T(8,128)(2,1)} %attention_grads.1), calls=%async_computation.2 | async-start | bytes 1179648 | tf_op jit(solution)/shard_map/all_to_all | solution.py:279
  120.2 27.5 %collective-permute-start.24 = (bf16[8,128,128]{2,1,0:T(8,128)(2,1)}, bf16[8,128,128]{2,1,0:T(8,128)(2,1)}, u32[]{:S(2)}, u32[]{:S(2)}) collective-permute-start(bf16[8,128,128]{2,1,0:T(8,128)(2,1)} %select_convert_fusion), channel_id=1, source_target_pairs={{0,16},{16,0},{32,48},{48,32},{64,80},{80,64},{96,112},{112,96},{1... | collective-permute-start | bytes 786440 | tf_op jit(solution)/shard_map/ppermute | solution.py:324
  120.5 29.0 %collective-permute-start.12 = (bf16[192,1024]{1,0:T(8,128)(2,1)}, bf16[192,1024]{1,0:T(8,128)(2,1)S(1)}, u32[]{:S(2)}, u32[]{:S(2)}) collective-permute-start(bf16[192,1024]{1,0:T(8,128)(2,1)} %get-tuple-element.22), channel_id=1, source_target_pairs={{0,3},{1,0},{2,1},{3,2},{4,7},{5,4},{6,5},{7,6},{8,11},{9,8},{10,9... | collective-permute-start | bytes 1179656 | tf_op jit(solution)/shard_map/ppermute | solution.py:254
  126.4 23.7 %collective-permute-start.13 = (bf16[192,1024]{1,0:T(8,128)(2,1)}, bf16[192,1024]{1,0:T(8,128)(2,1)S(1)}, u32[]{:S(2)}, u32[]{:S(2)}) collective-permute-start(bf16[192,1024]{1,0:T(8,128)(2,1)} %get-tuple-element.23), channel_id=1, source_target_pairs={{0,2},{1,3},{2,0},{3,1},{4,6},{5,7},{6,4},{7,5},{8,10},{9,11},{10,... | collective-permute-start | bytes 1179656 | tf_op jit(solution)/shard_map/ppermute | solution.py:254
  127.6 22.6 %collective-permute-start.14 = (bf16[192,1024]{1,0:T(8,128)(2,1)}, bf16[192,1024]{1,0:T(8,128)(2,1)S(1)}, u32[]{:S(2)}, u32[]{:S(2)}) collective-permute-start(bf16[192,1024]{1,0:T(8,128)(2,1)} %get-tuple-element.24), channel_id=1, source_target_pairs={{0,1},{1,2},{2,3},{3,0},{4,5},{5,6},{6,7},{7,4},{8,9},{9,10},{10,1... | collective-permute-start | bytes 1179656 | tf_op jit(solution)/shard_map/ppermute | solution.py:254
  139.0 35.3 %all-to-all-start.3 = ((bf16[16,144,128]{2,1,0:T(8,128)(2,1)}), bf16[16,144,128]{2,1,0:T(8,128)(2,1)S(1)}, u32[]{:S(2)}, u32[]{:S(2)}) async-start(bf16[16,144,128]{2,1,0:T(8,128)(2,1)} %get-tuple-element.30), calls=%async_computation.3 | async-start | bytes 1179648 | tf_op jit(solution)/shard_map/all_to_all | solution.py:279
  147.7 12.0 %collective-permute-start.19 = (bf16[192,1024]{1,0:T(8,128)(2,1)}, bf16[192,1024]{1,0:T(8,128)(2,1)S(1)}, u32[]{:S(2)}, u32[]{:S(2)}) collective-permute-start(bf16[192,1024]{1,0:T(8,128)(2,1)} %get-tuple-element.27), channel_id=1, source_target_pairs={{0,8},{1,9},{2,10},{3,11},{4,12},{5,13},{6,14},{7,15},{8,0},{9,1},... | collective-permute-start | bytes 1179656 | tf_op jit(solution)/shard_map/ppermute | solution.py:249
  149.5 19.4 %collective-permute-start.20 = (bf16[192,1024]{1,0:T(8,128)(2,1)}, bf16[192,1024]{1,0:T(8,128)(2,1)S(1)}, u32[]{:S(2)}, u32[]{:S(2)}) collective-permute-start(bf16[192,1024]{1,0:T(8,128)(2,1)} %get-tuple-element.28), channel_id=1, source_target_pairs={{0,4},{1,5},{2,6},{3,7},{4,8},{5,9},{6,10},{7,11},{8,12},{9,13},{1... | collective-permute-start | bytes 1179656 | tf_op jit(solution)/shard_map/ppermute | solution.py:249
  150.4 21.2 %collective-permute-start.15 = (bf16[48,1024]{1,0:T(8,128)(2,1)S(1)}, bf16[48,1024]{1,0:T(8,128)(2,1)S(1)}, u32[]{:S(2)}, u32[]{:S(2)}) collective-permute-start(bf16[48,1024]{1,0:T(8,128)(2,1)S(1)} %get-tuple-element.39), channel_id=1, source_target_pairs={{0,12},{1,13},{2,14},{3,15},{4,0},{5,1},{6,2},{7,3},{8,4},{9,5},{1... | collective-permute-start | bytes 294920 | tf_op jit(solution)/shard_map/ppermute | solution.py:249
  152.6 21.7 %collective-permute-start.17 = (bf16[48,1024]{1,0:T(8,128)(2,1)S(1)}, bf16[48,1024]{1,0:T(8,128)(2,1)S(1)}, u32[]{:S(2)}, u32[]{:S(2)}) collective-permute-start(bf16[48,1024]{1,0:T(8,128)(2,1)S(1)} %get-tuple-element.40), channel_id=1, source_target_pairs={{0,4},{1,5},{2,6},{3,7},{4,8},{5,9},{6,10},{7,11},{8,12},{9,13},{1... | collective-permute-start | bytes 294920 | tf_op jit(solution)/shard_map/ppermute | solution.py:249
  157.0 17.2 %collective-permute-start.16 = (bf16[48,1024]{1,0:T(8,128)(2,1)S(1)}, bf16[48,1024]{1,0:T(8,128)(2,1)S(1)}, u32[]{:S(2)}, u32[]{:S(2)}) collective-permute-start(bf16[48,1024]{1,0:T(8,128)(2,1)S(1)} %get-tuple-element.41), channel_id=1, source_target_pairs={{0,8},{1,9},{2,10},{3,11},{4,12},{5,13},{6,14},{7,15},{8,0},{9,1},... | collective-permute-start | bytes 294920 | tf_op jit(solution)/shard_map/ppermute | solution.py:249
  169.2 14.1 %collective-permute-start.21 = (bf16[48,1024]{1,0:T(8,128)(2,1)S(1)}, bf16[48,1024]{1,0:T(8,128)(2,1)S(1)}, u32[]{:S(2)}, u32[]{:S(2)}) collective-permute-start(bf16[48,1024]{1,0:T(8,128)(2,1)S(1)} %get-tuple-element.42), channel_id=1, source_target_pairs={{0,3},{1,0},{2,1},{3,2},{4,7},{5,4},{6,5},{7,6},{8,11},{9,8},{10,9... | collective-permute-start | bytes 294920 | tf_op jit(solution)/shard_map/ppermute | solution.py:254
  171.6 11.7 %collective-permute-start.23 = (bf16[48,1024]{1,0:T(8,128)(2,1)S(1)}, bf16[48,1024]{1,0:T(8,128)(2,1)S(1)}, u32[]{:S(2)}, u32[]{:S(2)}) collective-permute-start(bf16[48,1024]{1,0:T(8,128)(2,1)S(1)} %get-tuple-element.43), channel_id=1, source_target_pairs={{0,1},{1,2},{2,3},{3,0},{4,5},{5,6},{6,7},{7,4},{8,9},{9,10},{10,1... | collective-permute-start | bytes 294920 | tf_op jit(solution)/shard_map/ppermute | solution.py:254
  174.3 15.8 %all-to-all-start.4 = ((bf16[8,128,128]{2,1,0:T(8,128)(2,1)}), bf16[8,128,128]{2,1,0:T(8,128)(2,1)S(1)}, u32[]{:S(2)}, u32[]{:S(2)}) async-start(bf16[8,128,128]{2,1,0:T(8,128)(2,1)} %add_convert_fusion.2), calls=%async_computation.4 | async-start | bytes 524288 | tf_op jit(solution)/shard_map/all_to_all | solution.py:327
  (24 other events, 338.1 us)

commit v2 on v1

v2 whole, which is shorter than its diff:
```python
import jax
import jax.numpy as jnp
from jax import lax
from jax.experimental import pallas as pl
from jax.experimental.pallas import tpu as pltpu
from jax.sharding import PartitionSpec as P


BLOCK = 128
DPS = 8
SLOT = 144
TILE = 16
WINDOW = SLOT + TILE
CAP = 3
MASKED = -1e30
N_SEQ = 16
SIDE = 4
LANE_SPLIT = 64
SCALE = 0.125

VMEM = pltpu.MemorySpace.VMEM
SMEM = pltpu.MemorySpace.SMEM


def vmem_specs(count):
    return [pl.BlockSpec(memory_space=VMEM)] * count


def smem_specs(count):
    return [pl.BlockSpec(memory_space=SMEM)] * count


def dot(a, b, dims):
    return lax.dot_general(a, b, (dims, ((), ())), preferred_element_type=jnp.float32)


def select(equal):
    return jnp.where(equal, 1.0, 0.0).astype(jnp.bfloat16)


def window(start_ref, slot, row_count):
    start = start_ref[slot]
    base = pl.multiple_of(jnp.minimum(start // TILE * TILE, row_count - WINDOW), TILE)
    return pl.ds(base, WINDOW), start - base


def pack_rows(start_ref, count_ref, rows_ref, out_ref):
    lane = lax.broadcasted_iota(jnp.int32, (SLOT, WINDOW), 1)
    row = lax.broadcasted_iota(jnp.int32, (SLOT, WINDOW), 0)
    ahead = lane - row

    def step(slot, carry):
        span, skip = window(start_ref, slot, rows_ref.shape[0])
        chosen = select((ahead == skip) & (row < count_ref[slot]))
        out_ref[slot] = dot(chosen, rows_ref[span, :], ((1,), (0,))).astype(jnp.bfloat16)
        return carry

    lax.fori_loop(0, N_SEQ, step, 0, unroll=4)


def unpack_rows(start_ref, count_ref, packed_ref, sum_ref):
    lane = lax.broadcasted_iota(jnp.int32, (WINDOW, SLOT), 1)
    row = lax.broadcasted_iota(jnp.int32, (WINDOW, SLOT), 0)
    ahead = row - lane
    sum_ref[...] = jnp.zeros(sum_ref.shape, sum_ref.dtype)

    def step(slot, carry):
        span, skip = window(start_ref, slot, sum_ref.shape[0])
        chosen = select((ahead == skip) & (lane < count_ref[slot]))
        sum_ref[span, :] += dot(chosen, packed_ref[slot], ((1,), (0,)))
        return carry

    lax.fori_loop(0, N_SEQ, step, 0, unroll=4)


def block_rows(head_ref, behind_x, behind_y, unit):
    x, y = head_ref[0] // SIDE, head_ref[0] % SIDE
    block = (x + SIDE - behind_x) % SIDE * SIDE + (y + SIDE - behind_y) % SIDE
    return pl.ds(pl.multiple_of(block * unit, TILE), unit)


def pack_queries(start, count, queries):
    return pl.pallas_call(
        pack_rows,
        out_shape=jax.ShapeDtypeStruct((N_SEQ, SLOT, queries.shape[1]), jnp.bfloat16),
        in_specs=smem_specs(2) + vmem_specs(1),
        out_specs=pl.BlockSpec(memory_space=VMEM),
        name="pack_queries",
    )(start, count, queries)


def unpack_kernel(start_ref, count_ref, packed_ref, out_ref, sum_ref):
    unpack_rows(start_ref, count_ref, packed_ref, sum_ref)
    out_ref[...] = sum_ref[...].astype(jnp.bfloat16)


def unpack_grads(start, count, packed, row_count):
    shape = (row_count, packed.shape[2])
    return pl.pallas_call(
        unpack_kernel,
        out_shape=jax.ShapeDtypeStruct(shape, jnp.bfloat16),
        in_specs=smem_specs(2) + vmem_specs(1),
        out_specs=pl.BlockSpec(memory_space=VMEM),
        scratch_shapes=[pltpu.VMEM(shape, jnp.float32)],
        name="unpack_grads",
    )(start, count, packed)


def grad_kernel(start_ref, count_ref, head_ref, proj_ref, *refs):
    first, second, out_ref, rows_ref = refs[:SIDE], refs[SIDE : 2 * SIDE], refs[2 * SIDE], refs[2 * SIDE + 1]
    half = proj_ref.shape[1] // 2
    unit = rows_ref.shape[0] // (SIDE * SIDE)
    low = proj_ref[:, :half]
    high = proj_ref[:, half:]
    one = [dot(r[...], low, ((1,), (1,))) for r in first]
    two = [dot(r[...], high, ((1,), (1,))) for r in second]
    for a in range(SIDE):
        for b in range(SIDE):
            grads = one[a][b * unit : (b + 1) * unit] + two[b][a * unit : (a + 1) * unit]
            rows_ref[block_rows(head_ref, b, a, unit), :] = grads.astype(jnp.bfloat16)
    pack_rows(start_ref, count_ref, rows_ref, out_ref)


def attention_grads(start, count, head, out_proj, first, second):
    inner = out_proj.shape[0]
    row_count = SIDE * first[0].shape[0]
    return pl.pallas_call(
        grad_kernel,
        out_shape=jax.ShapeDtypeStruct((N_SEQ, SLOT, inner), jnp.bfloat16),
        in_specs=smem_specs(3) + vmem_specs(1 + 2 * SIDE),
        out_specs=pl.BlockSpec(memory_space=VMEM),
        scratch_shapes=[pltpu.VMEM((row_count, inner), jnp.bfloat16)],
        name="attention_grads",
    )(start, count, head, out_proj, *first, *second)


def two_heads(rows):
    low = lax.broadcasted_iota(jnp.int32, rows.shape, 1) < LANE_SPLIT
    zero = jnp.zeros_like(rows)
    return jnp.concatenate([jnp.where(low, rows, zero), jnp.where(low, zero, rows)], axis=0)


def one_row(stacked):
    half = stacked.shape[0] // 2
    low = lax.broadcasted_iota(jnp.int32, (half, stacked.shape[1]), 1) < LANE_SPLIT
    return jnp.where(low, stacked[:half], stacked[half:])


def document(refs, doc, block_total):
    source_ref, start_ref, count_ref = refs
    start = start_ref[doc]
    base = jnp.minimum(start, block_total - CAP)
    return source_ref[doc], base, start - base, count_ref[doc]


def forward_kernel(source_ref, start_ref, count_ref, q_ref, k_ref, v_ref, att_ref, w_ref):
    att_ref[...] = jnp.zeros(att_ref.shape, att_ref.dtype)
    refs = (source_ref, start_ref, count_ref)
    lane = lax.broadcasted_iota(jnp.int32, (1, CAP * BLOCK), 1)
    for doc in range(DPS):
        source, base, skip, count = document(refs, doc, k_ref.shape[0] // BLOCK)
        tokens = pl.ds(pl.multiple_of(base * BLOCK, BLOCK), CAP * BLOCK)
        admitted = (lane >= skip * BLOCK) & (lane < (skip + count) * BLOCK)
        queries = two_heads(q_ref[source])
        scores = dot(queries, k_ref[tokens, :], ((1,), (1,))) * SCALE
        scores = jnp.where(admitted, scores, MASKED)
        top = jnp.max(scores, axis=1, keepdims=True)
        terms = jnp.exp(scores - top)
        scale = 1.0 / jnp.sum(terms, axis=1, keepdims=True)
        weights = (terms * scale).astype(jnp.bfloat16)
        w_ref[doc] = weights
        mixed = dot(weights, v_ref[tokens, :], ((1,), (0,)))
        att_ref[source] = one_row(mixed).astype(jnp.bfloat16)


def forward(source, start, count, got_q, keys, values):
    return pl.pallas_call(
        forward_kernel,
        out_shape=(
            jax.ShapeDtypeStruct(got_q.shape, jnp.bfloat16),
            jax.ShapeDtypeStruct((DPS, 2 * SLOT, 3 * BLOCK), jnp.bfloat16),
        ),
        in_specs=smem_specs(3) + vmem_specs(3),
        out_specs=tuple(vmem_specs(2)),
        name="forward",
    )(source, start, count, got_q, keys, values)


def backward_kernel(
    source_ref, start_ref, count_ref, q_ref, g_ref, att_ref, w_ref, k_ref, v_ref, dq_ref, dk_ref, dv_ref
):
    dq_ref[...] = jnp.zeros(dq_ref.shape, dq_ref.dtype)
    refs = (source_ref, start_ref, count_ref)
    for doc in range(DPS):
        source, base, skip, _ = document(refs, doc, k_ref.shape[0] // BLOCK)
        tokens = pl.ds(pl.multiple_of(base * BLOCK, BLOCK), CAP * BLOCK)
        queries = two_heads(q_ref[source])
        grads = two_heads(g_ref[source])
        attended = att_ref[source].astype(jnp.float32)
        both = jnp.concatenate([attended, attended], axis=0)
        delta = jnp.sum(grads.astype(jnp.float32) * both, axis=1, keepdims=True)
        weights = w_ref[doc]
        dprobs = dot(grads, v_ref[tokens, :], ((1,), (1,)))
        dscores = (weights.astype(jnp.float32) * (dprobs - delta)).astype(jnp.bfloat16)
        dq = dot(dscores, k_ref[tokens, :], ((1,), (0,)))
        dq_ref[source] = (one_row(dq) * SCALE).astype(jnp.bfloat16)
        dk = (dot(dscores, queries, ((0,), (0,))) * SCALE).astype(jnp.bfloat16)
        dv = dot(weights, grads, ((0,), (0,))).astype(jnp.bfloat16)
        for part in range(CAP):
            rows = pl.ds(pl.multiple_of((base + part) * BLOCK, BLOCK), BLOCK)
            span = slice(part * BLOCK, (part + 1) * BLOCK)
            if part == CAP - 1:
                dk_ref[rows, :] = dk[span]
                dv_ref[rows, :] = dv[span]
            else:
                keep = skip > part
                dk_ref[rows, :] = jnp.where(keep, dk_ref[rows, :], dk[span])
                dv_ref[rows, :] = jnp.where(keep, dv_ref[rows, :], dv[span])


def backward(source, start, count, got_q, got_g, attended, weights, keys, values):
    return pl.pallas_call(
        backward_kernel,
        out_shape=(
            jax.ShapeDtypeStruct(got_q.shape, jnp.bfloat16),
            jax.ShapeDtypeStruct(keys.shape, jnp.bfloat16),
            jax.ShapeDtypeStruct(values.shape, jnp.bfloat16),
        ),
        in_specs=smem_specs(3) + vmem_specs(6),
        out_specs=tuple(vmem_specs(3)),
        name="backward",
    )(source, start, count, got_q, got_g, attended, weights, keys, values)


def mixed_kernel(start_ref, count_ref, head_ref, packed_ref, proj_ref, *refs):
    first, second = refs[:SIDE], refs[SIDE : 2 * SIDE]
    m_first, m_second = refs[2 * SIDE : 3 * SIDE], refs[3 * SIDE : 4 * SIDE]
    even_ref, odd_ref, sum_ref = refs[4 * SIDE :]
    unpack_rows(start_ref, count_ref, packed_ref, sum_ref)
    unit = sum_ref.shape[0] // (SIDE * SIDE)
    half = proj_ref.shape[1] // 2
    blocks = [
        [sum_ref[block_rows(head_ref, b, a, unit), :].astype(jnp.bfloat16) for b in range(SIDE)]
        for a in range(SIDE)
    ]
    rows = [jnp.concatenate(blocks[a], axis=0) for a in range(SIDE)]
    rows_two = [jnp.concatenate([blocks[a][b] for a in range(SIDE)], axis=0) for b in range(SIDE)]
    sums = []
    for part, ins, outs, cols in (
        (rows, first, m_first, slice(0, half)),
        (rows_two, second, m_second, slice(half, 2 * half)),
    ):
        term = None
        for p in range(SIDE):
            outs[p][...] = dot(part[p], proj_ref[:, cols], ((1,), (0,))).astype(jnp.bfloat16)
            more = dot(part[p], ins[p][...], ((0,), (0,)))
            term = more if term is None else term + more
        sums.append(term)
    per_half = half // BLOCK
    for h in range(2):
        for c in range(per_half):
            chunk = h * per_half + c
            target = even_ref if chunk % 2 == 0 else odd_ref
            target[chunk // 2] = sums[h][:, c * BLOCK : (c + 1) * BLOCK]


def mixed_parts(start, count, head, packed, out_proj, first, second):
    inner, width = out_proj.shape
    row_count = SIDE * first[0].shape[0]
    part = jax.ShapeDtypeStruct(first[0].shape, jnp.bfloat16)
    sums = jax.ShapeDtypeStruct((width // BLOCK // 2, inner, BLOCK), jnp.float32)
    outs = pl.pallas_call(
        mixed_kernel,
        out_shape=(part,) * (2 * SIDE) + (sums,) * 2,
        in_specs=smem_specs(3) + vmem_specs(2 + 2 * SIDE),
        out_specs=tuple(vmem_specs(2 * SIDE + 2)),
        scratch_shapes=[pltpu.VMEM((row_count, inner), jnp.float32)],
        name="mixed_parts",
    )(start, count, head, packed, out_proj, *first, *second)
    return outs[:SIDE], outs[SIDE : 2 * SIDE], outs[2 * SIDE], outs[2 * SIDE + 1]


def along_x(value, k):
    perm = [(x * SIDE + y, (x + k) % SIDE * SIDE + y) for x in range(SIDE) for y in range(SIDE)]
    return lax.ppermute(value, "head", perm)


def along_y(value, k):
    perm = [(x * SIDE + y, x * SIDE + (y + k) % SIDE) for x in range(SIDE) for y in range(SIDE)]
    return lax.ppermute(value, "head", perm)


def along_z(value, k):
    perm = [(s, (s + 2 * k) % N_SEQ) for s in range(N_SEQ)]
    return lax.ppermute(value, "seq", perm)


def shift(value, move, k):
    return move(value, k)


def gather(value, one, two):
    rows = jnp.concatenate([value] + [shift(value, one, k) for k in range(1, SIDE)], axis=0)
    return [rows] + [shift(rows, two, k) for k in range(1, SIDE)]


def total(parts):
    out = parts[0].astype(jnp.float32)
    for part in parts[1:]:
        out = out + part.astype(jnp.float32)
    return out.astype(jnp.bfloat16)


def scatter_sum(parts, one, two):
    rows = total([parts[0]] + [shift(parts[k], one, SIDE - k) for k in range(1, SIDE)])
    unit = rows.shape[0] // SIDE
    return total(
        [rows[:unit]]
        + [shift(rows[k * unit : (k + 1) * unit], two, SIDE - k) for k in range(1, SIDE)]
    )


def to_all(value):
    return lax.all_to_all(value, "seq", split_axis=0, concat_axis=0, tiled=True)


def work(queries, enc_keys, enc_values, out_proj, out_grad, block_doc, query_doc):
    shard = lax.axis_index("seq")
    head = lax.axis_index("head").astype(jnp.int32)[None]
    row_count = queries.shape[0]
    half = out_grad.shape[1] // 2

    docs_here = lax.dynamic_slice_in_dim(query_doc, shard * row_count, row_count)
    slots = jnp.arange(N_SEQ, dtype=jnp.int32)[:, None]
    mine = docs_here[None, :] // DPS == slots
    rows = jnp.arange(row_count, dtype=jnp.int32)
    row_start = jnp.min(jnp.where(mine, rows[None, :], row_count - 1), axis=1)
    row_span = jnp.sum(mine.astype(jnp.int32), axis=1)
    got_q = to_all(pack_queries(row_start, row_span, queries))

    first = gather(out_grad[:, :half], along_x, along_y)
    second = gather(out_grad[:, half:], along_y, along_x)

    my_docs = shard * DPS + jnp.arange(DPS, dtype=jnp.int32)
    all_rows = jnp.arange(query_doc.shape[0], dtype=jnp.int32)
    source = jnp.max(jnp.where(query_doc[None, :] == my_docs[:, None], all_rows[None, :], 0), axis=1) // row_count
    local_blocks = enc_keys.shape[0] // BLOCK
    blocks_here = lax.dynamic_slice_in_dim(block_doc, shard * local_blocks, local_blocks)
    start = jnp.sum((blocks_here[None, :] < my_docs[:, None]).astype(jnp.int32), axis=1)
    count = jnp.sum((blocks_here[None, :] == my_docs[:, None]).astype(jnp.int32), axis=1)

    attended, weights = forward(source, start, count, got_q, enc_keys, enc_values)
    home = to_all(attended)
    got_g = to_all(attention_grads(row_start, row_span, head, out_proj, first, second))

    m_first, m_second, even, odd = mixed_parts(row_start, row_span, head, home, out_proj, first, second)
    mixed = jnp.concatenate(
        [scatter_sum(m_first, along_y, along_x), scatter_sum(m_second, along_x, along_y)],
        axis=1,
    )

    core = shard % 2
    swap = [(s, s ^ 1) for s in range(N_SEQ)]
    theirs = jnp.where(core == 0, odd, even).astype(jnp.bfloat16)
    other = lax.ppermute(theirs, "seq", swap)
    pair = (jnp.where(core == 0, even, odd) + other.astype(jnp.float32)).astype(jnp.bfloat16)
    chips = N_SEQ // 2
    turned = lax.dynamic_slice_in_dim(jnp.concatenate([pair, pair], axis=0), shard // 2, chips)
    terms = [turned[0]] + [shift(turned[k], along_z, k) for k in range(1, chips)]
    grad_wo = terms[0].astype(jnp.float32)
    for term in terms[1:]:
        grad_wo = grad_wo + term.astype(jnp.float32)

    grads_q, grad_k, grad_v = backward(
        source, start, count, got_q, got_g, attended, weights, enc_keys, enc_values
    )
    grad_q = unpack_grads(row_start, row_span, to_all(grads_q), row_count)
    return (mixed, grad_q, grad_k, grad_v, grad_wo)


def solution(mesh):
    placed = (
        P("seq", "head"),
        P("seq", "head"),
        P("seq", "head"),
        P("head", None),
        P(("seq", "head"), None),
        P(),
        P(),
    )
    return jax.shard_map(
        work,
        mesh=mesh,
        in_specs=placed,
        out_specs=(
            P(("seq", "head"), None),
            P("seq", "head"),
            P("seq", "head"),
            P("seq", "head"),
            P("head", "seq"),
        ),
        check_vma=False,
    )
```

time: 193 us -> 197 us (1.021)
  starting transfers between devices: 62.8 us -> 72.3 us
  waiting for transfers between devices: 79.6 us -> 83.9 us
  Pallas kernels: 32.6 us -> 29 us
  local copies, waits for them, and re-layouts: 5.69 us -> 2.67 us
    ppermute x1 -> x8, starting transfers between devices: 0.22 us -> 15.4 us  [the longest x7 15.1 us: along_z(): return lax.ppermute(value, 'seq', perm)]
    ppermute x12, waiting for transfers between devices: 24.1 us -> 31.2 us  [along_y(): return lax.ppermute(value, 'head', perm)]
    all_to_all x1 -> x0, waiting for transfers between devices: 6.03 us -> none  [shards(): lax.all_to_all(pair, 'seq', split_axis=0, concat_axis=0, axis_index_group...]
    all_to_all x1 -> x0, starting transfers between devices: 5.99 us -> none  [shards(): lax.all_to_all(pair, 'seq', split_axis=0, concat_axis=0, axis_index_group...]
    broadcast_in_dim x4 -> x0, local copies, waits for them, and re-layouts: 3.04 us -> none  [the longest x1 0.96 us: shards(): grad_q = unpack_grads(slot_row[:, None], to_all(grads_q))]
    ppermute x1 -> x8, waiting for transfers between devices: 0.01 us -> 2.98 us  [the longest x7 2.97 us: along_z(): return lax.ppermute(value, 'seq', perm)]
    all_to_all x4, starting transfers between devices: 24.7 us -> 26.9 us  [to_all(): return lax.all_to_all(value, 'seq', split_axis=0, concat_axis=0, tiled=True)]
    ppermute x12, starting transfers between devices: 20.9 us -> 18.8 us  [along_y(): return lax.ppermute(value, 'head', perm)]
  transfers between devices with their start and end apart: 30 -> 36, of which waited for: 12 -> 16; matrix products, arithmetic and copies ran while one was open for 5% -> 3% of each run, Pallas kernels for 12% -> 9%
where the time goes in v2:
time: 197 us; the launch traced here: 196 us
  waiting for transfers between devices  83.9 us (43%)
  starting transfers between devices  72.3 us (37%)
  Pallas kernels  29 us (15%)
  other arithmetic  7.49 us (4%)
  local copies, waits for them, and re-layouts  2.67 us (1%)
    ppermute x12, waiting for transfers between devices, along_x(): return lax.ppermute(value, 'head', perm)  32.9 us
    ppermute x12, waiting for transfers between devices, along_y(): return lax.ppermute(value, 'head', perm)  31.2 us
    all_to_all x4, starting transfers between devices, to_all(): return lax.all_to_all(value, 'seq', split_axis=0, concat_axis=0, tiled=True)  26.9 us
    ppermute x12, starting transfers between devices, along_y(): return lax.ppermute(value, 'head', perm)  18.8 us
    all_to_all x4, waiting for transfers between devices, to_all(): return lax.all_to_all(value, 'seq', split_axis=0, concat_axis=0, tiled=True)  16.9 us
    ppermute x7, starting transfers between devices, along_z(): return lax.ppermute(value, 'seq', perm)  15.1 us
    ppermute x12, starting transfers between devices, along_x(): return lax.ppermute(value, 'head', perm)  11.2 us
    pallas_call x1, Pallas kernels, backward(): pl.pallas_call(backward_kernel, out_shape=(jax.ShapeDtypeStruct(got_q.sha...  6.63 us
  transfers between devices with their start and end apart: 36, of which 16 were waited for; matrix products, arithmetic and copies ran while one was open for 3% of the time, Pallas kernels for 9%

profile of v2, /device:TPU:1, one launch (start us, length us, event | category | flops | bytes accessed | tf_op | source)
XLA Modules:
  0.0 196.3 jit_solution(15494135488932490232)
XLA Ops:
  2.2 2.8 %pack_queries.1 = bf16[16,144,128]{2,1,0:T(8,128)(2,1)} custom-call(s32[16]{0:T(128)} %get-tuple-element.36.start_ref, s32[16]{0:T(128)} %get-tuple-element.35.count_ref, bf16[768,128]{1,0:T(8,128)(2,1)} %rows_ref.1), custom_call_target="tpu_custom_call" | custom-call | tf_op jit(solution)/shard_map/pack_queries/pallas_call | solution.py:83
  5.0 10.1 %all-to-all-start = ((bf16[16,144,128]{2,1,0:T(8,128)(2,1)}), bf16[16,144,128]{2,1,0:T(8,128)(2,1)S(1)}, u32[]{:S(2)}, u32[]{:S(2)}) async-start(bf16[16,144,128]{2,1,0:T(8,128)(2,1)} %pack_queries.1), calls=%async_computation | async-start | bytes 1179648 | tf_op jit(solution)/shard_map/all_to_all | solution.py:324
  16.7 16.9 %all-to-all-done.q_ref = bf16[16,144,128]{2,1,0:T(8,128)(2,1)S(1)} async-done(((bf16[16,144,128]{2,1,0:T(8,128)(2,1)}), bf16[16,144,128]{2,1,0:T(8,128)(2,1)S(1)}, u32[]{:S(2)}, u32[]{:S(2)}) %all-to-all-start) | async-done | bytes 589856 | tf_op jit(solution)/shard_map/all_to_all | solution.py:324
  34.4 6.2 %forward.1 = (bf16[16,144,128]{2,1,0:T(8,128)(2,1)}, bf16[8,288,384]{2,1,0:T(8,128)(2,1)}) custom-call(s32[8]{0:T(128)} %and_select_fusion.source_ref, s32[8]{0:T(128)} %get-tuple-element.38.start_ref, s32[8]{0:T(128)} %get-tuple-element.37.count_ref, bf16[16,144,128]{2,1,0:T(8,128)(2,1)} %copy-done, bf16[2048,128]{1,0:T(8,128)(2,1)} %k_ref.3, ...), custom_call_target="tpu_custom_call" | custom-call | tf_op jit(solution)/shard_map/forward/pallas_call | solution.py:177
  40.6 3.5 %all-to-all-start.1 = ((bf16[16,144,128]{2,1,0:T(8,128)(2,1)}), bf16[16,144,128]{2,1,0:T(8,128)(2,1)S(1)}, u32[]{:S(2)}, u32[]{:S(2)}) async-start(bf16[16,144,128]{2,1,0:T(8,128)(2,1)} %get-tuple-element.20.att_ref), calls=%async_computation.1 | async-start | bytes 1179648 | tf_op jit(solution)/shard_map/all_to_all | solution.py:324
  44.1 2.6 %collective-permute-start.2 = (bf16[48,1024]{1,0:T(8,128)(2,1)S(1)}, bf16[48,1024]{1,0:T(8,128)(2,1)S(1)}, u32[]{:S(2)}, u32[]{:S(2)}) collective-permute-start(bf16[48,1024]{1,0:T(8,128)(2,1)S(1)} %get-tuple-element.53), channel_id=1, source_target_pairs={{0,12},{1,13},{2,14},{3,15},{4,0},{5,1},{6,2},{7,3},{8,4},{9,5},{1... | collective-permute-start | bytes 294920 | tf_op jit(solution)/shard_map/ppermute | solution.py:285
  47.8 3.3 %collective-permute-done.2 = bf16[48,1024]{1,0:T(8,128)(2,1)S(1)} collective-permute-done((bf16[48,1024]{1,0:T(8,128)(2,1)S(1)}, bf16[48,1024]{1,0:T(8,128)(2,1)S(1)}, u32[]{:S(2)}, u32[]{:S(2)}) %collective-permute-start.2) | collective-permute-done | bytes 98336 | tf_op jit(solution)/shard_map/ppermute | solution.py:285
  55.1 2.8 %collective-permute-start.5 = (bf16[192,1024]{1,0:T(8,128)(2,1)S(1)}, bf16[192,1024]{1,0:T(8,128)(2,1)S(1)}, u32[]{:S(2)}, u32[]{:S(2)}) collective-permute-start(bf16[192,1024]{1,0:T(8,128)(2,1)S(1)} %pad_maximum_fusion.refs_0_), channel_id=1, source_target_pairs={{0,3},{1,0},{2,1},{3,2},{4,7},{5,4},{6,5},{7,6},{8,11},{9,8},{10,9... | collective-permute-start | bytes 1179656 | tf_op jit(solution)/shard_map/ppermute | solution.py:290
  59.4 3.6 %collective-permute-start.4 = (bf16[192,1024]{1,0:T(8,128)(2,1)S(1)}, bf16[192,1024]{1,0:T(8,128)(2,1)S(1)}, u32[]{:S(2)}, u32[]{:S(2)}) collective-permute-start(bf16[192,1024]{1,0:T(8,128)(2,1)S(1)} %pad_maximum_fusion.refs_0_), channel_id=1, source_target_pairs={{0,2},{1,3},{2,0},{3,1},{4,6},{5,7},{6,4},{7,5},{8,10},{9,11},{10,... | collective-permute-start | bytes 1179656 | tf_op jit(solution)/shard_map/ppermute | solution.py:290
  63.0 15.5 %collective-permute-done.8 = bf16[48,1024]{1,0:T(8,128)(2,1)S(1)} collective-permute-done((bf16[48,1024]{1,0:T(8,128)(2,1)S(1)}, bf16[48,1024]{1,0:T(8,128)(2,1)S(1)}, u32[]{:S(2)}, u32[]{:S(2)}) %collective-permute-start.8) | collective-permute-done | bytes 98336 | tf_op jit(solution)/shard_map/ppermute | solution.py:290
  80.3 10.0 %collective-permute-done.3.refs_1_ = bf16[192,1024]{1,0:T(8,128)(2,1)S(1)} collective-permute-done((bf16[192,1024]{1,0:T(8,128)(2,1)S(1)}, bf16[192,1024]{1,0:T(8,128)(2,1)S(1)}, u32[]{:S(2)}, u32[]{:S(2)}) %collective-permute-start.3) | collective-permute-done | bytes 393248 | tf_op jit(solution)/shard_map/ppermute | solution.py:290
  90.3 9.5 %collective-permute-done.9.refs_5_ = bf16[192,1024]{1,0:T(8,128)(2,1)} collective-permute-done((bf16[192,1024]{1,0:T(8,128)(2,1)S(1)}, bf16[192,1024]{1,0:T(8,128)(2,1)}, u32[]{:S(2)}, u32[]{:S(2)}) %collective-permute-start.9) | collective-permute-done | bytes 393248 | tf_op jit(solution)/shard_map/ppermute | solution.py:285
  99.8 4.8 %attention_grads.1 = bf16[16,144,128]{2,1,0:T(8,128)(2,1)} custom-call(s32[16]{0:T(128)} %get-tuple-element.36.start_ref, s32[16]{0:T(128)} %get-tuple-element.35.count_ref, s32[1]{0:T(128)} %bitcast.head_ref, bf16[128,2048]{1,0:T(8,128)(2,1)} %proj_ref.3, bf16[192,1024]{1,0:T(8,128)(2,1)} %copy-done.1, bf16[192,1024]{1,0:T(8,128)(2,1)} %copy-done.8, ...), custom_call_target="tpu_custom_call" | custom-call | tf_op jit(solution)/shard_map/attention_grads/pallas_call | solution.py:127
  104.6 3.9 %all-to-all-start.2 = ((bf16[16,144,128]{2,1,0:T(8,128)(2,1)}), bf16[16,144,128]{2,1,0:T(8,128)(2,1)S(1)}, u32[]{:S(2)}, u32[]{:S(2)}) async-start(bf16[16,144,128]{2,1,0:T(8,128)(2,1)} %attention_grads.1), calls=%async_computation.2 | async-start | bytes 1179648 | tf_op jit(solution)/shard_map/all_to_all | solution.py:324
  108.5 5.8 %mixed_parts.1 = (bf16[192,1024]{1,0:T(8,128)(2,1)}, bf16[192,1024]{1,0:T(8,128)(2,1)}, bf16[192,1024]{1,0:T(8,128)(2,1)}, bf16[192,1024]{1,0:T(8,128)(2,1)}, bf...) custom-call(s32[16]{0:T(128)} %get-tuple-element.36.start_ref, ...), custom_call_target="tpu_custom_call" | custom-call | tf_op jit(solution)/shard_map/mixed_parts/pallas_call | solution.py:272
  115.7 5.9 %collective-permute-start.12 = (bf16[192,1024]{1,0:T(8,128)(2,1)}, bf16[192,1024]{1,0:T(8,128)(2,1)S(1)}, u32[]{:S(2)}, u32[]{:S(2)}) collective-permute-start(bf16[192,1024]{1,0:T(8,128)(2,1)} %get-tuple-element.22), channel_id=1, source_target_pairs={{0,3},{1,0},{2,1},{3,2},{4,7},{5,4},{6,5},{7,6},{8,11},{9,8},{10,9... | collective-permute-start | bytes 1179656 | tf_op jit(solution)/shard_map/ppermute | solution.py:290
  129.4 3.8 %collective-permute-start.29 = (bf16[128,128]{1,0:T(8,128)(2,1)S(1)}, bf16[128,128]{1,0:T(8,128)(2,1)S(1)}, u32[]{:S(2)}, u32[]{:S(2)}) collective-permute-start(bf16[128,128]{1,0:T(8,128)(2,1)S(1)} %get-tuple-element.47), channel_id=1, source_target_pairs={{0,160},{16,176},{32,192},{48,208},{64,224},{80,240},{96,0},{112,1... | collective-permute-start | bytes 98312 | tf_op jit(solution)/shard_map/ppermute | solution.py:295
  135.1 3.0 %collective-permute-start.27 = (bf16[128,128]{1,0:T(8,128)(2,1)S(1)}, bf16[128,128]{1,0:T(8,128)(2,1)S(1)}, u32[]{:S(2)}, u32[]{:S(2)}) collective-permute-start(bf16[128,128]{1,0:T(8,128)(2,1)S(1)} %get-tuple-element.49), channel_id=1, source_target_pairs={{0,96},{16,112},{32,128},{48,144},{64,160},{80,176},{96,192},{112,... | collective-permute-start | bytes 98312 | tf_op jit(solution)/shard_map/ppermute | solution.py:295
  143.8 6.6 %backward.1 = (bf16[16,144,128]{2,1,0:T(8,128)(2,1)}, bf16[2048,128]{1,0:T(8,128)(2,1)}, bf16[2048,128]{1,0:T(8,128)(2,1)}) custom-call(s32[8]{0:T(128)} %and_select_fusion.source_ref, s32[8]{0:T(128)} %get-tuple-element.38.start_ref, s32[8]{0:T(128)} %get-tuple-element.37.count_ref, bf16[16,144,128]{2,1,0:T(8,128)(2,1)} %copy-done, ...), custom_call_target="tpu_custom_call" | custom-call | tf_op jit(solution)/shard_map/backward/pallas_call | solution.py:222
  150.4 9.4 %all-to-all-start.3 = ((bf16[16,144,128]{2,1,0:T(8,128)(2,1)}), bf16[16,144,128]{2,1,0:T(8,128)(2,1)S(1)}, u32[]{:S(2)}, u32[]{:S(2)}) async-start(bf16[16,144,128]{2,1,0:T(8,128)(2,1)} %get-tuple-element.30), calls=%async_computation.3 | async-start | bytes 1179648 | tf_op jit(solution)/shard_map/all_to_all | solution.py:324
  165.2 5.6 %collective-permute-done.18 = bf16[192,1024]{1,0:T(8,128)(2,1)S(1)} collective-permute-done((bf16[192,1024]{1,0:T(8,128)(2,1)}, bf16[192,1024]{1,0:T(8,128)(2,1)S(1)}, u32[]{:S(2)}, u32[]{:S(2)}) %collective-permute-start.18) | collective-permute-done | bytes 393248 | tf_op jit(solution)/shard_map/ppermute | solution.py:285
  173.4 9.1 %collective-permute-done.20 = bf16[192,1024]{1,0:T(8,128)(2,1)S(1)} collective-permute-done((bf16[192,1024]{1,0:T(8,128)(2,1)}, bf16[192,1024]{1,0:T(8,128)(2,1)S(1)}, u32[]{:S(2)}, u32[]{:S(2)}) %collective-permute-start.20) | collective-permute-done | bytes 393248 | tf_op jit(solution)/shard_map/ppermute | solution.py:285
  186.7 5.1 %collective-permute-done.23 = bf16[48,1024]{1,0:T(8,128)(2,1)S(1)} collective-permute-done((bf16[48,1024]{1,0:T(8,128)(2,1)S(1)}, bf16[48,1024]{1,0:T(8,128)(2,1)S(1)}, u32[]{:S(2)}, u32[]{:S(2)}) %collective-permute-start.23) | collective-permute-done | bytes 98336 | tf_op jit(solution)/shard_map/ppermute | solution.py:290
  193.5 2.8 %unpack_grads.1 = bf16[768,128]{1,0:T(8,128)(2,1)} custom-call(s32[16]{0:T(128)} %get-tuple-element.36.start_ref, s32[16]{0:T(128)} %get-tuple-element.35.count_ref, bf16[16,144,128]{2,1,0:T(8,128)(2,1)} %copy-done.4), custom_call_target="tpu_custom_call" | custom-call | tf_op jit(solution)/shard_map/unpack_grads/pallas_call | solution.py:99
  (108 shorter events, 43.0 us)
Async XLA Ops:
  5.0 28.6 %all-to-all-start = ((bf16[16,144,128]{2,1,0:T(8,128)(2,1)}), bf16[16,144,128]{2,1,0:T(8,128)(2,1)S(1)}, u32[]{:S(2)}, u32[]{:S(2)}) async-start(bf16[16,144,128]{2,1,0:T(8,128)(2,1)} %pack_queries.1), calls=%async_computation | async-start | bytes 1179648 | tf_op jit(solution)/shard_map/all_to_all | solution.py:324
  40.6 63.9 %all-to-all-start.1 = ((bf16[16,144,128]{2,1,0:T(8,128)(2,1)}), bf16[16,144,128]{2,1,0:T(8,128)(2,1)S(1)}, u32[]{:S(2)}, u32[]{:S(2)}) async-start(bf16[16,144,128]{2,1,0:T(8,128)(2,1)} %get-tuple-element.20.att_ref), calls=%async_computation.1 | async-start | bytes 1179648 | tf_op jit(solution)/shard_map/all_to_all | solution.py:324
  55.1 24.1 %collective-permute-start.5 = (bf16[192,1024]{1,0:T(8,128)(2,1)S(1)}, bf16[192,1024]{1,0:T(8,128)(2,1)S(1)}, u32[]{:S(2)}, u32[]{:S(2)}) collective-permute-start(bf16[192,1024]{1,0:T(8,128)(2,1)S(1)} %pad_maximum_fusion.refs_0_), channel_id=1, source_target_pairs={{0,3},{1,0},{2,1},{3,2},{4,7},{5,4},{6,5},{7,6},{8,11},{9,8},{10,9... | collective-permute-start | bytes 1179656 | tf_op jit(solution)/shard_map/ppermute | solution.py:290
  57.9 20.5 %collective-permute-start.8 = (bf16[48,1024]{1,0:T(8,128)(2,1)S(1)}, bf16[48,1024]{1,0:T(8,128)(2,1)S(1)}, u32[]{:S(2)}, u32[]{:S(2)}) collective-permute-start(bf16[48,1024]{1,0:T(8,128)(2,1)S(1)} %get-tuple-element.52), channel_id=1, source_target_pairs={{0,3},{1,0},{2,1},{3,2},{4,7},{5,4},{6,5},{7,6},{8,11},{9,8},{10,9... | collective-permute-start | bytes 294920 | tf_op jit(solution)/shard_map/ppermute | solution.py:290
  58.4 20.1 %collective-permute-start.7 = (bf16[48,1024]{1,0:T(8,128)(2,1)S(1)}, bf16[48,1024]{1,0:T(8,128)(2,1)S(1)}, u32[]{:S(2)}, u32[]{:S(2)}) collective-permute-start(bf16[48,1024]{1,0:T(8,128)(2,1)S(1)} %get-tuple-element.52), channel_id=1, source_target_pairs={{0,2},{1,3},{2,0},{3,1},{4,6},{5,7},{6,4},{7,5},{8,10},{9,11},{10,... | collective-permute-start | bytes 294920 | tf_op jit(solution)/shard_map/ppermute | solution.py:290
  58.4 20.0 %collective-permute-start.6 = (bf16[48,1024]{1,0:T(8,128)(2,1)S(1)}, bf16[48,1024]{1,0:T(8,128)(2,1)S(1)}, u32[]{:S(2)}, u32[]{:S(2)}) collective-permute-start(bf16[48,1024]{1,0:T(8,128)(2,1)S(1)} %get-tuple-element.52), channel_id=1, source_target_pairs={{0,1},{1,2},{2,3},{3,0},{4,5},{5,6},{6,7},{7,4},{8,9},{9,10},{10,1... | collective-permute-start | bytes 294920 | tf_op jit(solution)/shard_map/ppermute | solution.py:290
  59.4 20.9 %collective-permute-start.4 = (bf16[192,1024]{1,0:T(8,128)(2,1)S(1)}, bf16[192,1024]{1,0:T(8,128)(2,1)S(1)}, u32[]{:S(2)}, u32[]{:S(2)}) collective-permute-start(bf16[192,1024]{1,0:T(8,128)(2,1)S(1)} %pad_maximum_fusion.refs_0_), channel_id=1, source_target_pairs={{0,2},{1,3},{2,0},{3,1},{4,6},{5,7},{6,4},{7,5},{8,10},{9,11},{10,... | collective-permute-start | bytes 1179656 | tf_op jit(solution)/shard_map/ppermute | solution.py:290
  78.4 11.8 %collective-permute-start.3 = (bf16[192,1024]{1,0:T(8,128)(2,1)S(1)}, bf16[192,1024]{1,0:T(8,128)(2,1)S(1)}, u32[]{:S(2)}, u32[]{:S(2)}) collective-permute-start(bf16[192,1024]{1,0:T(8,128)(2,1)S(1)} %pad_maximum_fusion.refs_0_), channel_id=1, source_target_pairs={{0,1},{1,2},{2,3},{3,0},{4,5},{5,6},{6,7},{7,4},{8,9},{9,10},{10,1... | collective-permute-start | bytes 1179656 | tf_op jit(solution)/shard_map/ppermute | solution.py:290
  78.5 11.8 %collective-permute-start.11 = (bf16[192,1024]{1,0:T(8,128)(2,1)S(1)}, bf16[192,1024]{1,0:T(8,128)(2,1)S(1)}, u32[]{:S(2)}, u32[]{:S(2)}) collective-permute-start(bf16[192,1024]{1,0:T(8,128)(2,1)S(1)} %pad_maximum_fusion.1.refs_4_), channel_id=1, source_target_pairs={{0,12},{1,13},{2,14},{3,15},{4,0},{5,1},{6,2},{7,3},{8,4},{9,5},{1... | collective-permute-start | bytes 1179656 | tf_op jit(solution)/shard_map/ppermute | solution.py:285
  78.6 11.7 %collective-permute-start.10 = (bf16[192,1024]{1,0:T(8,128)(2,1)S(1)}, bf16[192,1024]{1,0:T(8,128)(2,1)S(1)}, u32[]{:S(2)}, u32[]{:S(2)}) collective-permute-start(bf16[192,1024]{1,0:T(8,128)(2,1)S(1)} %pad_maximum_fusion.1.refs_4_), channel_id=1, source_target_pairs={{0,8},{1,9},{2,10},{3,11},{4,12},{5,13},{6,14},{7,15},{8,0},{9,1},... | collective-permute-start | bytes 1179656 | tf_op jit(solution)/shard_map/ppermute | solution.py:285
  79.2 20.6 %collective-permute-start.9 = (bf16[192,1024]{1,0:T(8,128)(2,1)S(1)}, bf16[192,1024]{1,0:T(8,128)(2,1)}, u32[]{:S(2)}, u32[]{:S(2)}) collective-permute-start(bf16[192,1024]{1,0:T(8,128)(2,1)S(1)} %pad_maximum_fusion.1.refs_4_), channel_id=1, source_target_pairs={{0,4},{1,5},{2,6},{3,7},{4,8},{5,9},{6,10},{7,11},{8,12},{9,13},{1... | collective-permute-start | bytes 1179656 | tf_op jit(solution)/shard_map/ppermute | solution.py:285
  104.6 38.4 %all-to-all-start.2 = ((bf16[16,144,128]{2,1,0:T(8,128)(2,1)}), bf16[16,144,128]{2,1,0:T(8,128)(2,1)S(1)}, u32[]{:S(2)}, u32[]{:S(2)}) async-start(bf16[16,144,128]{2,1,0:T(8,128)(2,1)} %attention_grads.1), calls=%async_computation.2 | async-start | bytes 1179648 | tf_op jit(solution)/shard_map/all_to_all | solution.py:324
  115.7 46.4 %collective-permute-start.12 = (bf16[192,1024]{1,0:T(8,128)(2,1)}, bf16[192,1024]{1,0:T(8,128)(2,1)S(1)}, u32[]{:S(2)}, u32[]{:S(2)}) collective-permute-start(bf16[192,1024]{1,0:T(8,128)(2,1)} %get-tuple-element.22), channel_id=1, source_target_pairs={{0,3},{1,0},{2,1},{3,2},{4,7},{5,4},{6,5},{7,6},{8,11},{9,8},{10,9... | collective-permute-start | bytes 1179656 | tf_op jit(solution)/shard_map/ppermute | solution.py:290
  121.6 41.1 %collective-permute-start.13 = (bf16[192,1024]{1,0:T(8,128)(2,1)}, bf16[192,1024]{1,0:T(8,128)(2,1)S(1)}, u32[]{:S(2)}, u32[]{:S(2)}) collective-permute-start(bf16[192,1024]{1,0:T(8,128)(2,1)} %get-tuple-element.23), channel_id=1, source_target_pairs={{0,2},{1,3},{2,0},{3,1},{4,6},{5,7},{6,4},{7,5},{8,10},{9,11},{10,... | collective-permute-start | bytes 1179656 | tf_op jit(solution)/shard_map/ppermute | solution.py:290
  122.9 39.9 %collective-permute-start.14 = (bf16[192,1024]{1,0:T(8,128)(2,1)}, bf16[192,1024]{1,0:T(8,128)(2,1)S(1)}, u32[]{:S(2)}, u32[]{:S(2)}) collective-permute-start(bf16[192,1024]{1,0:T(8,128)(2,1)} %get-tuple-element.24), channel_id=1, source_target_pairs={{0,1},{1,2},{2,3},{3,0},{4,5},{5,6},{6,7},{7,4},{8,9},{9,10},{10,1... | collective-permute-start | bytes 1179656 | tf_op jit(solution)/shard_map/ppermute | solution.py:290
  139.9 20.0 %collective-permute-start.26 = (bf16[128,128]{1,0:T(8,128)(2,1)S(1)}, bf16[128,128]{1,0:T(8,128)(2,1)S(1)}, u32[]{:S(2)}, u32[]{:S(2)}) collective-permute-start(bf16[128,128]{1,0:T(8,128)(2,1)S(1)} %get-tuple-element.50), channel_id=1, source_target_pairs={{0,64},{16,80},{32,96},{48,112},{64,128},{80,144},{96,160},{112,17... | collective-permute-start | bytes 98312 | tf_op jit(solution)/shard_map/ppermute | solution.py:295
  141.3 20.1 %collective-permute-start.31 = (bf16[128,128]{1,0:T(8,128)(2,1)S(1)}, bf16[128,128]{1,0:T(8,128)(2,1)S(1)}, u32[]{:S(2)}, u32[]{:S(2)}) collective-permute-start(bf16[128,128]{1,0:T(8,128)(2,1)S(1)} %get-tuple-element.51), channel_id=1, source_target_pairs={{0,224},{16,240},{32,0},{48,16},{64,32},{80,48},{96,64},{112,80},{... | collective-permute-start | bytes 98312 | tf_op jit(solution)/shard_map/ppermute | solution.py:295
  150.4 42.2 %all-to-all-start.3 = ((bf16[16,144,128]{2,1,0:T(8,128)(2,1)}), bf16[16,144,128]{2,1,0:T(8,128)(2,1)S(1)}, u32[]{:S(2)}, u32[]{:S(2)}) async-start(bf16[16,144,128]{2,1,0:T(8,128)(2,1)} %get-tuple-element.30), calls=%async_computation.3 | async-start | bytes 1179648 | tf_op jit(solution)/shard_map/all_to_all | solution.py:324
  159.9 10.9 %collective-permute-start.18 = (bf16[192,1024]{1,0:T(8,128)(2,1)}, bf16[192,1024]{1,0:T(8,128)(2,1)S(1)}, u32[]{:S(2)}, u32[]{:S(2)}) collective-permute-start(bf16[192,1024]{1,0:T(8,128)(2,1)} %get-tuple-element.26), channel_id=1, source_target_pairs={{0,12},{1,13},{2,14},{3,15},{4,0},{5,1},{6,2},{7,3},{8,4},{9,5},{1... | collective-permute-start | bytes 1179656 | tf_op jit(solution)/shard_map/ppermute | solution.py:285
  161.4 12.0 %collective-permute-start.19 = (bf16[192,1024]{1,0:T(8,128)(2,1)}, bf16[192,1024]{1,0:T(8,128)(2,1)S(1)}, u32[]{:S(2)}, u32[]{:S(2)}) collective-permute-start(bf16[192,1024]{1,0:T(8,128)(2,1)} %get-tuple-element.27), channel_id=1, source_target_pairs={{0,8},{1,9},{2,10},{3,11},{4,12},{5,13},{6,14},{7,15},{8,0},{9,1},... | collective-permute-start | bytes 1179656 | tf_op jit(solution)/shard_map/ppermute | solution.py:285
  162.1 20.5 %collective-permute-start.20 = (bf16[192,1024]{1,0:T(8,128)(2,1)}, bf16[192,1024]{1,0:T(8,128)(2,1)S(1)}, u32[]{:S(2)}, u32[]{:S(2)}) collective-permute-start(bf16[192,1024]{1,0:T(8,128)(2,1)} %get-tuple-element.28), channel_id=1, source_target_pairs={{0,4},{1,5},{2,6},{3,7},{4,8},{5,9},{6,10},{7,11},{8,12},{9,13},{1... | collective-permute-start | bytes 1179656 | tf_op jit(solution)/shard_map/ppermute | solution.py:285
  163.0 21.5 %collective-permute-start.15 = (bf16[48,1024]{1,0:T(8,128)(2,1)S(1)}, bf16[48,1024]{1,0:T(8,128)(2,1)S(1)}, u32[]{:S(2)}, u32[]{:S(2)}) collective-permute-start(bf16[48,1024]{1,0:T(8,128)(2,1)S(1)} %get-tuple-element.39), channel_id=1, source_target_pairs={{0,12},{1,13},{2,14},{3,15},{4,0},{5,1},{6,2},{7,3},{8,4},{9,5},{1... | collective-permute-start | bytes 294920 | tf_op jit(solution)/shard_map/ppermute | solution.py:285
  165.1 20.8 %collective-permute-start.17 = (bf16[48,1024]{1,0:T(8,128)(2,1)S(1)}, bf16[48,1024]{1,0:T(8,128)(2,1)S(1)}, u32[]{:S(2)}, u32[]{:S(2)}) collective-permute-start(bf16[48,1024]{1,0:T(8,128)(2,1)S(1)} %get-tuple-element.40), channel_id=1, source_target_pairs={{0,4},{1,5},{2,6},{3,7},{4,8},{5,9},{6,10},{7,11},{8,12},{9,13},{1... | collective-permute-start | bytes 294920 | tf_op jit(solution)/shard_map/ppermute | solution.py:285
  170.7 15.3 %collective-permute-start.16 = (bf16[48,1024]{1,0:T(8,128)(2,1)S(1)}, bf16[48,1024]{1,0:T(8,128)(2,1)S(1)}, u32[]{:S(2)}, u32[]{:S(2)}) collective-permute-start(bf16[48,1024]{1,0:T(8,128)(2,1)S(1)} %get-tuple-element.41), channel_id=1, source_target_pairs={{0,8},{1,9},{2,10},{3,11},{4,12},{5,13},{6,14},{7,15},{8,0},{9,1},... | collective-permute-start | bytes 294920 | tf_op jit(solution)/shard_map/ppermute | solution.py:285
  (28 other events, 331.3 us)

commit v3 on v2

--- a/solution.py
+++ b/solution.py
@@ -20,6 +20,8 @@
 
 VMEM = pltpu.MemorySpace.VMEM
 SMEM = pltpu.MemorySpace.SMEM
+HBM = pltpu.MemorySpace.HBM
+LIMIT = pltpu.CompilerParams(vmem_limit_bytes=20 << 20)
 
 
 def vmem_specs(count):
@@ -85,6 +87,7 @@
         out_shape=jax.ShapeDtypeStruct((N_SEQ, SLOT, queries.shape[1]), jnp.bfloat16),
         in_specs=smem_specs(2) + vmem_specs(1),
         out_specs=pl.BlockSpec(memory_space=VMEM),
+        compiler_params=LIMIT,
         name="pack_queries",
     )(start, count, queries)
 
@@ -102,6 +105,7 @@
         in_specs=smem_specs(2) + vmem_specs(1),
         out_specs=pl.BlockSpec(memory_space=VMEM),
         scratch_shapes=[pltpu.VMEM(shape, jnp.float32)],
+        compiler_params=LIMIT,
         name="unpack_grads",
     )(start, count, packed)
 
@@ -130,6 +134,7 @@
         in_specs=smem_specs(3) + vmem_specs(1 + 2 * SIDE),
         out_specs=pl.BlockSpec(memory_space=VMEM),
         scratch_shapes=[pltpu.VMEM((row_count, inner), jnp.bfloat16)],
+        compiler_params=LIMIT,
         name="attention_grads",
     )(start, count, head, out_proj, *first, *second)
 
@@ -153,10 +158,11 @@
     return source_ref[doc], base, start - base, count_ref[doc]
 
 
-def forward_kernel(source_ref, start_ref, count_ref, q_ref, k_ref, v_ref, att_ref, w_ref):
+def forward_kernel(source_ref, start_ref, count_ref, q_ref, k_ref, v_ref, att_ref, w_ref, kept_ref, sems):
     att_ref[...] = jnp.zeros(att_ref.shape, att_ref.dtype)
     refs = (source_ref, start_ref, count_ref)
     lane = lax.broadcasted_iota(jnp.int32, (1, CAP * BLOCK), 1)
+    copies = []
     for doc in range(DPS):
         source, base, skip, count = document(refs, doc, k_ref.shape[0] // BLOCK)
         tokens = pl.ds(pl.multiple_of(base * BLOCK, BLOCK), CAP * BLOCK)
@@ -168,20 +174,24 @@
         terms = jnp.exp(scores - top)
         scale = 1.0 / jnp.sum(terms, axis=1, keepdims=True)
         weights = (terms * scale).astype(jnp.bfloat16)
-        w_ref[doc] = weights
+        kept_ref[doc] = weights
+        copies.append(pltpu.make_async_copy(kept_ref.at[doc], w_ref.at[doc], sems.at[doc]))
+        copies[-1].start()
         mixed = dot(weights, v_ref[tokens, :], ((1,), (0,)))
         att_ref[source] = one_row(mixed).astype(jnp.bfloat16)
+    for copy in copies:
+        copy.wait()
 
 
 def forward(source, start, count, got_q, keys, values):
+    weights = (DPS, 2 * SLOT, CAP * BLOCK)
     return pl.pallas_call(
         forward_kernel,
-        out_shape=(
-            jax.ShapeDtypeStruct(got_q.shape, jnp.bfloat16),
-            jax.ShapeDtypeStruct((DPS, 2 * SLOT, 3 * BLOCK), jnp.bfloat16),
-        ),
+        out_shape=(jax.ShapeDtypeStruct(got_q.shape, jnp.bfloat16), HBM(weights, jnp.bfloat16)),
         in_specs=smem_specs(3) + vmem_specs(3),
-        out_specs=tuple(vmem_specs(2)),
+        out_specs=(*vmem_specs(1), pl.BlockSpec(memory_space=HBM)),
+        scratch_shapes=[pltpu.VMEM(weights, jnp.bfloat16), pltpu.SemaphoreType.DMA((DPS,))],
+        compiler_params=LIMIT,
         name="forward",
     )(source, start, count, got_q, keys, values)
 
@@ -228,14 +238,15 @@
         ),
         in_specs=smem_specs(3) + vmem_specs(6),
         out_specs=tuple(vmem_specs(3)),
+        compiler_params=LIMIT,
         name="backward",
     )(source, start, count, got_q, got_g, attended, weights, keys, values)
 
 
 def mixed_kernel(start_ref, count_ref, head_ref, packed_ref, proj_ref, *refs):
     first, second = refs[:SIDE], refs[SIDE : 2 * SIDE]
-    m_first, m_second = refs[2 * SIDE : 3 * SIDE], refs[3 * SIDE : 4 * SIDE]
-    even_ref, odd_ref, sum_ref = refs[4 * SIDE :]
+    outs = refs[2 * SIDE : 4 * SIDE]
+    even_ref, odd_ref, sum_ref, sent_ref, weight_ref, sems = refs[4 * SIDE :]
     unpack_rows(start_ref, count_ref, packed_ref, sum_ref)
     unit = sum_ref.shape[0] // (SIDE * SIDE)
     half = proj_ref.shape[1] // 2
@@ -245,14 +256,18 @@
     ]
     rows = [jnp.concatenate(blocks[a], axis=0) for a in range(SIDE)]
     rows_two = [jnp.concatenate([blocks[a][b] for a in range(SIDE)], axis=0) for b in range(SIDE)]
+    copies = []
+    for h, part in enumerate((rows, rows_two)):
+        cols = slice(h * half, (h + 1) * half)
+        for p in (1, 3, 2, 0):
+            place = h * SIDE + p
+            sent_ref[place] = dot(part[p], proj_ref[:, cols], ((1,), (0,))).astype(jnp.bfloat16)
+            copies.append(pltpu.make_async_copy(sent_ref.at[place], outs[place], sems.at[place]))
+            copies[-1].start()
     sums = []
-    for part, ins, outs, cols in (
-        (rows, first, m_first, slice(0, half)),
-        (rows_two, second, m_second, slice(half, 2 * half)),
-    ):
+    for part, ins in ((rows, first), (rows_two, second)):
         term = None
         for p in range(SIDE):
-            outs[p][...] = dot(part[p], proj_ref[:, cols], ((1,), (0,))).astype(jnp.bfloat16)
             more = dot(part[p], ins[p][...], ((0,), (0,)))
             term = more if term is None else term + more
         sums.append(term)
@@ -260,21 +275,31 @@
     for h in range(2):
         for c in range(per_half):
             chunk = h * per_half + c
-            target = even_ref if chunk % 2 == 0 else odd_ref
-            target[chunk // 2] = sums[h][:, c * BLOCK : (c + 1) * BLOCK]
+            weight_ref[chunk % 2, chunk // 2] = sums[h][:, c * BLOCK : (c + 1) * BLOCK]
+    for c, out_ref in enumerate((even_ref, odd_ref)):
+        copies.append(pltpu.make_async_copy(weight_ref.at[c], out_ref, sems.at[2 * SIDE + c]))
+        copies[-1].start()
+    for copy in copies:
+        copy.wait()
 
 
 def mixed_parts(start, count, head, packed, out_proj, first, second):
     inner, width = out_proj.shape
     row_count = SIDE * first[0].shape[0]
-    part = jax.ShapeDtypeStruct(first[0].shape, jnp.bfloat16)
-    sums = jax.ShapeDtypeStruct((width // BLOCK // 2, inner, BLOCK), jnp.float32)
+    part = HBM(first[0].shape, jnp.bfloat16)
+    sums = HBM((width // BLOCK // 2, inner, BLOCK), jnp.float32)
     outs = pl.pallas_call(
         mixed_kernel,
         out_shape=(part,) * (2 * SIDE) + (sums,) * 2,
         in_specs=smem_specs(3) + vmem_specs(2 + 2 * SIDE),
-        out_specs=tuple(vmem_specs(2 * SIDE + 2)),
-        scratch_shapes=[pltpu.VMEM((row_count, inner), jnp.float32)],
+        out_specs=tuple([pl.BlockSpec(memory_space=HBM)] * (2 * SIDE + 2)),
+        scratch_shapes=[
+            pltpu.VMEM((row_count, inner), jnp.float32),
+            pltpu.VMEM((2 * SIDE, *first[0].shape), jnp.bfloat16),
+            pltpu.VMEM((2, width // BLOCK // 2, inner, BLOCK), jnp.float32),
+            pltpu.SemaphoreType.DMA((2 * SIDE + 2,)),
+        ],
+        compiler_params=LIMIT,
         name="mixed_parts",
     )(start, count, head, packed, out_proj, *first, *second)
     return outs[:SIDE], outs[SIDE : 2 * SIDE], outs[2 * SIDE], outs[2 * SIDE + 1]
@@ -290,9 +315,11 @@
     return lax.ppermute(value, "head", perm)
 
 
-def along_z(value, k):
-    perm = [(s, (s + 2 * k) % N_SEQ) for s in range(N_SEQ)]
-    return lax.ppermute(value, "seq", perm)
+def halve(low, high, side, distance):
+    swap = [(s, s ^ distance) for s in range(N_SEQ)]
+    theirs = jnp.where(side == 0, high, low).astype(jnp.bfloat16)
+    other = lax.ppermute(theirs, "seq", swap)
+    return jnp.where(side == 0, low, high) + other.astype(jnp.float32)
 
 
 def shift(value, move, k):
@@ -312,12 +339,11 @@
 
 
 def scatter_sum(parts, one, two):
-    rows = total([parts[0]] + [shift(parts[k], one, SIDE - k) for k in range(1, SIDE)])
+    terms = [parts[0]] + [shift(parts[k], one, SIDE - k) for k in range(1, SIDE)]
+    rows = total(terms)
     unit = rows.shape[0] // SIDE
-    return total(
-        [rows[:unit]]
-        + [shift(rows[k * unit : (k + 1) * unit], two, SIDE - k) for k in range(1, SIDE)]
-    )
+    terms = [rows[:unit]] + [shift(rows[k * unit : (k + 1) * unit], two, SIDE - k) for k in range(1, SIDE)]
+    return total(terms)
 
 
 def to_all(value):
@@ -360,16 +386,12 @@
     )
 
     core = shard % 2
-    swap = [(s, s ^ 1) for s in range(N_SEQ)]
-    theirs = jnp.where(core == 0, odd, even).astype(jnp.bfloat16)
-    other = lax.ppermute(theirs, "seq", swap)
-    pair = (jnp.where(core == 0, even, odd) + other.astype(jnp.float32)).astype(jnp.bfloat16)
-    chips = N_SEQ // 2
-    turned = lax.dynamic_slice_in_dim(jnp.concatenate([pair, pair], axis=0), shard // 2, chips)
-    terms = [turned[0]] + [shift(turned[k], along_z, k) for k in range(1, chips)]
-    grad_wo = terms[0].astype(jnp.float32)
-    for term in terms[1:]:
-        grad_wo = grad_wo + term.astype(jnp.float32)
+    chip = shard // 2
+    grad_wo = halve(even, odd, core, 1)
+    for bit in range(3):
+        halves = grad_wo.reshape(-1, 2, *grad_wo.shape[1:])
+        grad_wo = halve(halves[:, 0], halves[:, 1], (chip >> bit) & 1, 2 << bit)
+    grad_wo = grad_wo[0]
 
     grads_q, grad_k, grad_v = backward(
         source, start, count, got_q, got_g, attended, weights, enc_keys, enc_values

time: 197 us -> 189 us (0.959)
  the two profiles are of different devices: /device:TPU:1 before, /device:TPU:8 now
where the time goes in v3:
time: 189 us; the launch traced here: 188 us
  starting transfers between devices  81.5 us (43%)
  waiting for transfers between devices  71 us (38%)
  Pallas kernels  24.9 us (13%)
  other arithmetic  5.95 us (3%)
  local copies, waits for them, and re-layouts  3.59 us (2%)
    ppermute x12, waiting for transfers between devices, along_y(): return lax.ppermute(value, 'head', perm)  37.3 us
    ppermute x12, starting transfers between devices, along_y(): return lax.ppermute(value, 'head', perm)  36.9 us
    all_to_all x4, starting transfers between devices, to_all(): return lax.all_to_all(value, 'seq', split_axis=0, concat_axis=0, tiled=True)  24.1 us
    all_to_all x4, waiting for transfers between devices, to_all(): return lax.all_to_all(value, 'seq', split_axis=0, concat_axis=0, tiled=True)  21.6 us
    ppermute x12, waiting for transfers between devices, along_x(): return lax.ppermute(value, 'head', perm)  10.8 us
    ppermute x12, starting transfers between devices, along_x(): return lax.ppermute(value, 'head', perm)  10.7 us
    ppermute x4, starting transfers between devices, halve(): other = lax.ppermute(theirs, 'seq', swap)  9.85 us
    pallas_call x1, Pallas kernels, forward(): pl.pallas_call(forward_kernel, out_shape=(jax.ShapeDtypeStruct(got_q.shap...  5.54 us
  transfers between devices with their start and end apart: 32, of which 13 were waited for; matrix products, arithmetic and copies ran while one was open for 2% of the time, Pallas kernels for 9%

profile of v3, /device:TPU:8, one launch (start us, length us, event | category | flops | bytes accessed | tf_op | source)
XLA Modules:
  0.0 187.8 jit_solution(3091720732829810723)
XLA Ops:
  5.0 8.7 %all-to-all-start = ((bf16[16,144,128]{2,1,0:T(8,128)(2,1)}), bf16[16,144,128]{2,1,0:T(8,128)(2,1)S(1)}, u32[]{:S(2)}, u32[]{:S(2)}) async-start(bf16[16,144,128]{2,1,0:T(8,128)(2,1)} %pack_queries.1), calls=%async_computation | async-start | bytes 1179648 | tf_op jit(solution)/shard_map/all_to_all | solution.py:350
  14.3 16.5 %all-to-all-done.q_ref = bf16[16,144,128]{2,1,0:T(8,128)(2,1)S(1)} async-done(((bf16[16,144,128]{2,1,0:T(8,128)(2,1)}), bf16[16,144,128]{2,1,0:T(8,128)(2,1)S(1)}, u32[]{:S(2)}, u32[]{:S(2)}) %all-to-all-start) | async-done | bytes 589856 | tf_op jit(solution)/shard_map/all_to_all | solution.py:350
  30.8 5.5 %forward.1 = (bf16[16,144,128]{2,1,0:T(8,128)(2,1)}, bf16[8,288,384]{2,1,0:T(8,128)(2,1)}) custom-call(s32[8]{0:T(128)S(1)} %and_select_fusion.source_ref, s32[8]{0:T(128)S(1)} %get-tuple-element.38.start_ref, s32[8]{0:T(128)S(1)} %get-tuple-element.37.count_ref, bf16[16,144,128]{2,1,0:T(8,128)(2,1)S(1)} %all-to-all-done.q_ref, ...), custom_call_target="tpu_custom_call" | custom-call | tf_op jit(solution)/shard_map/forward/pallas_call | solution.py:188
  36.4 4.6 %all-to-all-start.1 = ((bf16[16,144,128]{2,1,0:T(8,128)(2,1)}), bf16[16,144,128]{2,1,0:T(8,128)(2,1)S(1)}, u32[]{:S(2)}, u32[]{:S(2)}) async-start(bf16[16,144,128]{2,1,0:T(8,128)(2,1)} %get-tuple-element.20.att_ref), calls=%async_computation.1 | async-start | bytes 1179648 | tf_op jit(solution)/shard_map/all_to_all | solution.py:350
  41.0 2.8 %collective-permute-start.2 = (bf16[48,1024]{1,0:T(8,128)(2,1)S(1)}, bf16[48,1024]{1,0:T(8,128)(2,1)S(1)}, u32[]{:S(2)}, u32[]{:S(2)}) collective-permute-start(bf16[48,1024]{1,0:T(8,128)(2,1)S(1)} %get-tuple-element.46), channel_id=1, source_target_pairs={{0,12},{1,13},{2,14},{3,15},{4,0},{5,1},{6,2},{7,3},{8,4},{9,5},{1... | collective-permute-start | bytes 294920 | tf_op jit(solution)/shard_map/ppermute | solution.py:310
  45.5 3.5 %collective-permute-done.2 = bf16[48,1024]{1,0:T(8,128)(2,1)S(1)} collective-permute-done((bf16[48,1024]{1,0:T(8,128)(2,1)S(1)}, bf16[48,1024]{1,0:T(8,128)(2,1)S(1)}, u32[]{:S(2)}, u32[]{:S(2)}) %collective-permute-start.2) | collective-permute-done | bytes 98336 | tf_op jit(solution)/shard_map/ppermute | solution.py:310
  53.3 3.0 %collective-permute-start.8 = (bf16[48,1024]{1,0:T(8,128)(2,1)S(1)}, bf16[48,1024]{1,0:T(8,128)(2,1)S(1)}, u32[]{:S(2)}, u32[]{:S(2)}) collective-permute-start(bf16[48,1024]{1,0:T(8,128)(2,1)S(1)} %get-tuple-element.45), channel_id=1, source_target_pairs={{0,3},{1,0},{2,1},{3,2},{4,7},{5,4},{6,5},{7,6},{8,11},{9,8},{10,9... | collective-permute-start | bytes 294920 | tf_op jit(solution)/shard_map/ppermute | solution.py:315
  59.8 6.2 %collective-permute-done.8 = bf16[48,1024]{1,0:T(8,128)(2,1)S(1)} collective-permute-done((bf16[48,1024]{1,0:T(8,128)(2,1)S(1)}, bf16[48,1024]{1,0:T(8,128)(2,1)S(1)}, u32[]{:S(2)}, u32[]{:S(2)}) %collective-permute-start.8) | collective-permute-done | bytes 98336 | tf_op jit(solution)/shard_map/ppermute | solution.py:315
  72.4 5.2 %collective-permute-done.4.refs_2_ = bf16[192,1024]{1,0:T(8,128)(2,1)S(1)} collective-permute-done((bf16[192,1024]{1,0:T(8,128)(2,1)S(1)}, bf16[192,1024]{1,0:T(8,128)(2,1)S(1)}, u32[]{:S(2)}, u32[]{:S(2)}) %collective-permute-start.4) | collective-permute-done | bytes 393248 | tf_op jit(solution)/shard_map/ppermute | solution.py:315
  77.5 8.4 %collective-permute-done.3.refs_1_ = bf16[192,1024]{1,0:T(8,128)(2,1)} collective-permute-done((bf16[192,1024]{1,0:T(8,128)(2,1)S(1)}, bf16[192,1024]{1,0:T(8,128)(2,1)}, u32[]{:S(2)}, u32[]{:S(2)}) %collective-permute-start.3) | collective-permute-done | bytes 393248 | tf_op jit(solution)/shard_map/ppermute | solution.py:315
  86.0 3.6 %collective-permute-done.9.refs_5_ = bf16[192,1024]{1,0:T(8,128)(2,1)} collective-permute-done((bf16[192,1024]{1,0:T(8,128)(2,1)S(1)}, bf16[192,1024]{1,0:T(8,128)(2,1)}, u32[]{:S(2)}, u32[]{:S(2)}) %collective-permute-start.9) | collective-permute-done | bytes 393248 | tf_op jit(solution)/shard_map/ppermute | solution.py:310
  89.6 4.2 %attention_grads.1 = bf16[16,144,128]{2,1,0:T(8,128)(2,1)} custom-call(s32[16]{0:T(128)S(1)} %get-tuple-element.36.start_ref, s32[16]{0:T(128)S(1)} %get-tuple-element.35.count_ref, s32[1]{0:T(128)} %bitcast.head_ref, bf16[128,2048]{1,0:T(8,128)(2,1)S(1)} %copy-done, bf16[192,1024]{1,0:T(8,128)(2,1)S(1)} %pad_maximum_fusion.refs_0_, ...), custom_call_target="tpu_custom_call" | custom-call | tf_op jit(solution)/shard_map/attention_grads/pallas_call | solution.py:131
  93.7 5.7 %all-to-all-start.2 = ((bf16[16,144,128]{2,1,0:T(8,128)(2,1)}), bf16[16,144,128]{2,1,0:T(8,128)(2,1)S(1)}, u32[]{:S(2)}, u32[]{:S(2)}) async-start(bf16[16,144,128]{2,1,0:T(8,128)(2,1)} %attention_grads.1), calls=%async_computation.2 | async-start | bytes 1179648 | tf_op jit(solution)/shard_map/all_to_all | solution.py:350
  100.4 5.0 %mixed_parts.1 = (bf16[192,1024]{1,0:T(8,128)(2,1)}, bf16[192,1024]{1,0:T(8,128)(2,1)}, bf16[192,1024]{1,0:T(8,128)(2,1)}, bf16[192,1024]{1,0:T(8,128)(2,1)}, bf...) custom-call(s32[16]{0:T(128)S(1)} %get-tuple-element.36.start_ref, ...), custom_call_target="tpu_custom_call" | custom-call | tf_op jit(solution)/shard_map/mixed_parts/pallas_call | solution.py:291
  111.4 5.1 %all-to-all-done.2.g_ref = bf16[16,144,128]{2,1,0:T(8,128)(2,1)S(1)} async-done(((bf16[16,144,128]{2,1,0:T(8,128)(2,1)}), bf16[16,144,128]{2,1,0:T(8,128)(2,1)S(1)}, u32[]{:S(2)}, u32[]{:S(2)}) %all-to-all-start.2) | async-done | bytes 589856 | tf_op jit(solution)/shard_map/all_to_all | solution.py:350
  118.0 5.5 %backward.1 = (bf16[16,144,128]{2,1,0:T(8,128)(2,1)}, bf16[2048,128]{1,0:T(8,128)(2,1)}, bf16[2048,128]{1,0:T(8,128)(2,1)}) custom-call(s32[8]{0:T(128)S(1)} %and_select_fusion.source_ref, s32[8]{0:T(128)S(1)} %get-tuple-element.38.start_ref, s32[8]{0:T(128)S(1)} %get-tuple-element.37.count_ref, bf16[16,144,128]{2,1,0:T(8,128)(2,1)S(1)} %all-to-all-done.q_ref, ...), custom_call_target="tpu_custom_call" | custom-call | tf_op jit(solution)/shard_map/backward/pallas_call | solution.py:232
  123.5 5.1 %all-to-all-start.3 = ((bf16[16,144,128]{2,1,0:T(8,128)(2,1)}), bf16[16,144,128]{2,1,0:T(8,128)(2,1)S(1)}, u32[]{:S(2)}, u32[]{:S(2)}) async-start(bf16[16,144,128]{2,1,0:T(8,128)(2,1)} %get-tuple-element.30), calls=%async_computation.3 | async-start | bytes 1179648 | tf_op jit(solution)/shard_map/all_to_all | solution.py:350
  128.6 6.1 %collective-permute-start.12 = (bf16[192,1024]{1,0:T(8,128)(2,1)}, bf16[192,1024]{1,0:T(8,128)(2,1)S(1)}, u32[]{:S(2)}, u32[]{:S(2)}) collective-permute-start(bf16[192,1024]{1,0:T(8,128)(2,1)} %get-tuple-element.22), channel_id=1, source_target_pairs={{0,3},{1,0},{2,1},{3,2},{4,7},{5,4},{6,5},{7,6},{8,11},{9,8},{10,9... | collective-permute-start | bytes 1179656 | tf_op jit(solution)/shard_map/ppermute | solution.py:315
  134.7 6.9 %collective-permute-start.13 = (bf16[192,1024]{1,0:T(8,128)(2,1)}, bf16[192,1024]{1,0:T(8,128)(2,1)S(1)}, u32[]{:S(2)}, u32[]{:S(2)}) collective-permute-start(bf16[192,1024]{1,0:T(8,128)(2,1)} %get-tuple-element.23), channel_id=1, source_target_pairs={{0,2},{1,3},{2,0},{3,1},{4,6},{5,7},{6,4},{7,5},{8,10},{9,11},{10,... | collective-permute-start | bytes 1179656 | tf_op jit(solution)/shard_map/ppermute | solution.py:315
  143.8 6.4 %collective-permute-done.12 = bf16[192,1024]{1,0:T(8,128)(2,1)S(1)} collective-permute-done((bf16[192,1024]{1,0:T(8,128)(2,1)}, bf16[192,1024]{1,0:T(8,128)(2,1)S(1)}, u32[]{:S(2)}, u32[]{:S(2)}) %collective-permute-start.12) | collective-permute-done | bytes 393248 | tf_op jit(solution)/shard_map/ppermute | solution.py:315
  150.2 9.6 %collective-permute-done.13 = bf16[192,1024]{1,0:T(8,128)(2,1)S(1)} collective-permute-done((bf16[192,1024]{1,0:T(8,128)(2,1)}, bf16[192,1024]{1,0:T(8,128)(2,1)S(1)}, u32[]{:S(2)}, u32[]{:S(2)}) %collective-permute-start.13) | collective-permute-done | bytes 393248 | tf_op jit(solution)/shard_map/ppermute | solution.py:315
  165.5 7.7 %collective-permute-start.21 = (bf16[48,1024]{1,0:T(8,128)(2,1)S(1)}, bf16[48,1024]{1,0:T(8,128)(2,1)S(1)}, u32[]{:S(2)}, u32[]{:S(2)}) collective-permute-start(bf16[48,1024]{1,0:T(8,128)(2,1)S(1)} %get-tuple-element.42), channel_id=1, source_target_pairs={{0,3},{1,0},{2,1},{3,2},{4,7},{5,4},{6,5},{7,6},{8,11},{9,8},{10,9... | collective-permute-start | bytes 294920 | tf_op jit(solution)/shard_map/ppermute | solution.py:315
  173.3 5.7 %collective-permute-start.22 = (bf16[48,1024]{1,0:T(8,128)(2,1)S(1)}, bf16[48,1024]{1,0:T(8,128)(2,1)S(1)}, u32[]{:S(2)}, u32[]{:S(2)}) collective-permute-start(bf16[48,1024]{1,0:T(8,128)(2,1)S(1)} %get-tuple-element.44), channel_id=1, source_target_pairs={{0,2},{1,3},{2,0},{3,1},{4,6},{5,7},{6,4},{7,5},{8,10},{9,11},{10,... | collective-permute-start | bytes 294920 | tf_op jit(solution)/shard_map/ppermute | solution.py:315
  179.0 5.0 %collective-permute-start.27 = (bf16[1,128,128]{2,1,0:T(8,128)(2,1)S(1)}, bf16[1,128,128]{2,1,0:T(8,128)(2,1)S(1)}, u32[]{:S(2)}, u32[]{:S(2)}) collective-permute-start(bf16[1,128,128]{2,1,0:T(8,128)(2,1)S(1)} %fusion.6), channel_id=1, source_target_pairs={{0,128},{16,144},{32,160},{48,176},{64,192},{80,208},{96,224},{112... | collective-permute-start | bytes 98312 | tf_op jit(solution)/shard_map/ppermute | solution.py:321
  (103 shorter events, 40.7 us)
Async XLA Ops:
  5.0 25.8 %all-to-all-start = ((bf16[16,144,128]{2,1,0:T(8,128)(2,1)}), bf16[16,144,128]{2,1,0:T(8,128)(2,1)S(1)}, u32[]{:S(2)}, u32[]{:S(2)}) async-start(bf16[16,144,128]{2,1,0:T(8,128)(2,1)} %pack_queries.1), calls=%async_computation | async-start | bytes 1179648 | tf_op jit(solution)/shard_map/all_to_all | solution.py:350
  36.4 57.4 %all-to-all-start.1 = ((bf16[16,144,128]{2,1,0:T(8,128)(2,1)}), bf16[16,144,128]{2,1,0:T(8,128)(2,1)S(1)}, u32[]{:S(2)}, u32[]{:S(2)}) async-start(bf16[16,144,128]{2,1,0:T(8,128)(2,1)} %get-tuple-element.20.att_ref), calls=%async_computation.1 | async-start | bytes 1179648 | tf_op jit(solution)/shard_map/all_to_all | solution.py:350
  52.7 18.8 %collective-permute-start.5 = (bf16[192,1024]{1,0:T(8,128)(2,1)S(1)}, bf16[192,1024]{1,0:T(8,128)(2,1)S(1)}, u32[]{:S(2)}, u32[]{:S(2)}) collective-permute-start(bf16[192,1024]{1,0:T(8,128)(2,1)S(1)} %pad_maximum_fusion.refs_0_), channel_id=1, source_target_pairs={{0,3},{1,0},{2,1},{3,2},{4,7},{5,4},{6,5},{7,6},{8,11},{9,8},{10,9... | collective-permute-start | bytes 1179656 | tf_op jit(solution)/shard_map/ppermute | solution.py:315
  53.3 12.7 %collective-permute-start.8 = (bf16[48,1024]{1,0:T(8,128)(2,1)S(1)}, bf16[48,1024]{1,0:T(8,128)(2,1)S(1)}, u32[]{:S(2)}, u32[]{:S(2)}) collective-permute-start(bf16[48,1024]{1,0:T(8,128)(2,1)S(1)} %get-tuple-element.45), channel_id=1, source_target_pairs={{0,3},{1,0},{2,1},{3,2},{4,7},{5,4},{6,5},{7,6},{8,11},{9,8},{10,9... | collective-permute-start | bytes 294920 | tf_op jit(solution)/shard_map/ppermute | solution.py:315
  56.3 13.7 %collective-permute-start.7 = (bf16[48,1024]{1,0:T(8,128)(2,1)S(1)}, bf16[48,1024]{1,0:T(8,128)(2,1)S(1)}, u32[]{:S(2)}, u32[]{:S(2)}) collective-permute-start(bf16[48,1024]{1,0:T(8,128)(2,1)S(1)} %get-tuple-element.45), channel_id=1, source_target_pairs={{0,2},{1,3},{2,0},{3,1},{4,6},{5,7},{6,4},{7,5},{8,10},{9,11},{10,... | collective-permute-start | bytes 294920 | tf_op jit(solution)/shard_map/ppermute | solution.py:315
  56.3 13.7 %collective-permute-start.6 = (bf16[48,1024]{1,0:T(8,128)(2,1)S(1)}, bf16[48,1024]{1,0:T(8,128)(2,1)S(1)}, u32[]{:S(2)}, u32[]{:S(2)}) collective-permute-start(bf16[48,1024]{1,0:T(8,128)(2,1)S(1)} %get-tuple-element.45), channel_id=1, source_target_pairs={{0,1},{1,2},{2,3},{3,0},{4,5},{5,6},{6,7},{7,4},{8,9},{9,10},{10,1... | collective-permute-start | bytes 294920 | tf_op jit(solution)/shard_map/ppermute | solution.py:315
  58.5 19.1 %collective-permute-start.4 = (bf16[192,1024]{1,0:T(8,128)(2,1)S(1)}, bf16[192,1024]{1,0:T(8,128)(2,1)S(1)}, u32[]{:S(2)}, u32[]{:S(2)}) collective-permute-start(bf16[192,1024]{1,0:T(8,128)(2,1)S(1)} %pad_maximum_fusion.refs_0_), channel_id=1, source_target_pairs={{0,2},{1,3},{2,0},{3,1},{4,6},{5,7},{6,4},{7,5},{8,10},{9,11},{10,... | collective-permute-start | bytes 1179656 | tf_op jit(solution)/shard_map/ppermute | solution.py:315
  66.0 19.9 %collective-permute-start.3 = (bf16[192,1024]{1,0:T(8,128)(2,1)S(1)}, bf16[192,1024]{1,0:T(8,128)(2,1)}, u32[]{:S(2)}, u32[]{:S(2)}) collective-permute-start(bf16[192,1024]{1,0:T(8,128)(2,1)S(1)} %pad_maximum_fusion.refs_0_), channel_id=1, source_target_pairs={{0,1},{1,2},{2,3},{3,0},{4,5},{5,6},{6,7},{7,4},{8,9},{9,10},{10,1... | collective-permute-start | bytes 1179656 | tf_op jit(solution)/shard_map/ppermute | solution.py:315
  70.1 15.9 %collective-permute-start.11 = (bf16[192,1024]{1,0:T(8,128)(2,1)S(1)}, bf16[192,1024]{1,0:T(8,128)(2,1)}, u32[]{:S(2)}, u32[]{:S(2)}) collective-permute-start(bf16[192,1024]{1,0:T(8,128)(2,1)S(1)} %pad_maximum_fusion.1.refs_4_), channel_id=1, source_target_pairs={{0,12},{1,13},{2,14},{3,15},{4,0},{5,1},{6,2},{7,3},{8,4},{9,5},{1... | collective-permute-start | bytes 1179656 | tf_op jit(solution)/shard_map/ppermute | solution.py:310
  70.7 15.2 %collective-permute-start.10 = (bf16[192,1024]{1,0:T(8,128)(2,1)S(1)}, bf16[192,1024]{1,0:T(8,128)(2,1)}, u32[]{:S(2)}, u32[]{:S(2)}) collective-permute-start(bf16[192,1024]{1,0:T(8,128)(2,1)S(1)} %pad_maximum_fusion.1.refs_4_), channel_id=1, source_target_pairs={{0,8},{1,9},{2,10},{3,11},{4,12},{5,13},{6,14},{7,15},{8,0},{9,1},... | collective-permute-start | bytes 1179656 | tf_op jit(solution)/shard_map/ppermute | solution.py:310
  71.5 18.1 %collective-permute-start.9 = (bf16[192,1024]{1,0:T(8,128)(2,1)S(1)}, bf16[192,1024]{1,0:T(8,128)(2,1)}, u32[]{:S(2)}, u32[]{:S(2)}) collective-permute-start(bf16[192,1024]{1,0:T(8,128)(2,1)S(1)} %pad_maximum_fusion.1.refs_4_), channel_id=1, source_target_pairs={{0,4},{1,5},{2,6},{3,7},{4,8},{5,9},{6,10},{7,11},{8,12},{9,13},{1... | collective-permute-start | bytes 1179656 | tf_op jit(solution)/shard_map/ppermute | solution.py:310
  93.7 22.8 %all-to-all-start.2 = ((bf16[16,144,128]{2,1,0:T(8,128)(2,1)}), bf16[16,144,128]{2,1,0:T(8,128)(2,1)S(1)}, u32[]{:S(2)}, u32[]{:S(2)}) async-start(bf16[16,144,128]{2,1,0:T(8,128)(2,1)} %attention_grads.1), calls=%async_computation.2 | async-start | bytes 1179648 | tf_op jit(solution)/shard_map/all_to_all | solution.py:350
  109.5 34.2 %collective-permute-start.25 = (bf16[4,128,128]{2,1,0:T(8,128)(2,1)S(1)}, bf16[4,128,128]{2,1,0:T(8,128)(2,1)S(1)}, u32[]{:S(2)}, u32[]{:S(2)}) collective-permute-start(bf16[4,128,128]{2,1,0:T(8,128)(2,1)S(1)} %fusion), channel_id=1, source_target_pairs={{0,32},{16,48},{32,0},{48,16},{64,96},{80,112},{96,64},{112,80},{1... | collective-permute-start | bytes 393224 | tf_op jit(solution)/shard_map/ppermute | solution.py:321
  123.5 61.4 %all-to-all-start.3 = ((bf16[16,144,128]{2,1,0:T(8,128)(2,1)}), bf16[16,144,128]{2,1,0:T(8,128)(2,1)S(1)}, u32[]{:S(2)}, u32[]{:S(2)}) async-start(bf16[16,144,128]{2,1,0:T(8,128)(2,1)} %get-tuple-element.30), calls=%async_computation.3 | async-start | bytes 1179648 | tf_op jit(solution)/shard_map/all_to_all | solution.py:350
  128.6 21.6 %collective-permute-start.12 = (bf16[192,1024]{1,0:T(8,128)(2,1)}, bf16[192,1024]{1,0:T(8,128)(2,1)S(1)}, u32[]{:S(2)}, u32[]{:S(2)}) collective-permute-start(bf16[192,1024]{1,0:T(8,128)(2,1)} %get-tuple-element.22), channel_id=1, source_target_pairs={{0,3},{1,0},{2,1},{3,2},{4,7},{5,4},{6,5},{7,6},{8,11},{9,8},{10,9... | collective-permute-start | bytes 1179656 | tf_op jit(solution)/shard_map/ppermute | solution.py:315
  134.7 25.1 %collective-permute-start.13 = (bf16[192,1024]{1,0:T(8,128)(2,1)}, bf16[192,1024]{1,0:T(8,128)(2,1)S(1)}, u32[]{:S(2)}, u32[]{:S(2)}) collective-permute-start(bf16[192,1024]{1,0:T(8,128)(2,1)} %get-tuple-element.23), channel_id=1, source_target_pairs={{0,2},{1,3},{2,0},{3,1},{4,6},{5,7},{6,4},{7,5},{8,10},{9,11},{10,... | collective-permute-start | bytes 1179656 | tf_op jit(solution)/shard_map/ppermute | solution.py:315
  141.7 20.5 %collective-permute-start.14 = (bf16[192,1024]{1,0:T(8,128)(2,1)}, bf16[192,1024]{1,0:T(8,128)(2,1)S(1)}, u32[]{:S(2)}, u32[]{:S(2)}) collective-permute-start(bf16[192,1024]{1,0:T(8,128)(2,1)} %get-tuple-element.24), channel_id=1, source_target_pairs={{0,1},{1,2},{2,3},{3,0},{4,5},{5,6},{6,7},{7,4},{8,9},{9,10},{10,1... | collective-permute-start | bytes 1179656 | tf_op jit(solution)/shard_map/ppermute | solution.py:315
  142.6 21.1 %collective-permute-start.18 = (bf16[192,1024]{1,0:T(8,128)(2,1)}, bf16[192,1024]{1,0:T(8,128)(2,1)S(1)}, u32[]{:S(2)}, u32[]{:S(2)}) collective-permute-start(bf16[192,1024]{1,0:T(8,128)(2,1)} %get-tuple-element.26), channel_id=1, source_target_pairs={{0,12},{1,13},{2,14},{3,15},{4,0},{5,1},{6,2},{7,3},{8,4},{9,5},{1... | collective-permute-start | bytes 1179656 | tf_op jit(solution)/shard_map/ppermute | solution.py:310
  143.6 20.9 %collective-permute-start.19 = (bf16[192,1024]{1,0:T(8,128)(2,1)S(1)}, bf16[192,1024]{1,0:T(8,128)(2,1)S(1)}, u32[]{:S(2)}, u32[]{:S(2)}) collective-permute-start(bf16[192,1024]{1,0:T(8,128)(2,1)S(1)} %copy-done.14), channel_id=1, source_target_pairs={{0,8},{1,9},{2,10},{3,11},{4,12},{5,13},{6,14},{7,15},{8,0},{9,1},... | collective-permute-start | bytes 1179656 | tf_op jit(solution)/shard_map/ppermute | solution.py:310
  150.2 14.9 %collective-permute-start.20 = (bf16[192,1024]{1,0:T(8,128)(2,1)S(1)}, bf16[192,1024]{1,0:T(8,128)(2,1)S(1)}, u32[]{:S(2)}, u32[]{:S(2)}) collective-permute-start(bf16[192,1024]{1,0:T(8,128)(2,1)S(1)} %copy-done.13), channel_id=1, source_target_pairs={{0,4},{1,5},{2,6},{3,7},{4,8},{5,9},{6,10},{7,11},{8,12},{9,13},{1... | collective-permute-start | bytes 1179656 | tf_op jit(solution)/shard_map/ppermute | solution.py:310
  159.8 13.4 %collective-permute-start.26 = (bf16[2,128,128]{2,1,0:T(8,128)(2,1)S(1)}, bf16[2,128,128]{2,1,0:T(8,128)(2,1)S(1)}, u32[]{:S(2)}, u32[]{:S(2)}) collective-permute-start(bf16[2,128,128]{2,1,0:T(8,128)(2,1)S(1)} %fusion.4), channel_id=1, source_target_pairs={{0,64},{16,80},{32,96},{48,112},{64,0},{80,16},{96,32},{112,48},{1... | collective-permute-start | bytes 196616 | tf_op jit(solution)/shard_map/ppermute | solution.py:321
  163.6 15.4 %collective-permute-start.17 = (bf16[48,1024]{1,0:T(8,128)(2,1)S(1)}, bf16[48,1024]{1,0:T(8,128)(2,1)S(1)}, u32[]{:S(2)}, u32[]{:S(2)}) collective-permute-start(bf16[48,1024]{1,0:T(8,128)(2,1)S(1)} %get-tuple-element.40), channel_id=1, source_target_pairs={{0,4},{1,5},{2,6},{3,7},{4,8},{5,9},{6,10},{7,11},{8,12},{9,13},{1... | collective-permute-start | bytes 294920 | tf_op jit(solution)/shard_map/ppermute | solution.py:310
  164.6 19.5 %collective-permute-start.16 = (bf16[48,1024]{1,0:T(8,128)(2,1)S(1)}, bf16[48,1024]{1,0:T(8,128)(2,1)S(1)}, u32[]{:S(2)}, u32[]{:S(2)}) collective-permute-start(bf16[48,1024]{1,0:T(8,128)(2,1)S(1)} %get-tuple-element.41), channel_id=1, source_target_pairs={{0,8},{1,9},{2,10},{3,11},{4,12},{5,13},{6,14},{7,15},{8,0},{9,1},... | collective-permute-start | bytes 294920 | tf_op jit(solution)/shard_map/ppermute | solution.py:310
  165.5 18.6 %collective-permute-start.21 = (bf16[48,1024]{1,0:T(8,128)(2,1)S(1)}, bf16[48,1024]{1,0:T(8,128)(2,1)S(1)}, u32[]{:S(2)}, u32[]{:S(2)}) collective-permute-start(bf16[48,1024]{1,0:T(8,128)(2,1)S(1)} %get-tuple-element.42), channel_id=1, source_target_pairs={{0,3},{1,0},{2,1},{3,2},{4,7},{5,4},{6,5},{7,6},{8,11},{9,8},{10,9... | collective-permute-start | bytes 294920 | tf_op jit(solution)/shard_map/ppermute | solution.py:315
  (24 other events, 392.1 us)

commit v4 on v3

--- a/solution.py
+++ b/solution.py
@@ -158,7 +158,7 @@
     return source_ref[doc], base, start - base, count_ref[doc]
 
 
-def forward_kernel(source_ref, start_ref, count_ref, q_ref, k_ref, v_ref, att_ref, w_ref, kept_ref, sems):
+def forward_kernel(source_ref, start_ref, count_ref, q_ref, k_ref, v_ref, att_ref, out_ref, w_ref, sems):
     att_ref[...] = jnp.zeros(att_ref.shape, att_ref.dtype)
     refs = (source_ref, start_ref, count_ref)
     lane = lax.broadcasted_iota(jnp.int32, (1, CAP * BLOCK), 1)
@@ -167,68 +167,78 @@
         source, base, skip, count = document(refs, doc, k_ref.shape[0] // BLOCK)
         tokens = pl.ds(pl.multiple_of(base * BLOCK, BLOCK), CAP * BLOCK)
         admitted = (lane >= skip * BLOCK) & (lane < (skip + count) * BLOCK)
-        queries = two_heads(q_ref[source])
-        scores = dot(queries, k_ref[tokens, :], ((1,), (1,))) * SCALE
+        queries = two_heads(q_ref[source] * SCALE)
+        scores = dot(queries, k_ref[tokens, :], ((1,), (1,)))
         scores = jnp.where(admitted, scores, MASKED)
         top = jnp.max(scores, axis=1, keepdims=True)
         terms = jnp.exp(scores - top)
         scale = 1.0 / jnp.sum(terms, axis=1, keepdims=True)
         weights = (terms * scale).astype(jnp.bfloat16)
-        kept_ref[doc] = weights
-        copies.append(pltpu.make_async_copy(kept_ref.at[doc], w_ref.at[doc], sems.at[doc]))
+        for part in range(CAP):
+            mine = weights[:, part * BLOCK : (part + 1) * BLOCK]
+            if part < CAP - 1:
+                mine = jnp.where(skip > part, w_ref[base + part], mine)
+            w_ref[base + part] = mine
+        copies.append(pltpu.make_async_copy(w_ref.at[doc], out_ref.at[doc], sems.at[doc]))
         copies[-1].start()
         mixed = dot(weights, v_ref[tokens, :], ((1,), (0,)))
         att_ref[source] = one_row(mixed).astype(jnp.bfloat16)
+    rest = slice(DPS, w_ref.shape[0])
+    copies.append(pltpu.make_async_copy(w_ref.at[rest], out_ref.at[rest], sems.at[DPS]))
+    copies[-1].start()
     for copy in copies:
         copy.wait()
 
 
 def forward(source, start, count, got_q, keys, values):
-    weights = (DPS, 2 * SLOT, CAP * BLOCK)
+    weights = (keys.shape[0] // BLOCK, 2 * SLOT, BLOCK)
     return pl.pallas_call(
         forward_kernel,
-        out_shape=(jax.ShapeDtypeStruct(got_q.shape, jnp.bfloat16), HBM(weights, jnp.bfloat16)),
+        out_shape=(
+            jax.ShapeDtypeStruct(got_q.shape, jnp.bfloat16),
+            HBM(weights, jnp.bfloat16),
+        ),
         in_specs=smem_specs(3) + vmem_specs(3),
         out_specs=(*vmem_specs(1), pl.BlockSpec(memory_space=HBM)),
-        scratch_shapes=[pltpu.VMEM(weights, jnp.bfloat16), pltpu.SemaphoreType.DMA((DPS,))],
+        scratch_shapes=[pltpu.VMEM(weights, jnp.bfloat16), pltpu.SemaphoreType.DMA((DPS + 1,))],
         compiler_params=LIMIT,
         name="forward",
     )(source, start, count, got_q, keys, values)
 
 
 def backward_kernel(
-    source_ref, start_ref, count_ref, q_ref, g_ref, att_ref, w_ref, k_ref, v_ref, dq_ref, dk_ref, dv_ref
+    source_ref, owner_ref, q_ref, g_ref, att_ref, kept_ref, k_ref, v_ref,
+    dq_ref, dk_ref, dv_ref, w_ref, sem, queries_ref, grads_ref, delta_ref, sum_ref
 ):
+    fetch = pltpu.make_async_copy(kept_ref, w_ref, sem)
+    fetch.start()
     dq_ref[...] = jnp.zeros(dq_ref.shape, dq_ref.dtype)
-    refs = (source_ref, start_ref, count_ref)
     for doc in range(DPS):
-        source, base, skip, _ = document(refs, doc, k_ref.shape[0] // BLOCK)
-        tokens = pl.ds(pl.multiple_of(base * BLOCK, BLOCK), CAP * BLOCK)
-        queries = two_heads(q_ref[source])
+        source = source_ref[doc]
+        queries_ref[doc] = two_heads(q_ref[source])
         grads = two_heads(g_ref[source])
+        grads_ref[doc] = grads
         attended = att_ref[source].astype(jnp.float32)
         both = jnp.concatenate([attended, attended], axis=0)
-        delta = jnp.sum(grads.astype(jnp.float32) * both, axis=1, keepdims=True)
-        weights = w_ref[doc]
+        delta_ref[doc] = jnp.sum(grads.astype(jnp.float32) * both, axis=1, keepdims=True)
+        sum_ref[doc] = jnp.zeros(sum_ref.shape[1:], sum_ref.dtype)
+    fetch.wait()
+    for block in range(w_ref.shape[0]):
+        doc = owner_ref[block]
+        tokens = slice(block * BLOCK, (block + 1) * BLOCK)
+        grads = grads_ref[doc]
+        weights = w_ref[block]
         dprobs = dot(grads, v_ref[tokens, :], ((1,), (1,)))
-        dscores = (weights.astype(jnp.float32) * (dprobs - delta)).astype(jnp.bfloat16)
-        dq = dot(dscores, k_ref[tokens, :], ((1,), (0,)))
-        dq_ref[source] = (one_row(dq) * SCALE).astype(jnp.bfloat16)
-        dk = (dot(dscores, queries, ((0,), (0,))) * SCALE).astype(jnp.bfloat16)
-        dv = dot(weights, grads, ((0,), (0,))).astype(jnp.bfloat16)
-        for part in range(CAP):
-            rows = pl.ds(pl.multiple_of((base + part) * BLOCK, BLOCK), BLOCK)
-            span = slice(part * BLOCK, (part + 1) * BLOCK)
-            if part == CAP - 1:
-                dk_ref[rows, :] = dk[span]
-                dv_ref[rows, :] = dv[span]
-            else:
-                keep = skip > part
-                dk_ref[rows, :] = jnp.where(keep, dk_ref[rows, :], dk[span])
-                dv_ref[rows, :] = jnp.where(keep, dv_ref[rows, :], dv[span])
-
-
-def backward(source, start, count, got_q, got_g, attended, weights, keys, values):
+        dscores = (weights.astype(jnp.float32) * (dprobs - delta_ref[doc])).astype(jnp.bfloat16)
+        sum_ref[doc] += dot(dscores, k_ref[tokens, :], ((1,), (0,)))
+        dk_ref[tokens, :] = (dot(dscores, queries_ref[doc], ((0,), (0,))) * SCALE).astype(jnp.bfloat16)
+        dv_ref[tokens, :] = dot(weights, grads, ((0,), (0,))).astype(jnp.bfloat16)
+    for doc in range(DPS):
+        dq_ref[source_ref[doc]] = (one_row(sum_ref[doc]) * SCALE).astype(jnp.bfloat16)
+
+
+def backward(source, owner, got_q, got_g, attended, weights, keys, values):
+    stacked = (DPS, 2 * SLOT, got_q.shape[2])
     return pl.pallas_call(
         backward_kernel,
         out_shape=(
@@ -236,17 +246,25 @@
             jax.ShapeDtypeStruct(keys.shape, jnp.bfloat16),
             jax.ShapeDtypeStruct(values.shape, jnp.bfloat16),
         ),
-        in_specs=smem_specs(3) + vmem_specs(6),
+        in_specs=smem_specs(2) + vmem_specs(3) + [pl.BlockSpec(memory_space=HBM)] + vmem_specs(2),
         out_specs=tuple(vmem_specs(3)),
+        scratch_shapes=[
+            pltpu.VMEM(weights.shape, jnp.bfloat16),
+            pltpu.SemaphoreType.DMA,
+            pltpu.VMEM(stacked, jnp.bfloat16),
+            pltpu.VMEM(stacked, jnp.bfloat16),
+            pltpu.VMEM((DPS, 2 * SLOT, 1), jnp.float32),
+            pltpu.VMEM(stacked, jnp.float32),
+        ],
         compiler_params=LIMIT,
         name="backward",
-    )(source, start, count, got_q, got_g, attended, weights, keys, values)
-
-
-def mixed_kernel(start_ref, count_ref, head_ref, packed_ref, proj_ref, *refs):
+    )(source, owner, got_q, got_g, attended, weights, keys, values)
+
+
+def mixed_kernel(start_ref, count_ref, head_ref, core_ref, packed_ref, proj_ref, *refs):
     first, second = refs[:SIDE], refs[SIDE : 2 * SIDE]
     outs = refs[2 * SIDE : 4 * SIDE]
-    even_ref, odd_ref, sum_ref, sent_ref, weight_ref, sems = refs[4 * SIDE :]
+    mine_ref, theirs_ref, sum_ref, sent_ref, weight_ref, other_ref, sems = refs[4 * SIDE :]
     unpack_rows(start_ref, count_ref, packed_ref, sum_ref)
     unit = sum_ref.shape[0] // (SIDE * SIDE)
     half = proj_ref.shape[1] // 2
@@ -276,32 +294,36 @@
         for c in range(per_half):
             chunk = h * per_half + c
             weight_ref[chunk % 2, chunk // 2] = sums[h][:, c * BLOCK : (c + 1) * BLOCK]
-    for c, out_ref in enumerate((even_ref, odd_ref)):
-        copies.append(pltpu.make_async_copy(weight_ref.at[c], out_ref, sems.at[2 * SIDE + c]))
-        copies[-1].start()
+    core = core_ref[0]
+    other_ref[...] = weight_ref[1 - core].astype(jnp.bfloat16)
+    copies.append(pltpu.make_async_copy(other_ref, theirs_ref, sems.at[2 * SIDE]))
+    copies[-1].start()
+    copies.append(pltpu.make_async_copy(weight_ref.at[core], mine_ref, sems.at[2 * SIDE + 1]))
+    copies[-1].start()
     for copy in copies:
         copy.wait()
 
 
-def mixed_parts(start, count, head, packed, out_proj, first, second):
+def mixed_parts(start, count, head, core, packed, out_proj, first, second):
     inner, width = out_proj.shape
     row_count = SIDE * first[0].shape[0]
     part = HBM(first[0].shape, jnp.bfloat16)
-    sums = HBM((width // BLOCK // 2, inner, BLOCK), jnp.float32)
+    chunks = (width // BLOCK // 2, inner, BLOCK)
     outs = pl.pallas_call(
         mixed_kernel,
-        out_shape=(part,) * (2 * SIDE) + (sums,) * 2,
-        in_specs=smem_specs(3) + vmem_specs(2 + 2 * SIDE),
+        out_shape=(part,) * (2 * SIDE) + (HBM(chunks, jnp.float32), HBM(chunks, jnp.bfloat16)),
+        in_specs=smem_specs(4) + vmem_specs(2 + 2 * SIDE),
         out_specs=tuple([pl.BlockSpec(memory_space=HBM)] * (2 * SIDE + 2)),
         scratch_shapes=[
             pltpu.VMEM((row_count, inner), jnp.float32),
             pltpu.VMEM((2 * SIDE, *first[0].shape), jnp.bfloat16),
-            pltpu.VMEM((2, width // BLOCK // 2, inner, BLOCK), jnp.float32),
+            pltpu.VMEM((2, *chunks), jnp.float32),
+            pltpu.VMEM(chunks, jnp.bfloat16),
             pltpu.SemaphoreType.DMA((2 * SIDE + 2,)),
         ],
         compiler_params=LIMIT,
         name="mixed_parts",
-    )(start, count, head, packed, out_proj, *first, *second)
+    )(start, count, head, core, packed, out_proj, *first, *second)
     return outs[:SIDE], outs[SIDE : 2 * SIDE], outs[2 * SIDE], outs[2 * SIDE + 1]
 
 
@@ -315,11 +337,15 @@
     return lax.ppermute(value, "head", perm)
 
 
+def add_other(mine, theirs, distance):
+    swap = [(s, s ^ distance) for s in range(N_SEQ)]
+    other = lax.ppermute(theirs, "seq", swap)
+    return mine + other.astype(jnp.float32)
+
+
 def halve(low, high, side, distance):
-    swap = [(s, s ^ distance) for s in range(N_SEQ)]
     theirs = jnp.where(side == 0, high, low).astype(jnp.bfloat16)
-    other = lax.ppermute(theirs, "seq", swap)
-    return jnp.where(side == 0, low, high) + other.astype(jnp.float32)
+    return add_other(jnp.where(side == 0, low, high), theirs, distance)
 
 
 def shift(value, move, k):
@@ -375,26 +401,28 @@
     start = jnp.sum((blocks_here[None, :] < my_docs[:, None]).astype(jnp.int32), axis=1)
     count = jnp.sum((blocks_here[None, :] == my_docs[:, None]).astype(jnp.int32), axis=1)
 
+    owner = blocks_here - shard * DPS
+
     attended, weights = forward(source, start, count, got_q, enc_keys, enc_values)
     home = to_all(attended)
     got_g = to_all(attention_grads(row_start, row_span, head, out_proj, first, second))
 
-    m_first, m_second, even, odd = mixed_parts(row_start, row_span, head, home, out_proj, first, second)
+    core = shard % 2
+    m_first, m_second, mine, theirs = mixed_parts(row_start, row_span, head, core[None], home, out_proj, first, second)
     mixed = jnp.concatenate(
         [scatter_sum(m_first, along_y, along_x), scatter_sum(m_second, along_x, along_y)],
         axis=1,
     )
 
-    core = shard % 2
     chip = shard // 2
-    grad_wo = halve(even, odd, core, 1)
+    grad_wo = add_other(mine, theirs, 1)
     for bit in range(3):
         halves = grad_wo.reshape(-1, 2, *grad_wo.shape[1:])
         grad_wo = halve(halves[:, 0], halves[:, 1], (chip >> bit) & 1, 2 << bit)
     grad_wo = grad_wo[0]
 
     grads_q, grad_k, grad_v = backward(
-        source, start, count, got_q, got_g, attended, weights, enc_keys, enc_values
+        source, owner, got_q, got_g, attended, weights, enc_keys, enc_values
     )
     grad_q = unpack_grads(row_start, row_span, to_all(grads_q), row_count)
     return (mixed, grad_q, grad_k, grad_v, grad_wo)

time: 189 us -> 191 us (1.011)
  Pallas kernels: 24.9 us -> 27.5 us
    pallas_call x1, Pallas kernels: 5.51 us -> 7.73 us  [backward(): pl.pallas_call(backward_kernel, out_shape=(jax.ShapeDtypeStruct(got_q.sha...]
  transfers between devices with their start and end apart: 32 -> 32, of which waited for: 13 -> 13; matrix products, arithmetic and copies ran while one was open for 2% -> 2% of each run, Pallas kernels for 9% -> 10%
where the time goes in v4:
time: 191 us; the launch traced here: 190 us
  starting transfers between devices  81.1 us (42%)
  waiting for transfers between devices  72.2 us (38%)
  Pallas kernels  27.5 us (14%)
  other arithmetic  4.79 us (3%)
  local copies, waits for them, and re-layouts  3.34 us (2%)
    ppermute x12, waiting for transfers between devices, along_y(): return lax.ppermute(value, 'head', perm)  37.5 us
    ppermute x12, starting transfers between devices, along_y(): return lax.ppermute(value, 'head', perm)  37 us
    all_to_all x4, starting transfers between devices, to_all(): return lax.all_to_all(value, 'seq', split_axis=0, concat_axis=0, tiled=True)  23.8 us
    all_to_all x4, waiting for transfers between devices, to_all(): return lax.all_to_all(value, 'seq', split_axis=0, concat_axis=0, tiled=True)  22.6 us
    ppermute x12, waiting for transfers between devices, along_x(): return lax.ppermute(value, 'head', perm)  10.8 us
    ppermute x12, starting transfers between devices, along_x(): return lax.ppermute(value, 'head', perm)  10.6 us
    ppermute x4, starting transfers between devices, add_other(): other = lax.ppermute(theirs, 'seq', swap)  9.72 us
    pallas_call x1, Pallas kernels, backward(): pl.pallas_call(backward_kernel, out_shape=(jax.ShapeDtypeStruct(got_q.sha...  7.73 us
  transfers between devices with their start and end apart: 32, of which 13 were waited for; matrix products, arithmetic and copies ran while one was open for 2% of the time, Pallas kernels for 10%

profile of v4, /device:TPU:8, one launch (start us, length us, event | category | flops | bytes accessed | tf_op | source)
XLA Modules:
  0.0 189.9 jit_solution(4724957938832266946)
XLA Ops:
  5.0 8.6 %all-to-all-start = ((bf16[16,144,128]{2,1,0:T(8,128)(2,1)}), bf16[16,144,128]{2,1,0:T(8,128)(2,1)S(1)}, u32[]{:S(2)}, u32[]{:S(2)}) async-start(bf16[16,144,128]{2,1,0:T(8,128)(2,1)} %pack_queries.1), calls=%async_computation | async-start | bytes 1179648 | tf_op jit(solution)/shard_map/all_to_all | solution.py:376
  14.1 16.5 %all-to-all-done.q_ref = bf16[16,144,128]{2,1,0:T(8,128)(2,1)S(1)} async-done(((bf16[16,144,128]{2,1,0:T(8,128)(2,1)}), bf16[16,144,128]{2,1,0:T(8,128)(2,1)S(1)}, u32[]{:S(2)}, u32[]{:S(2)}) %all-to-all-start) | async-done | bytes 589856 | tf_op jit(solution)/shard_map/all_to_all | solution.py:376
  30.7 5.7 %forward.1 = (bf16[16,144,128]{2,1,0:T(8,128)(2,1)}, bf16[16,288,128]{2,1,0:T(8,128)(2,1)}) custom-call(s32[8]{0:T(128)S(1)} %and_select_fusion.source_ref, s32[8]{0:T(128)S(1)} %get-tuple-element.38.start_ref, s32[8]{0:T(128)S(1)} %get-tuple-element.37.count_ref, bf16[16,144,128]{2,1,0:T(8,128)(2,1)S(1)} %all-to-all-done.q_ref, ...), custom_call_target="tpu_custom_call" | custom-call | tf_op jit(solution)/shard_map/forward/pallas_call | solution.py:195
  36.4 4.5 %all-to-all-start.1 = ((bf16[16,144,128]{2,1,0:T(8,128)(2,1)}), bf16[16,144,128]{2,1,0:T(8,128)(2,1)S(1)}, u32[]{:S(2)}, u32[]{:S(2)}) async-start(bf16[16,144,128]{2,1,0:T(8,128)(2,1)} %get-tuple-element.20.att_ref), calls=%async_computation.1 | async-start | bytes 1179648 | tf_op jit(solution)/shard_map/all_to_all | solution.py:376
  40.9 2.8 %collective-permute-start.2 = (bf16[48,1024]{1,0:T(8,128)(2,1)S(1)}, bf16[48,1024]{1,0:T(8,128)(2,1)S(1)}, u32[]{:S(2)}, u32[]{:S(2)}) collective-permute-start(bf16[48,1024]{1,0:T(8,128)(2,1)S(1)} %get-tuple-element.48), channel_id=1, source_target_pairs={{0,12},{1,13},{2,14},{3,15},{4,0},{5,1},{6,2},{7,3},{8,4},{9,5},{1... | collective-permute-start | bytes 294920 | tf_op jit(solution)/shard_map/ppermute | solution.py:332
  45.4 3.5 %collective-permute-done.2 = bf16[48,1024]{1,0:T(8,128)(2,1)S(1)} collective-permute-done((bf16[48,1024]{1,0:T(8,128)(2,1)S(1)}, bf16[48,1024]{1,0:T(8,128)(2,1)S(1)}, u32[]{:S(2)}, u32[]{:S(2)}) %collective-permute-start.2) | collective-permute-done | bytes 98336 | tf_op jit(solution)/shard_map/ppermute | solution.py:332
  53.2 3.0 %collective-permute-start.8 = (bf16[48,1024]{1,0:T(8,128)(2,1)S(1)}, bf16[48,1024]{1,0:T(8,128)(2,1)S(1)}, u32[]{:S(2)}, u32[]{:S(2)}) collective-permute-start(bf16[48,1024]{1,0:T(8,128)(2,1)S(1)} %get-tuple-element.47), channel_id=1, source_target_pairs={{0,3},{1,0},{2,1},{3,2},{4,7},{5,4},{6,5},{7,6},{8,11},{9,8},{10,9... | collective-permute-start | bytes 294920 | tf_op jit(solution)/shard_map/ppermute | solution.py:337
  59.7 6.2 %collective-permute-done.8 = bf16[48,1024]{1,0:T(8,128)(2,1)S(1)} collective-permute-done((bf16[48,1024]{1,0:T(8,128)(2,1)S(1)}, bf16[48,1024]{1,0:T(8,128)(2,1)S(1)}, u32[]{:S(2)}, u32[]{:S(2)}) %collective-permute-start.8) | collective-permute-done | bytes 98336 | tf_op jit(solution)/shard_map/ppermute | solution.py:337
  72.3 5.3 %collective-permute-done.4.refs_2_ = bf16[192,1024]{1,0:T(8,128)(2,1)} collective-permute-done((bf16[192,1024]{1,0:T(8,128)(2,1)S(1)}, bf16[192,1024]{1,0:T(8,128)(2,1)}, u32[]{:S(2)}, u32[]{:S(2)}) %collective-permute-start.4) | collective-permute-done | bytes 393248 | tf_op jit(solution)/shard_map/ppermute | solution.py:337
  77.6 8.3 %collective-permute-done.3.refs_1_ = bf16[192,1024]{1,0:T(8,128)(2,1)} collective-permute-done((bf16[192,1024]{1,0:T(8,128)(2,1)S(1)}, bf16[192,1024]{1,0:T(8,128)(2,1)}, u32[]{:S(2)}, u32[]{:S(2)}) %collective-permute-start.3) | collective-permute-done | bytes 393248 | tf_op jit(solution)/shard_map/ppermute | solution.py:337
  85.9 3.6 %collective-permute-done.9.refs_5_ = bf16[192,1024]{1,0:T(8,128)(2,1)} collective-permute-done((bf16[192,1024]{1,0:T(8,128)(2,1)S(1)}, bf16[192,1024]{1,0:T(8,128)(2,1)}, u32[]{:S(2)}, u32[]{:S(2)}) %collective-permute-start.9) | collective-permute-done | bytes 393248 | tf_op jit(solution)/shard_map/ppermute | solution.py:332
  89.5 4.3 %attention_grads.1 = bf16[16,144,128]{2,1,0:T(8,128)(2,1)} custom-call(s32[16]{0:T(128)S(1)} %get-tuple-element.36.start_ref, s32[16]{0:T(128)S(1)} %get-tuple-element.35.count_ref, s32[1]{0:T(128)} %bitcast.head_ref, bf16[128,2048]{1,0:T(8,128)(2,1)S(1)} %copy-done.3, bf16[192,1024]{1,0:T(8,128)(2,1)S(1)} %pad_maximum_fusion.refs_0_, ...), custom_call_target="tpu_custom_call" | custom-call | tf_op jit(solution)/shard_map/attention_grads/pallas_call | solution.py:131
  93.8 5.6 %all-to-all-start.2 = ((bf16[16,144,128]{2,1,0:T(8,128)(2,1)}), bf16[16,144,128]{2,1,0:T(8,128)(2,1)S(1)}, u32[]{:S(2)}, u32[]{:S(2)}) async-start(bf16[16,144,128]{2,1,0:T(8,128)(2,1)} %attention_grads.1), calls=%async_computation.2 | async-start | bytes 1179648 | tf_op jit(solution)/shard_map/all_to_all | solution.py:376
  100.5 5.0 %mixed_parts.1 = (bf16[192,1024]{1,0:T(8,128)(2,1)}, bf16[192,1024]{1,0:T(8,128)(2,1)}, bf16[192,1024]{1,0:T(8,128)(2,1)}, bf16[192,1024]{1,0:T(8,128)(2,1)}, bf...) custom-call(s32[16]{0:T(128)S(1)} %get-tuple-element.36.start_ref, ...), custom_call_target="tpu_custom_call" | custom-call | tf_op jit(solution)/shard_map/mixed_parts/pallas_call | solution.py:312
  110.5 6.0 %all-to-all-done.2.g_ref = bf16[16,144,128]{2,1,0:T(8,128)(2,1)S(1)} async-done(((bf16[16,144,128]{2,1,0:T(8,128)(2,1)}), bf16[16,144,128]{2,1,0:T(8,128)(2,1)S(1)}, u32[]{:S(2)}, u32[]{:S(2)}) %all-to-all-start.2) | async-done | bytes 589856 | tf_op jit(solution)/shard_map/all_to_all | solution.py:376
  117.8 7.7 %backward.1 = (bf16[16,144,128]{2,1,0:T(8,128)(2,1)}, bf16[2048,128]{1,0:T(8,128)(2,1)}, bf16[2048,128]{1,0:T(8,128)(2,1)}) custom-call(s32[8]{0:T(128)S(1)} %and_select_fusion.source_ref, s32[16]{0:T(128)S(1)} %get-tuple-element.39.owner_ref, bf16[16,144,128]{2,1,0:T(8,128)(2,1)S(1)} %all-to-all-done.q_ref, bf16[16,144,128]{2,1,0:T(8,128)(2,1)S(1)} %all-to-all-done.2.g_ref, ...), custom_call_target="tpu_custom_call" | custom-call | tf_op jit(solution)/shard_map/backward/pallas_call | solution.py:242
  125.6 5.1 %all-to-all-start.3 = ((bf16[16,144,128]{2,1,0:T(8,128)(2,1)}), bf16[16,144,128]{2,1,0:T(8,128)(2,1)S(1)}, u32[]{:S(2)}, u32[]{:S(2)}) async-start(bf16[16,144,128]{2,1,0:T(8,128)(2,1)} %get-tuple-element.30), calls=%async_computation.3 | async-start | bytes 1179648 | tf_op jit(solution)/shard_map/all_to_all | solution.py:376
  130.7 6.1 %collective-permute-start.12 = (bf16[192,1024]{1,0:T(8,128)(2,1)}, bf16[192,1024]{1,0:T(8,128)(2,1)S(1)}, u32[]{:S(2)}, u32[]{:S(2)}) collective-permute-start(bf16[192,1024]{1,0:T(8,128)(2,1)} %get-tuple-element.22), channel_id=1, source_target_pairs={{0,3},{1,0},{2,1},{3,2},{4,7},{5,4},{6,5},{7,6},{8,11},{9,8},{10,9... | collective-permute-start | bytes 1179656 | tf_op jit(solution)/shard_map/ppermute | solution.py:337
  136.8 6.9 %collective-permute-start.13 = (bf16[192,1024]{1,0:T(8,128)(2,1)}, bf16[192,1024]{1,0:T(8,128)(2,1)S(1)}, u32[]{:S(2)}, u32[]{:S(2)}) collective-permute-start(bf16[192,1024]{1,0:T(8,128)(2,1)} %get-tuple-element.23), channel_id=1, source_target_pairs={{0,2},{1,3},{2,0},{3,1},{4,6},{5,7},{6,4},{7,5},{8,10},{9,11},{10,... | collective-permute-start | bytes 1179656 | tf_op jit(solution)/shard_map/ppermute | solution.py:337
  145.8 6.6 %collective-permute-done.12 = bf16[192,1024]{1,0:T(8,128)(2,1)S(1)} collective-permute-done((bf16[192,1024]{1,0:T(8,128)(2,1)}, bf16[192,1024]{1,0:T(8,128)(2,1)S(1)}, u32[]{:S(2)}, u32[]{:S(2)}) %collective-permute-start.12) | collective-permute-done | bytes 393248 | tf_op jit(solution)/shard_map/ppermute | solution.py:337
  152.4 9.6 %collective-permute-done.13 = bf16[192,1024]{1,0:T(8,128)(2,1)S(1)} collective-permute-done((bf16[192,1024]{1,0:T(8,128)(2,1)}, bf16[192,1024]{1,0:T(8,128)(2,1)S(1)}, u32[]{:S(2)}, u32[]{:S(2)}) %collective-permute-start.13) | collective-permute-done | bytes 393248 | tf_op jit(solution)/shard_map/ppermute | solution.py:337
  167.6 7.8 %collective-permute-start.21 = (bf16[48,1024]{1,0:T(8,128)(2,1)S(1)}, bf16[48,1024]{1,0:T(8,128)(2,1)S(1)}, u32[]{:S(2)}, u32[]{:S(2)}) collective-permute-start(bf16[48,1024]{1,0:T(8,128)(2,1)S(1)} %get-tuple-element.44), channel_id=1, source_target_pairs={{0,3},{1,0},{2,1},{3,2},{4,7},{5,4},{6,5},{7,6},{8,11},{9,8},{10,9... | collective-permute-start | bytes 294920 | tf_op jit(solution)/shard_map/ppermute | solution.py:337
  175.4 5.7 %collective-permute-start.22 = (bf16[48,1024]{1,0:T(8,128)(2,1)S(1)}, bf16[48,1024]{1,0:T(8,128)(2,1)S(1)}, u32[]{:S(2)}, u32[]{:S(2)}) collective-permute-start(bf16[48,1024]{1,0:T(8,128)(2,1)S(1)} %get-tuple-element.46), channel_id=1, source_target_pairs={{0,2},{1,3},{2,0},{3,1},{4,6},{5,7},{6,4},{7,5},{8,10},{9,11},{10,... | collective-permute-start | bytes 294920 | tf_op jit(solution)/shard_map/ppermute | solution.py:337
  181.1 5.0 %collective-permute-start.27 = (bf16[1,128,128]{2,1,0:T(8,128)(2,1)S(1)}, bf16[1,128,128]{2,1,0:T(8,128)(2,1)S(1)}, u32[]{:S(2)}, u32[]{:S(2)}) collective-permute-start(bf16[1,128,128]{2,1,0:T(8,128)(2,1)S(1)} %fusion.6), channel_id=1, source_target_pairs={{0,128},{16,144},{32,160},{48,176},{64,192},{80,208},{96,224},{112... | collective-permute-start | bytes 98312 | tf_op jit(solution)/shard_map/ppermute | solution.py:342
  (100 shorter events, 39.4 us)
Async XLA Ops:
  5.0 25.7 %all-to-all-start = ((bf16[16,144,128]{2,1,0:T(8,128)(2,1)}), bf16[16,144,128]{2,1,0:T(8,128)(2,1)S(1)}, u32[]{:S(2)}, u32[]{:S(2)}) async-start(bf16[16,144,128]{2,1,0:T(8,128)(2,1)} %pack_queries.1), calls=%async_computation | async-start | bytes 1179648 | tf_op jit(solution)/shard_map/all_to_all | solution.py:376
  36.4 57.4 %all-to-all-start.1 = ((bf16[16,144,128]{2,1,0:T(8,128)(2,1)}), bf16[16,144,128]{2,1,0:T(8,128)(2,1)S(1)}, u32[]{:S(2)}, u32[]{:S(2)}) async-start(bf16[16,144,128]{2,1,0:T(8,128)(2,1)} %get-tuple-element.20.att_ref), calls=%async_computation.1 | async-start | bytes 1179648 | tf_op jit(solution)/shard_map/all_to_all | solution.py:376
  52.6 18.8 %collective-permute-start.5 = (bf16[192,1024]{1,0:T(8,128)(2,1)S(1)}, bf16[192,1024]{1,0:T(8,128)(2,1)S(1)}, u32[]{:S(2)}, u32[]{:S(2)}) collective-permute-start(bf16[192,1024]{1,0:T(8,128)(2,1)S(1)} %pad_maximum_fusion.refs_0_), channel_id=1, source_target_pairs={{0,3},{1,0},{2,1},{3,2},{4,7},{5,4},{6,5},{7,6},{8,11},{9,8},{10,9... | collective-permute-start | bytes 1179656 | tf_op jit(solution)/shard_map/ppermute | solution.py:337
  53.2 12.7 %collective-permute-start.8 = (bf16[48,1024]{1,0:T(8,128)(2,1)S(1)}, bf16[48,1024]{1,0:T(8,128)(2,1)S(1)}, u32[]{:S(2)}, u32[]{:S(2)}) collective-permute-start(bf16[48,1024]{1,0:T(8,128)(2,1)S(1)} %get-tuple-element.47), channel_id=1, source_target_pairs={{0,3},{1,0},{2,1},{3,2},{4,7},{5,4},{6,5},{7,6},{8,11},{9,8},{10,9... | collective-permute-start | bytes 294920 | tf_op jit(solution)/shard_map/ppermute | solution.py:337
  56.2 13.7 %collective-permute-start.7 = (bf16[48,1024]{1,0:T(8,128)(2,1)S(1)}, bf16[48,1024]{1,0:T(8,128)(2,1)S(1)}, u32[]{:S(2)}, u32[]{:S(2)}) collective-permute-start(bf16[48,1024]{1,0:T(8,128)(2,1)S(1)} %get-tuple-element.47), channel_id=1, source_target_pairs={{0,2},{1,3},{2,0},{3,1},{4,6},{5,7},{6,4},{7,5},{8,10},{9,11},{10,... | collective-permute-start | bytes 294920 | tf_op jit(solution)/shard_map/ppermute | solution.py:337
  56.2 13.7 %collective-permute-start.6 = (bf16[48,1024]{1,0:T(8,128)(2,1)S(1)}, bf16[48,1024]{1,0:T(8,128)(2,1)S(1)}, u32[]{:S(2)}, u32[]{:S(2)}) collective-permute-start(bf16[48,1024]{1,0:T(8,128)(2,1)S(1)} %get-tuple-element.47), channel_id=1, source_target_pairs={{0,1},{1,2},{2,3},{3,0},{4,5},{5,6},{6,7},{7,4},{8,9},{9,10},{10,1... | collective-permute-start | bytes 294920 | tf_op jit(solution)/shard_map/ppermute | solution.py:337
  58.4 19.2 %collective-permute-start.4 = (bf16[192,1024]{1,0:T(8,128)(2,1)S(1)}, bf16[192,1024]{1,0:T(8,128)(2,1)}, u32[]{:S(2)}, u32[]{:S(2)}) collective-permute-start(bf16[192,1024]{1,0:T(8,128)(2,1)S(1)} %pad_maximum_fusion.refs_0_), channel_id=1, source_target_pairs={{0,2},{1,3},{2,0},{3,1},{4,6},{5,7},{6,4},{7,5},{8,10},{9,11},{10,... | collective-permute-start | bytes 1179656 | tf_op jit(solution)/shard_map/ppermute | solution.py:337
  65.9 20.0 %collective-permute-start.3 = (bf16[192,1024]{1,0:T(8,128)(2,1)S(1)}, bf16[192,1024]{1,0:T(8,128)(2,1)}, u32[]{:S(2)}, u32[]{:S(2)}) collective-permute-start(bf16[192,1024]{1,0:T(8,128)(2,1)S(1)} %pad_maximum_fusion.refs_0_), channel_id=1, source_target_pairs={{0,1},{1,2},{2,3},{3,0},{4,5},{5,6},{6,7},{7,4},{8,9},{9,10},{10,1... | collective-permute-start | bytes 1179656 | tf_op jit(solution)/shard_map/ppermute | solution.py:337
  70.0 15.9 %collective-permute-start.11 = (bf16[192,1024]{1,0:T(8,128)(2,1)S(1)}, bf16[192,1024]{1,0:T(8,128)(2,1)}, u32[]{:S(2)}, u32[]{:S(2)}) collective-permute-start(bf16[192,1024]{1,0:T(8,128)(2,1)S(1)} %pad_maximum_fusion.1.refs_4_), channel_id=1, source_target_pairs={{0,12},{1,13},{2,14},{3,15},{4,0},{5,1},{6,2},{7,3},{8,4},{9,5},{1... | collective-permute-start | bytes 1179656 | tf_op jit(solution)/shard_map/ppermute | solution.py:332
  70.6 15.2 %collective-permute-start.10 = (bf16[192,1024]{1,0:T(8,128)(2,1)S(1)}, bf16[192,1024]{1,0:T(8,128)(2,1)}, u32[]{:S(2)}, u32[]{:S(2)}) collective-permute-start(bf16[192,1024]{1,0:T(8,128)(2,1)S(1)} %pad_maximum_fusion.1.refs_4_), channel_id=1, source_target_pairs={{0,8},{1,9},{2,10},{3,11},{4,12},{5,13},{6,14},{7,15},{8,0},{9,1},... | collective-permute-start | bytes 1179656 | tf_op jit(solution)/shard_map/ppermute | solution.py:332
  71.4 18.1 %collective-permute-start.9 = (bf16[192,1024]{1,0:T(8,128)(2,1)S(1)}, bf16[192,1024]{1,0:T(8,128)(2,1)}, u32[]{:S(2)}, u32[]{:S(2)}) collective-permute-start(bf16[192,1024]{1,0:T(8,128)(2,1)S(1)} %pad_maximum_fusion.1.refs_4_), channel_id=1, source_target_pairs={{0,4},{1,5},{2,6},{3,7},{4,8},{5,9},{6,10},{7,11},{8,12},{9,13},{1... | collective-permute-start | bytes 1179656 | tf_op jit(solution)/shard_map/ppermute | solution.py:332
  93.8 22.8 %all-to-all-start.2 = ((bf16[16,144,128]{2,1,0:T(8,128)(2,1)}), bf16[16,144,128]{2,1,0:T(8,128)(2,1)S(1)}, u32[]{:S(2)}, u32[]{:S(2)}) async-start(bf16[16,144,128]{2,1,0:T(8,128)(2,1)} %attention_grads.1), calls=%async_computation.2 | async-start | bytes 1179648 | tf_op jit(solution)/shard_map/all_to_all | solution.py:376
  108.5 37.2 %collective-permute-start.25 = (bf16[4,128,128]{2,1,0:T(8,128)(2,1)S(1)}, bf16[4,128,128]{2,1,0:T(8,128)(2,1)S(1)}, u32[]{:S(2)}, u32[]{:S(2)}) collective-permute-start(bf16[4,128,128]{2,1,0:T(8,128)(2,1)S(1)} %fusion), channel_id=1, source_target_pairs={{0,32},{16,48},{32,0},{48,16},{64,96},{80,112},{96,64},{112,80},{1... | collective-permute-start | bytes 393224 | tf_op jit(solution)/shard_map/ppermute | solution.py:342
  125.6 61.4 %all-to-all-start.3 = ((bf16[16,144,128]{2,1,0:T(8,128)(2,1)}), bf16[16,144,128]{2,1,0:T(8,128)(2,1)S(1)}, u32[]{:S(2)}, u32[]{:S(2)}) async-start(bf16[16,144,128]{2,1,0:T(8,128)(2,1)} %get-tuple-element.30), calls=%async_computation.3 | async-start | bytes 1179648 | tf_op jit(solution)/shard_map/all_to_all | solution.py:376
  130.7 21.7 %collective-permute-start.12 = (bf16[192,1024]{1,0:T(8,128)(2,1)}, bf16[192,1024]{1,0:T(8,128)(2,1)S(1)}, u32[]{:S(2)}, u32[]{:S(2)}) collective-permute-start(bf16[192,1024]{1,0:T(8,128)(2,1)} %get-tuple-element.22), channel_id=1, source_target_pairs={{0,3},{1,0},{2,1},{3,2},{4,7},{5,4},{6,5},{7,6},{8,11},{9,8},{10,9... | collective-permute-start | bytes 1179656 | tf_op jit(solution)/shard_map/ppermute | solution.py:337
  136.8 25.1 %collective-permute-start.13 = (bf16[192,1024]{1,0:T(8,128)(2,1)}, bf16[192,1024]{1,0:T(8,128)(2,1)S(1)}, u32[]{:S(2)}, u32[]{:S(2)}) collective-permute-start(bf16[192,1024]{1,0:T(8,128)(2,1)} %get-tuple-element.23), channel_id=1, source_target_pairs={{0,2},{1,3},{2,0},{3,1},{4,6},{5,7},{6,4},{7,5},{8,10},{9,11},{10,... | collective-permute-start | bytes 1179656 | tf_op jit(solution)/shard_map/ppermute | solution.py:337
  143.8 20.5 %collective-permute-start.14 = (bf16[192,1024]{1,0:T(8,128)(2,1)}, bf16[192,1024]{1,0:T(8,128)(2,1)S(1)}, u32[]{:S(2)}, u32[]{:S(2)}) collective-permute-start(bf16[192,1024]{1,0:T(8,128)(2,1)} %get-tuple-element.24), channel_id=1, source_target_pairs={{0,1},{1,2},{2,3},{3,0},{4,5},{5,6},{6,7},{7,4},{8,9},{9,10},{10,1... | collective-permute-start | bytes 1179656 | tf_op jit(solution)/shard_map/ppermute | solution.py:337
  144.6 21.1 %collective-permute-start.18 = (bf16[192,1024]{1,0:T(8,128)(2,1)S(1)}, bf16[192,1024]{1,0:T(8,128)(2,1)S(1)}, u32[]{:S(2)}, u32[]{:S(2)}) collective-permute-start(bf16[192,1024]{1,0:T(8,128)(2,1)S(1)} %copy-done.14), channel_id=1, source_target_pairs={{0,12},{1,13},{2,14},{3,15},{4,0},{5,1},{6,2},{7,3},{8,4},{9,5},{1... | collective-permute-start | bytes 1179656 | tf_op jit(solution)/shard_map/ppermute | solution.py:332
  145.7 20.9 %collective-permute-start.19 = (bf16[192,1024]{1,0:T(8,128)(2,1)S(1)}, bf16[192,1024]{1,0:T(8,128)(2,1)S(1)}, u32[]{:S(2)}, u32[]{:S(2)}) collective-permute-start(bf16[192,1024]{1,0:T(8,128)(2,1)S(1)} %copy-done.13), channel_id=1, source_target_pairs={{0,8},{1,9},{2,10},{3,11},{4,12},{5,13},{6,14},{7,15},{8,0},{9,1},... | collective-permute-start | bytes 1179656 | tf_op jit(solution)/shard_map/ppermute | solution.py:332
  152.4 14.9 %collective-permute-start.20 = (bf16[192,1024]{1,0:T(8,128)(2,1)S(1)}, bf16[192,1024]{1,0:T(8,128)(2,1)S(1)}, u32[]{:S(2)}, u32[]{:S(2)}) collective-permute-start(bf16[192,1024]{1,0:T(8,128)(2,1)S(1)} %copy-done.12), channel_id=1, source_target_pairs={{0,4},{1,5},{2,6},{3,7},{4,8},{5,9},{6,10},{7,11},{8,12},{9,13},{1... | collective-permute-start | bytes 1179656 | tf_op jit(solution)/shard_map/ppermute | solution.py:332
  162.0 13.4 %collective-permute-start.26 = (bf16[2,128,128]{2,1,0:T(8,128)(2,1)S(1)}, bf16[2,128,128]{2,1,0:T(8,128)(2,1)S(1)}, u32[]{:S(2)}, u32[]{:S(2)}) collective-permute-start(bf16[2,128,128]{2,1,0:T(8,128)(2,1)S(1)} %fusion.4), channel_id=1, source_target_pairs={{0,64},{16,80},{32,96},{48,112},{64,0},{80,16},{96,32},{112,48},{1... | collective-permute-start | bytes 196616 | tf_op jit(solution)/shard_map/ppermute | solution.py:342
  165.7 15.4 %collective-permute-start.17 = (bf16[48,1024]{1,0:T(8,128)(2,1)S(1)}, bf16[48,1024]{1,0:T(8,128)(2,1)S(1)}, u32[]{:S(2)}, u32[]{:S(2)}) collective-permute-start(bf16[48,1024]{1,0:T(8,128)(2,1)S(1)} %get-tuple-element.42), channel_id=1, source_target_pairs={{0,4},{1,5},{2,6},{3,7},{4,8},{5,9},{6,10},{7,11},{8,12},{9,13},{1... | collective-permute-start | bytes 294920 | tf_op jit(solution)/shard_map/ppermute | solution.py:332
  166.7 19.5 %collective-permute-start.16 = (bf16[48,1024]{1,0:T(8,128)(2,1)S(1)}, bf16[48,1024]{1,0:T(8,128)(2,1)S(1)}, u32[]{:S(2)}, u32[]{:S(2)}) collective-permute-start(bf16[48,1024]{1,0:T(8,128)(2,1)S(1)} %get-tuple-element.43), channel_id=1, source_target_pairs={{0,8},{1,9},{2,10},{3,11},{4,12},{5,13},{6,14},{7,15},{8,0},{9,1},... | collective-permute-start | bytes 294920 | tf_op jit(solution)/shard_map/ppermute | solution.py:332
  167.6 18.6 %collective-permute-start.21 = (bf16[48,1024]{1,0:T(8,128)(2,1)S(1)}, bf16[48,1024]{1,0:T(8,128)(2,1)S(1)}, u32[]{:S(2)}, u32[]{:S(2)}) collective-permute-start(bf16[48,1024]{1,0:T(8,128)(2,1)S(1)} %get-tuple-element.44), channel_id=1, source_target_pairs={{0,3},{1,0},{2,1},{3,2},{4,7},{5,4},{6,5},{7,6},{8,11},{9,8},{10,9... | collective-permute-start | bytes 294920 | tf_op jit(solution)/shard_map/ppermute | solution.py:337
  (23 other events, 336.5 us)

commit v5 on v3

--- a/solution.py
+++ b/solution.py
@@ -167,8 +167,8 @@
         source, base, skip, count = document(refs, doc, k_ref.shape[0] // BLOCK)
         tokens = pl.ds(pl.multiple_of(base * BLOCK, BLOCK), CAP * BLOCK)
         admitted = (lane >= skip * BLOCK) & (lane < (skip + count) * BLOCK)
-        queries = two_heads(q_ref[source])
-        scores = dot(queries, k_ref[tokens, :], ((1,), (1,))) * SCALE
+        queries = two_heads(q_ref[source] * SCALE)
+        scores = dot(queries, k_ref[tokens, :], ((1,), (1,)))
         scores = jnp.where(admitted, scores, MASKED)
         top = jnp.max(scores, axis=1, keepdims=True)
         terms = jnp.exp(scores - top)
@@ -243,10 +243,10 @@
     )(source, start, count, got_q, got_g, attended, weights, keys, values)
 
 
-def mixed_kernel(start_ref, count_ref, head_ref, packed_ref, proj_ref, *refs):
+def mixed_kernel(start_ref, count_ref, head_ref, core_ref, packed_ref, proj_ref, *refs):
     first, second = refs[:SIDE], refs[SIDE : 2 * SIDE]
     outs = refs[2 * SIDE : 4 * SIDE]
-    even_ref, odd_ref, sum_ref, sent_ref, weight_ref, sems = refs[4 * SIDE :]
+    mine_ref, theirs_ref, sum_ref, sent_ref, weight_ref, other_ref, sems = refs[4 * SIDE :]
     unpack_rows(start_ref, count_ref, packed_ref, sum_ref)
     unit = sum_ref.shape[0] // (SIDE * SIDE)
     half = proj_ref.shape[1] // 2
@@ -276,32 +276,36 @@
         for c in range(per_half):
             chunk = h * per_half + c
             weight_ref[chunk % 2, chunk // 2] = sums[h][:, c * BLOCK : (c + 1) * BLOCK]
-    for c, out_ref in enumerate((even_ref, odd_ref)):
-        copies.append(pltpu.make_async_copy(weight_ref.at[c], out_ref, sems.at[2 * SIDE + c]))
-        copies[-1].start()
+    core = core_ref[0]
+    other_ref[...] = weight_ref[1 - core].astype(jnp.bfloat16)
+    copies.append(pltpu.make_async_copy(other_ref, theirs_ref, sems.at[2 * SIDE]))
+    copies[-1].start()
+    copies.append(pltpu.make_async_copy(weight_ref.at[core], mine_ref, sems.at[2 * SIDE + 1]))
+    copies[-1].start()
     for copy in copies:
         copy.wait()
 
 
-def mixed_parts(start, count, head, packed, out_proj, first, second):
+def mixed_parts(start, count, head, core, packed, out_proj, first, second):
     inner, width = out_proj.shape
     row_count = SIDE * first[0].shape[0]
     part = HBM(first[0].shape, jnp.bfloat16)
-    sums = HBM((width // BLOCK // 2, inner, BLOCK), jnp.float32)
+    chunks = (width // BLOCK // 2, inner, BLOCK)
     outs = pl.pallas_call(
         mixed_kernel,
-        out_shape=(part,) * (2 * SIDE) + (sums,) * 2,
-        in_specs=smem_specs(3) + vmem_specs(2 + 2 * SIDE),
+        out_shape=(part,) * (2 * SIDE) + (HBM(chunks, jnp.float32), HBM(chunks, jnp.bfloat16)),
+        in_specs=smem_specs(4) + vmem_specs(2 + 2 * SIDE),
         out_specs=tuple([pl.BlockSpec(memory_space=HBM)] * (2 * SIDE + 2)),
         scratch_shapes=[
             pltpu.VMEM((row_count, inner), jnp.float32),
             pltpu.VMEM((2 * SIDE, *first[0].shape), jnp.bfloat16),
-            pltpu.VMEM((2, width // BLOCK // 2, inner, BLOCK), jnp.float32),
+            pltpu.VMEM((2, *chunks), jnp.float32),
+            pltpu.VMEM(chunks, jnp.bfloat16),
             pltpu.SemaphoreType.DMA((2 * SIDE + 2,)),
         ],
         compiler_params=LIMIT,
         name="mixed_parts",
-    )(start, count, head, packed, out_proj, *first, *second)
+    )(start, count, head, core, packed, out_proj, *first, *second)
     return outs[:SIDE], outs[SIDE : 2 * SIDE], outs[2 * SIDE], outs[2 * SIDE + 1]
 
 
@@ -315,11 +319,15 @@
     return lax.ppermute(value, "head", perm)
 
 
+def add_other(mine, theirs, distance):
+    swap = [(s, s ^ distance) for s in range(N_SEQ)]
+    other = lax.ppermute(theirs, "seq", swap)
+    return mine + other.astype(jnp.float32)
+
+
 def halve(low, high, side, distance):
-    swap = [(s, s ^ distance) for s in range(N_SEQ)]
     theirs = jnp.where(side == 0, high, low).astype(jnp.bfloat16)
-    other = lax.ppermute(theirs, "seq", swap)
-    return jnp.where(side == 0, low, high) + other.astype(jnp.float32)
+    return add_other(jnp.where(side == 0, low, high), theirs, distance)
 
 
 def shift(value, move, k):
@@ -342,7 +350,9 @@
     terms = [parts[0]] + [shift(parts[k], one, SIDE - k) for k in range(1, SIDE)]
     rows = total(terms)
     unit = rows.shape[0] // SIDE
-    terms = [rows[:unit]] + [shift(rows[k * unit : (k + 1) * unit], two, SIDE - k) for k in range(1, SIDE)]
+    terms = [rows[:unit]] + [
+        shift(rows[k * unit : (k + 1) * unit], two, SIDE - k) for k in range(1, SIDE)
+    ]
     return total(terms)
 
 
@@ -379,15 +389,15 @@
     home = to_all(attended)
     got_g = to_all(attention_grads(row_start, row_span, head, out_proj, first, second))
 
-    m_first, m_second, even, odd = mixed_parts(row_start, row_span, head, home, out_proj, first, second)
+    core = shard % 2
+    m_first, m_second, mine, theirs = mixed_parts(row_start, row_span, head, core[None], home, out_proj, first, second)
     mixed = jnp.concatenate(
         [scatter_sum(m_first, along_y, along_x), scatter_sum(m_second, along_x, along_y)],
         axis=1,
     )
 
-    core = shard % 2
     chip = shard // 2
-    grad_wo = halve(even, odd, core, 1)
+    grad_wo = add_other(mine, theirs, 1)
     for bit in range(3):
         halves = grad_wo.reshape(-1, 2, *grad_wo.shape[1:])
         grad_wo = halve(halves[:, 0], halves[:, 1], (chip >> bit) & 1, 2 << bit)

time: 189 us -> 189 us (level)
  no operation moved by 1% of the time
where the time goes in v5:
time: 189 us; the launch traced here: 188 us
  starting transfers between devices  81.5 us (43%)
  waiting for transfers between devices  72.3 us (38%)
  Pallas kernels  24.8 us (13%)
  other arithmetic  4.72 us (2%)
  local copies, waits for them, and re-layouts  3.59 us (2%)
    ppermute x12, waiting for transfers between devices, along_y(): return lax.ppermute(value, 'head', perm)  37.3 us
    ppermute x12, starting transfers between devices, along_y(): return lax.ppermute(value, 'head', perm)  37 us
    all_to_all x4, starting transfers between devices, to_all(): return lax.all_to_all(value, 'seq', split_axis=0, concat_axis=0, tiled=True)  24.1 us
    all_to_all x4, waiting for transfers between devices, to_all(): return lax.all_to_all(value, 'seq', split_axis=0, concat_axis=0, tiled=True)  22.7 us
    ppermute x12, waiting for transfers between devices, along_x(): return lax.ppermute(value, 'head', perm)  10.8 us
    ppermute x12, starting transfers between devices, along_x(): return lax.ppermute(value, 'head', perm)  10.7 us
    ppermute x4, starting transfers between devices, add_other(): other = lax.ppermute(theirs, 'seq', swap)  9.83 us
    pallas_call x1, Pallas kernels, forward(): pl.pallas_call(forward_kernel, out_shape=(jax.ShapeDtypeStruct(got_q.shap...  5.57 us
  transfers between devices with their start and end apart: 32, of which 13 were waited for; matrix products, arithmetic and copies ran while one was open for 2% of the time, Pallas kernels for 9%

profile of v5, /device:TPU:8, one launch (start us, length us, event | category | flops | bytes accessed | tf_op | source)
XLA Modules:
  0.0 187.9 jit_solution(7026518002118909455)
XLA Ops:
  5.0 8.7 %all-to-all-start = ((bf16[16,144,128]{2,1,0:T(8,128)(2,1)}), bf16[16,144,128]{2,1,0:T(8,128)(2,1)S(1)}, u32[]{:S(2)}, u32[]{:S(2)}) async-start(bf16[16,144,128]{2,1,0:T(8,128)(2,1)} %pack_queries.1), calls=%async_computation | async-start | bytes 1179648 | tf_op jit(solution)/shard_map/all_to_all | solution.py:360
  14.3 16.5 %all-to-all-done.q_ref = bf16[16,144,128]{2,1,0:T(8,128)(2,1)S(1)} async-done(((bf16[16,144,128]{2,1,0:T(8,128)(2,1)}), bf16[16,144,128]{2,1,0:T(8,128)(2,1)S(1)}, u32[]{:S(2)}, u32[]{:S(2)}) %all-to-all-start) | async-done | bytes 589856 | tf_op jit(solution)/shard_map/all_to_all | solution.py:360
  30.8 5.6 %forward.1 = (bf16[16,144,128]{2,1,0:T(8,128)(2,1)}, bf16[8,288,384]{2,1,0:T(8,128)(2,1)}) custom-call(s32[8]{0:T(128)S(1)} %and_select_fusion.source_ref, s32[8]{0:T(128)S(1)} %get-tuple-element.38.start_ref, s32[8]{0:T(128)S(1)} %get-tuple-element.37.count_ref, bf16[16,144,128]{2,1,0:T(8,128)(2,1)S(1)} %all-to-all-done.q_ref, ...), custom_call_target="tpu_custom_call" | custom-call | tf_op jit(solution)/shard_map/forward/pallas_call | solution.py:188
  36.4 4.6 %all-to-all-start.1 = ((bf16[16,144,128]{2,1,0:T(8,128)(2,1)}), bf16[16,144,128]{2,1,0:T(8,128)(2,1)S(1)}, u32[]{:S(2)}, u32[]{:S(2)}) async-start(bf16[16,144,128]{2,1,0:T(8,128)(2,1)} %get-tuple-element.20.att_ref), calls=%async_computation.1 | async-start | bytes 1179648 | tf_op jit(solution)/shard_map/all_to_all | solution.py:360
  41.0 2.8 %collective-permute-start.2 = (bf16[48,1024]{1,0:T(8,128)(2,1)S(1)}, bf16[48,1024]{1,0:T(8,128)(2,1)S(1)}, u32[]{:S(2)}, u32[]{:S(2)}) collective-permute-start(bf16[48,1024]{1,0:T(8,128)(2,1)S(1)} %get-tuple-element.46), channel_id=1, source_target_pairs={{0,12},{1,13},{2,14},{3,15},{4,0},{5,1},{6,2},{7,3},{8,4},{9,5},{1... | collective-permute-start | bytes 294920 | tf_op jit(solution)/shard_map/ppermute | solution.py:314
  45.6 3.5 %collective-permute-done.2 = bf16[48,1024]{1,0:T(8,128)(2,1)S(1)} collective-permute-done((bf16[48,1024]{1,0:T(8,128)(2,1)S(1)}, bf16[48,1024]{1,0:T(8,128)(2,1)S(1)}, u32[]{:S(2)}, u32[]{:S(2)}) %collective-permute-start.2) | collective-permute-done | bytes 98336 | tf_op jit(solution)/shard_map/ppermute | solution.py:314
  53.3 3.0 %collective-permute-start.8 = (bf16[48,1024]{1,0:T(8,128)(2,1)S(1)}, bf16[48,1024]{1,0:T(8,128)(2,1)S(1)}, u32[]{:S(2)}, u32[]{:S(2)}) collective-permute-start(bf16[48,1024]{1,0:T(8,128)(2,1)S(1)} %get-tuple-element.45), channel_id=1, source_target_pairs={{0,3},{1,0},{2,1},{3,2},{4,7},{5,4},{6,5},{7,6},{8,11},{9,8},{10,9... | collective-permute-start | bytes 294920 | tf_op jit(solution)/shard_map/ppermute | solution.py:319
  59.8 6.2 %collective-permute-done.8 = bf16[48,1024]{1,0:T(8,128)(2,1)S(1)} collective-permute-done((bf16[48,1024]{1,0:T(8,128)(2,1)S(1)}, bf16[48,1024]{1,0:T(8,128)(2,1)S(1)}, u32[]{:S(2)}, u32[]{:S(2)}) %collective-permute-start.8) | collective-permute-done | bytes 98336 | tf_op jit(solution)/shard_map/ppermute | solution.py:319
  72.4 5.2 %collective-permute-done.4.refs_2_ = bf16[192,1024]{1,0:T(8,128)(2,1)S(1)} collective-permute-done((bf16[192,1024]{1,0:T(8,128)(2,1)S(1)}, bf16[192,1024]{1,0:T(8,128)(2,1)S(1)}, u32[]{:S(2)}, u32[]{:S(2)}) %collective-permute-start.4) | collective-permute-done | bytes 393248 | tf_op jit(solution)/shard_map/ppermute | solution.py:319
  77.6 8.4 %collective-permute-done.3.refs_1_ = bf16[192,1024]{1,0:T(8,128)(2,1)} collective-permute-done((bf16[192,1024]{1,0:T(8,128)(2,1)S(1)}, bf16[192,1024]{1,0:T(8,128)(2,1)}, u32[]{:S(2)}, u32[]{:S(2)}) %collective-permute-start.3) | collective-permute-done | bytes 393248 | tf_op jit(solution)/shard_map/ppermute | solution.py:319
  86.0 3.6 %collective-permute-done.9.refs_5_ = bf16[192,1024]{1,0:T(8,128)(2,1)} collective-permute-done((bf16[192,1024]{1,0:T(8,128)(2,1)S(1)}, bf16[192,1024]{1,0:T(8,128)(2,1)}, u32[]{:S(2)}, u32[]{:S(2)}) %collective-permute-start.9) | collective-permute-done | bytes 393248 | tf_op jit(solution)/shard_map/ppermute | solution.py:314
  89.6 4.2 %attention_grads.1 = bf16[16,144,128]{2,1,0:T(8,128)(2,1)} custom-call(s32[16]{0:T(128)S(1)} %get-tuple-element.36.start_ref, s32[16]{0:T(128)S(1)} %get-tuple-element.35.count_ref, s32[1]{0:T(128)} %bitcast.head_ref, bf16[128,2048]{1,0:T(8,128)(2,1)S(1)} %copy-done, bf16[192,1024]{1,0:T(8,128)(2,1)S(1)} %pad_maximum_fusion.refs_0_, ...), custom_call_target="tpu_custom_call" | custom-call | tf_op jit(solution)/shard_map/attention_grads/pallas_call | solution.py:131
  93.8 5.7 %all-to-all-start.2 = ((bf16[16,144,128]{2,1,0:T(8,128)(2,1)}), bf16[16,144,128]{2,1,0:T(8,128)(2,1)S(1)}, u32[]{:S(2)}, u32[]{:S(2)}) async-start(bf16[16,144,128]{2,1,0:T(8,128)(2,1)} %attention_grads.1), calls=%async_computation.2 | async-start | bytes 1179648 | tf_op jit(solution)/shard_map/all_to_all | solution.py:360
  100.4 4.9 %mixed_parts.1 = (bf16[192,1024]{1,0:T(8,128)(2,1)}, bf16[192,1024]{1,0:T(8,128)(2,1)}, bf16[192,1024]{1,0:T(8,128)(2,1)}, bf16[192,1024]{1,0:T(8,128)(2,1)}, bf...) custom-call(s32[16]{0:T(128)S(1)} %get-tuple-element.36.start_ref, ...), custom_call_target="tpu_custom_call" | custom-call | tf_op jit(solution)/shard_map/mixed_parts/pallas_call | solution.py:294
  110.4 6.2 %all-to-all-done.2.g_ref = bf16[16,144,128]{2,1,0:T(8,128)(2,1)S(1)} async-done(((bf16[16,144,128]{2,1,0:T(8,128)(2,1)}), bf16[16,144,128]{2,1,0:T(8,128)(2,1)S(1)}, u32[]{:S(2)}, u32[]{:S(2)}) %all-to-all-start.2) | async-done | bytes 589856 | tf_op jit(solution)/shard_map/all_to_all | solution.py:360
  118.0 5.5 %backward.1 = (bf16[16,144,128]{2,1,0:T(8,128)(2,1)}, bf16[2048,128]{1,0:T(8,128)(2,1)}, bf16[2048,128]{1,0:T(8,128)(2,1)}) custom-call(s32[8]{0:T(128)S(1)} %and_select_fusion.source_ref, s32[8]{0:T(128)S(1)} %get-tuple-element.38.start_ref, s32[8]{0:T(128)S(1)} %get-tuple-element.37.count_ref, bf16[16,144,128]{2,1,0:T(8,128)(2,1)S(1)} %all-to-all-done.q_ref, ...), custom_call_target="tpu_custom_call" | custom-call | tf_op jit(solution)/shard_map/backward/pallas_call | solution.py:232
  123.6 5.1 %all-to-all-start.3 = ((bf16[16,144,128]{2,1,0:T(8,128)(2,1)}), bf16[16,144,128]{2,1,0:T(8,128)(2,1)S(1)}, u32[]{:S(2)}, u32[]{:S(2)}) async-start(bf16[16,144,128]{2,1,0:T(8,128)(2,1)} %get-tuple-element.30), calls=%async_computation.3 | async-start | bytes 1179648 | tf_op jit(solution)/shard_map/all_to_all | solution.py:360
  128.6 6.1 %collective-permute-start.12 = (bf16[192,1024]{1,0:T(8,128)(2,1)}, bf16[192,1024]{1,0:T(8,128)(2,1)S(1)}, u32[]{:S(2)}, u32[]{:S(2)}) collective-permute-start(bf16[192,1024]{1,0:T(8,128)(2,1)} %get-tuple-element.22), channel_id=1, source_target_pairs={{0,3},{1,0},{2,1},{3,2},{4,7},{5,4},{6,5},{7,6},{8,11},{9,8},{10,9... | collective-permute-start | bytes 1179656 | tf_op jit(solution)/shard_map/ppermute | solution.py:319
  134.8 6.9 %collective-permute-start.13 = (bf16[192,1024]{1,0:T(8,128)(2,1)}, bf16[192,1024]{1,0:T(8,128)(2,1)S(1)}, u32[]{:S(2)}, u32[]{:S(2)}) collective-permute-start(bf16[192,1024]{1,0:T(8,128)(2,1)} %get-tuple-element.23), channel_id=1, source_target_pairs={{0,2},{1,3},{2,0},{3,1},{4,6},{5,7},{6,4},{7,5},{8,10},{9,11},{10,... | collective-permute-start | bytes 1179656 | tf_op jit(solution)/shard_map/ppermute | solution.py:319
  143.8 6.4 %collective-permute-done.12 = bf16[192,1024]{1,0:T(8,128)(2,1)S(1)} collective-permute-done((bf16[192,1024]{1,0:T(8,128)(2,1)}, bf16[192,1024]{1,0:T(8,128)(2,1)S(1)}, u32[]{:S(2)}, u32[]{:S(2)}) %collective-permute-start.12) | collective-permute-done | bytes 393248 | tf_op jit(solution)/shard_map/ppermute | solution.py:319
  150.3 9.6 %collective-permute-done.13 = bf16[192,1024]{1,0:T(8,128)(2,1)S(1)} collective-permute-done((bf16[192,1024]{1,0:T(8,128)(2,1)}, bf16[192,1024]{1,0:T(8,128)(2,1)S(1)}, u32[]{:S(2)}, u32[]{:S(2)}) %collective-permute-start.13) | collective-permute-done | bytes 393248 | tf_op jit(solution)/shard_map/ppermute | solution.py:319
  165.5 7.7 %collective-permute-start.21 = (bf16[48,1024]{1,0:T(8,128)(2,1)S(1)}, bf16[48,1024]{1,0:T(8,128)(2,1)S(1)}, u32[]{:S(2)}, u32[]{:S(2)}) collective-permute-start(bf16[48,1024]{1,0:T(8,128)(2,1)S(1)} %get-tuple-element.42), channel_id=1, source_target_pairs={{0,3},{1,0},{2,1},{3,2},{4,7},{5,4},{6,5},{7,6},{8,11},{9,8},{10,9... | collective-permute-start | bytes 294920 | tf_op jit(solution)/shard_map/ppermute | solution.py:319
  173.3 5.7 %collective-permute-start.22 = (bf16[48,1024]{1,0:T(8,128)(2,1)S(1)}, bf16[48,1024]{1,0:T(8,128)(2,1)S(1)}, u32[]{:S(2)}, u32[]{:S(2)}) collective-permute-start(bf16[48,1024]{1,0:T(8,128)(2,1)S(1)} %get-tuple-element.44), channel_id=1, source_target_pairs={{0,2},{1,3},{2,0},{3,1},{4,6},{5,7},{6,4},{7,5},{8,10},{9,11},{10,... | collective-permute-start | bytes 294920 | tf_op jit(solution)/shard_map/ppermute | solution.py:319
  179.0 5.0 %collective-permute-start.27 = (bf16[1,128,128]{2,1,0:T(8,128)(2,1)S(1)}, bf16[1,128,128]{2,1,0:T(8,128)(2,1)S(1)}, u32[]{:S(2)}, u32[]{:S(2)}) collective-permute-start(bf16[1,128,128]{2,1,0:T(8,128)(2,1)S(1)} %fusion.6), channel_id=1, source_target_pairs={{0,128},{16,144},{32,160},{48,176},{64,192},{80,208},{96,224},{112... | collective-permute-start | bytes 98312 | tf_op jit(solution)/shard_map/ppermute | solution.py:324
  (102 shorter events, 39.7 us)
Async XLA Ops:
  5.0 25.8 %all-to-all-start = ((bf16[16,144,128]{2,1,0:T(8,128)(2,1)}), bf16[16,144,128]{2,1,0:T(8,128)(2,1)S(1)}, u32[]{:S(2)}, u32[]{:S(2)}) async-start(bf16[16,144,128]{2,1,0:T(8,128)(2,1)} %pack_queries.1), calls=%async_computation | async-start | bytes 1179648 | tf_op jit(solution)/shard_map/all_to_all | solution.py:360
  36.4 57.4 %all-to-all-start.1 = ((bf16[16,144,128]{2,1,0:T(8,128)(2,1)}), bf16[16,144,128]{2,1,0:T(8,128)(2,1)S(1)}, u32[]{:S(2)}, u32[]{:S(2)}) async-start(bf16[16,144,128]{2,1,0:T(8,128)(2,1)} %get-tuple-element.20.att_ref), calls=%async_computation.1 | async-start | bytes 1179648 | tf_op jit(solution)/shard_map/all_to_all | solution.py:360
  52.8 18.8 %collective-permute-start.5 = (bf16[192,1024]{1,0:T(8,128)(2,1)S(1)}, bf16[192,1024]{1,0:T(8,128)(2,1)S(1)}, u32[]{:S(2)}, u32[]{:S(2)}) collective-permute-start(bf16[192,1024]{1,0:T(8,128)(2,1)S(1)} %pad_maximum_fusion.refs_0_), channel_id=1, source_target_pairs={{0,3},{1,0},{2,1},{3,2},{4,7},{5,4},{6,5},{7,6},{8,11},{9,8},{10,9... | collective-permute-start | bytes 1179656 | tf_op jit(solution)/shard_map/ppermute | solution.py:319
  53.3 12.7 %collective-permute-start.8 = (bf16[48,1024]{1,0:T(8,128)(2,1)S(1)}, bf16[48,1024]{1,0:T(8,128)(2,1)S(1)}, u32[]{:S(2)}, u32[]{:S(2)}) collective-permute-start(bf16[48,1024]{1,0:T(8,128)(2,1)S(1)} %get-tuple-element.45), channel_id=1, source_target_pairs={{0,3},{1,0},{2,1},{3,2},{4,7},{5,4},{6,5},{7,6},{8,11},{9,8},{10,9... | collective-permute-start | bytes 294920 | tf_op jit(solution)/shard_map/ppermute | solution.py:319
  56.3 13.7 %collective-permute-start.7 = (bf16[48,1024]{1,0:T(8,128)(2,1)S(1)}, bf16[48,1024]{1,0:T(8,128)(2,1)S(1)}, u32[]{:S(2)}, u32[]{:S(2)}) collective-permute-start(bf16[48,1024]{1,0:T(8,128)(2,1)S(1)} %get-tuple-element.45), channel_id=1, source_target_pairs={{0,2},{1,3},{2,0},{3,1},{4,6},{5,7},{6,4},{7,5},{8,10},{9,11},{10,... | collective-permute-start | bytes 294920 | tf_op jit(solution)/shard_map/ppermute | solution.py:319
  56.3 13.7 %collective-permute-start.6 = (bf16[48,1024]{1,0:T(8,128)(2,1)S(1)}, bf16[48,1024]{1,0:T(8,128)(2,1)S(1)}, u32[]{:S(2)}, u32[]{:S(2)}) collective-permute-start(bf16[48,1024]{1,0:T(8,128)(2,1)S(1)} %get-tuple-element.45), channel_id=1, source_target_pairs={{0,1},{1,2},{2,3},{3,0},{4,5},{5,6},{6,7},{7,4},{8,9},{9,10},{10,1... | collective-permute-start | bytes 294920 | tf_op jit(solution)/shard_map/ppermute | solution.py:319
  58.5 19.1 %collective-permute-start.4 = (bf16[192,1024]{1,0:T(8,128)(2,1)S(1)}, bf16[192,1024]{1,0:T(8,128)(2,1)S(1)}, u32[]{:S(2)}, u32[]{:S(2)}) collective-permute-start(bf16[192,1024]{1,0:T(8,128)(2,1)S(1)} %pad_maximum_fusion.refs_0_), channel_id=1, source_target_pairs={{0,2},{1,3},{2,0},{3,1},{4,6},{5,7},{6,4},{7,5},{8,10},{9,11},{10,... | collective-permute-start | bytes 1179656 | tf_op jit(solution)/shard_map/ppermute | solution.py:319
  66.0 20.0 %collective-permute-start.3 = (bf16[192,1024]{1,0:T(8,128)(2,1)S(1)}, bf16[192,1024]{1,0:T(8,128)(2,1)}, u32[]{:S(2)}, u32[]{:S(2)}) collective-permute-start(bf16[192,1024]{1,0:T(8,128)(2,1)S(1)} %pad_maximum_fusion.refs_0_), channel_id=1, source_target_pairs={{0,1},{1,2},{2,3},{3,0},{4,5},{5,6},{6,7},{7,4},{8,9},{9,10},{10,1... | collective-permute-start | bytes 1179656 | tf_op jit(solution)/shard_map/ppermute | solution.py:319
  70.1 15.9 %collective-permute-start.11 = (bf16[192,1024]{1,0:T(8,128)(2,1)S(1)}, bf16[192,1024]{1,0:T(8,128)(2,1)}, u32[]{:S(2)}, u32[]{:S(2)}) collective-permute-start(bf16[192,1024]{1,0:T(8,128)(2,1)S(1)} %pad_maximum_fusion.1.refs_4_), channel_id=1, source_target_pairs={{0,12},{1,13},{2,14},{3,15},{4,0},{5,1},{6,2},{7,3},{8,4},{9,5},{1... | collective-permute-start | bytes 1179656 | tf_op jit(solution)/shard_map/ppermute | solution.py:314
  70.7 15.2 %collective-permute-start.10 = (bf16[192,1024]{1,0:T(8,128)(2,1)S(1)}, bf16[192,1024]{1,0:T(8,128)(2,1)}, u32[]{:S(2)}, u32[]{:S(2)}) collective-permute-start(bf16[192,1024]{1,0:T(8,128)(2,1)S(1)} %pad_maximum_fusion.1.refs_4_), channel_id=1, source_target_pairs={{0,8},{1,9},{2,10},{3,11},{4,12},{5,13},{6,14},{7,15},{8,0},{9,1},... | collective-permute-start | bytes 1179656 | tf_op jit(solution)/shard_map/ppermute | solution.py:314
  71.5 18.1 %collective-permute-start.9 = (bf16[192,1024]{1,0:T(8,128)(2,1)S(1)}, bf16[192,1024]{1,0:T(8,128)(2,1)}, u32[]{:S(2)}, u32[]{:S(2)}) collective-permute-start(bf16[192,1024]{1,0:T(8,128)(2,1)S(1)} %pad_maximum_fusion.1.refs_4_), channel_id=1, source_target_pairs={{0,4},{1,5},{2,6},{3,7},{4,8},{5,9},{6,10},{7,11},{8,12},{9,13},{1... | collective-permute-start | bytes 1179656 | tf_op jit(solution)/shard_map/ppermute | solution.py:314
  93.8 22.8 %all-to-all-start.2 = ((bf16[16,144,128]{2,1,0:T(8,128)(2,1)}), bf16[16,144,128]{2,1,0:T(8,128)(2,1)S(1)}, u32[]{:S(2)}, u32[]{:S(2)}) async-start(bf16[16,144,128]{2,1,0:T(8,128)(2,1)} %attention_grads.1), calls=%async_computation.2 | async-start | bytes 1179648 | tf_op jit(solution)/shard_map/all_to_all | solution.py:360
  108.4 35.2 %collective-permute-start.25 = (bf16[4,128,128]{2,1,0:T(8,128)(2,1)S(1)}, bf16[4,128,128]{2,1,0:T(8,128)(2,1)S(1)}, u32[]{:S(2)}, u32[]{:S(2)}) collective-permute-start(bf16[4,128,128]{2,1,0:T(8,128)(2,1)S(1)} %fusion), channel_id=1, source_target_pairs={{0,32},{16,48},{32,0},{48,16},{64,96},{80,112},{96,64},{112,80},{1... | collective-permute-start | bytes 393224 | tf_op jit(solution)/shard_map/ppermute | solution.py:324
  123.6 61.4 %all-to-all-start.3 = ((bf16[16,144,128]{2,1,0:T(8,128)(2,1)}), bf16[16,144,128]{2,1,0:T(8,128)(2,1)S(1)}, u32[]{:S(2)}, u32[]{:S(2)}) async-start(bf16[16,144,128]{2,1,0:T(8,128)(2,1)} %get-tuple-element.30), calls=%async_computation.3 | async-start | bytes 1179648 | tf_op jit(solution)/shard_map/all_to_all | solution.py:360
  128.6 21.6 %collective-permute-start.12 = (bf16[192,1024]{1,0:T(8,128)(2,1)}, bf16[192,1024]{1,0:T(8,128)(2,1)S(1)}, u32[]{:S(2)}, u32[]{:S(2)}) collective-permute-start(bf16[192,1024]{1,0:T(8,128)(2,1)} %get-tuple-element.22), channel_id=1, source_target_pairs={{0,3},{1,0},{2,1},{3,2},{4,7},{5,4},{6,5},{7,6},{8,11},{9,8},{10,9... | collective-permute-start | bytes 1179656 | tf_op jit(solution)/shard_map/ppermute | solution.py:319
  134.8 25.1 %collective-permute-start.13 = (bf16[192,1024]{1,0:T(8,128)(2,1)}, bf16[192,1024]{1,0:T(8,128)(2,1)S(1)}, u32[]{:S(2)}, u32[]{:S(2)}) collective-permute-start(bf16[192,1024]{1,0:T(8,128)(2,1)} %get-tuple-element.23), channel_id=1, source_target_pairs={{0,2},{1,3},{2,0},{3,1},{4,6},{5,7},{6,4},{7,5},{8,10},{9,11},{10,... | collective-permute-start | bytes 1179656 | tf_op jit(solution)/shard_map/ppermute | solution.py:319
  141.7 20.5 %collective-permute-start.14 = (bf16[192,1024]{1,0:T(8,128)(2,1)}, bf16[192,1024]{1,0:T(8,128)(2,1)S(1)}, u32[]{:S(2)}, u32[]{:S(2)}) collective-permute-start(bf16[192,1024]{1,0:T(8,128)(2,1)} %get-tuple-element.24), channel_id=1, source_target_pairs={{0,1},{1,2},{2,3},{3,0},{4,5},{5,6},{6,7},{7,4},{8,9},{9,10},{10,1... | collective-permute-start | bytes 1179656 | tf_op jit(solution)/shard_map/ppermute | solution.py:319
  142.6 21.1 %collective-permute-start.18 = (bf16[192,1024]{1,0:T(8,128)(2,1)}, bf16[192,1024]{1,0:T(8,128)(2,1)S(1)}, u32[]{:S(2)}, u32[]{:S(2)}) collective-permute-start(bf16[192,1024]{1,0:T(8,128)(2,1)} %get-tuple-element.26), channel_id=1, source_target_pairs={{0,12},{1,13},{2,14},{3,15},{4,0},{5,1},{6,2},{7,3},{8,4},{9,5},{1... | collective-permute-start | bytes 1179656 | tf_op jit(solution)/shard_map/ppermute | solution.py:314
  143.7 20.9 %collective-permute-start.19 = (bf16[192,1024]{1,0:T(8,128)(2,1)S(1)}, bf16[192,1024]{1,0:T(8,128)(2,1)S(1)}, u32[]{:S(2)}, u32[]{:S(2)}) collective-permute-start(bf16[192,1024]{1,0:T(8,128)(2,1)S(1)} %copy-done.14), channel_id=1, source_target_pairs={{0,8},{1,9},{2,10},{3,11},{4,12},{5,13},{6,14},{7,15},{8,0},{9,1},... | collective-permute-start | bytes 1179656 | tf_op jit(solution)/shard_map/ppermute | solution.py:314
  150.3 14.9 %collective-permute-start.20 = (bf16[192,1024]{1,0:T(8,128)(2,1)S(1)}, bf16[192,1024]{1,0:T(8,128)(2,1)S(1)}, u32[]{:S(2)}, u32[]{:S(2)}) collective-permute-start(bf16[192,1024]{1,0:T(8,128)(2,1)S(1)} %copy-done.13), channel_id=1, source_target_pairs={{0,4},{1,5},{2,6},{3,7},{4,8},{5,9},{6,10},{7,11},{8,12},{9,13},{1... | collective-permute-start | bytes 1179656 | tf_op jit(solution)/shard_map/ppermute | solution.py:314
  159.9 13.4 %collective-permute-start.26 = (bf16[2,128,128]{2,1,0:T(8,128)(2,1)S(1)}, bf16[2,128,128]{2,1,0:T(8,128)(2,1)S(1)}, u32[]{:S(2)}, u32[]{:S(2)}) collective-permute-start(bf16[2,128,128]{2,1,0:T(8,128)(2,1)S(1)} %fusion.4), channel_id=1, source_target_pairs={{0,64},{16,80},{32,96},{48,112},{64,0},{80,16},{96,32},{112,48},{1... | collective-permute-start | bytes 196616 | tf_op jit(solution)/shard_map/ppermute | solution.py:324
  163.6 15.4 %collective-permute-start.17 = (bf16[48,1024]{1,0:T(8,128)(2,1)S(1)}, bf16[48,1024]{1,0:T(8,128)(2,1)S(1)}, u32[]{:S(2)}, u32[]{:S(2)}) collective-permute-start(bf16[48,1024]{1,0:T(8,128)(2,1)S(1)} %get-tuple-element.40), channel_id=1, source_target_pairs={{0,4},{1,5},{2,6},{3,7},{4,8},{5,9},{6,10},{7,11},{8,12},{9,13},{1... | collective-permute-start | bytes 294920 | tf_op jit(solution)/shard_map/ppermute | solution.py:314
  164.6 19.5 %collective-permute-start.16 = (bf16[48,1024]{1,0:T(8,128)(2,1)S(1)}, bf16[48,1024]{1,0:T(8,128)(2,1)S(1)}, u32[]{:S(2)}, u32[]{:S(2)}) collective-permute-start(bf16[48,1024]{1,0:T(8,128)(2,1)S(1)} %get-tuple-element.41), channel_id=1, source_target_pairs={{0,8},{1,9},{2,10},{3,11},{4,12},{5,13},{6,14},{7,15},{8,0},{9,1},... | collective-permute-start | bytes 294920 | tf_op jit(solution)/shard_map/ppermute | solution.py:314
  165.5 18.6 %collective-permute-start.21 = (bf16[48,1024]{1,0:T(8,128)(2,1)S(1)}, bf16[48,1024]{1,0:T(8,128)(2,1)S(1)}, u32[]{:S(2)}, u32[]{:S(2)}) collective-permute-start(bf16[48,1024]{1,0:T(8,128)(2,1)S(1)} %get-tuple-element.42), channel_id=1, source_target_pairs={{0,3},{1,0},{2,1},{3,2},{4,7},{5,4},{6,5},{7,6},{8,11},{9,8},{10,9... | collective-permute-start | bytes 294920 | tf_op jit(solution)/shard_map/ppermute | solution.py:319
  (24 other events, 392.4 us)

commit v6 on v5

--- a/solution.py
+++ b/solution.py
@@ -353,7 +353,7 @@
     terms = [rows[:unit]] + [
         shift(rows[k * unit : (k + 1) * unit], two, SIDE - k) for k in range(1, SIDE)
     ]
-    return total(terms)
+    return terms
 
 
 def to_all(value):
@@ -391,10 +391,9 @@
 
     core = shard % 2
     m_first, m_second, mine, theirs = mixed_parts(row_start, row_span, head, core[None], home, out_proj, first, second)
-    mixed = jnp.concatenate(
-        [scatter_sum(m_first, along_y, along_x), scatter_sum(m_second, along_x, along_y)],
-        axis=1,
-    )
+    m_first = scatter_sum(m_first, along_y, along_x)
+    m_second = scatter_sum(m_second, along_x, along_y)
+    mixed = total([jnp.concatenate(pair, axis=1) for pair in zip(m_first, m_second)])
 
     chip = shard // 2
     grad_wo = add_other(mine, theirs, 1)

time: 189 us -> 190 us (level)
  waiting for transfers between devices: 72.3 us -> 76.4 us
  starting transfers between devices: 81.5 us -> 78.4 us
    ppermute x12, starting transfers between devices: 37 us -> 33.3 us  [along_y(): return lax.ppermute(value, 'head', perm)]
    ppermute x4, waiting for transfers between devices: 1.38 us -> 3.92 us  [add_other(): other = lax.ppermute(theirs, 'seq', swap)]
  transfers between devices with their start and end apart: 32 -> 32, of which waited for: 13 -> 15; matrix products, arithmetic and copies ran while one was open for 2% -> 2% of each run, Pallas kernels for 9% -> 9%
where the time goes in v6:
time: 190 us; the launch traced here: 189 us
  starting transfers between devices  78.4 us (41%)
  waiting for transfers between devices  76.4 us (40%)
  Pallas kernels  24.8 us (13%)
  other arithmetic  4.7 us (2%)
  local copies, waits for them, and re-layouts  3.6 us (2%)
    ppermute x12, waiting for transfers between devices, along_y(): return lax.ppermute(value, 'head', perm)  39 us
    ppermute x12, starting transfers between devices, along_y(): return lax.ppermute(value, 'head', perm)  33.3 us
    all_to_all x4, starting transfers between devices, to_all(): return lax.all_to_all(value, 'seq', split_axis=0, concat_axis=0, tiled=True)  24.1 us
    all_to_all x4, waiting for transfers between devices, to_all(): return lax.all_to_all(value, 'seq', split_axis=0, concat_axis=0, tiled=True)  22.7 us
    ppermute x12, starting transfers between devices, along_x(): return lax.ppermute(value, 'head', perm)  11.4 us
    ppermute x12, waiting for transfers between devices, along_x(): return lax.ppermute(value, 'head', perm)  10.8 us
    ppermute x4, starting transfers between devices, add_other(): other = lax.ppermute(theirs, 'seq', swap)  9.74 us
    pallas_call x1, Pallas kernels, forward(): pl.pallas_call(forward_kernel, out_shape=(jax.ShapeDtypeStruct(got_q.shap...  5.57 us
  transfers between devices with their start and end apart: 32, of which 15 were waited for; matrix products, arithmetic and copies ran while one was open for 2% of the time, Pallas kernels for 9%

profile of v6, /device:TPU:8, one launch (start us, length us, event | category | flops | bytes accessed | tf_op | source)
XLA Modules:
  0.0 188.9 jit_solution(7886444950700017967)
XLA Ops:
  5.0 8.7 %all-to-all-start = ((bf16[16,144,128]{2,1,0:T(8,128)(2,1)}), bf16[16,144,128]{2,1,0:T(8,128)(2,1)S(1)}, u32[]{:S(2)}, u32[]{:S(2)}) async-start(bf16[16,144,128]{2,1,0:T(8,128)(2,1)} %pack_queries.1), calls=%async_computation | async-start | bytes 1179648 | tf_op jit(solution)/shard_map/all_to_all | solution.py:360
  14.3 16.5 %all-to-all-done.q_ref = bf16[16,144,128]{2,1,0:T(8,128)(2,1)S(1)} async-done(((bf16[16,144,128]{2,1,0:T(8,128)(2,1)}), bf16[16,144,128]{2,1,0:T(8,128)(2,1)S(1)}, u32[]{:S(2)}, u32[]{:S(2)}) %all-to-all-start) | async-done | bytes 589856 | tf_op jit(solution)/shard_map/all_to_all | solution.py:360
  30.8 5.6 %forward.1 = (bf16[16,144,128]{2,1,0:T(8,128)(2,1)}, bf16[8,288,384]{2,1,0:T(8,128)(2,1)}) custom-call(s32[8]{0:T(128)S(1)} %and_select_fusion.source_ref, s32[8]{0:T(128)S(1)} %get-tuple-element.38.start_ref, s32[8]{0:T(128)S(1)} %get-tuple-element.37.count_ref, bf16[16,144,128]{2,1,0:T(8,128)(2,1)S(1)} %all-to-all-done.q_ref, ...), custom_call_target="tpu_custom_call" | custom-call | tf_op jit(solution)/shard_map/forward/pallas_call | solution.py:188
  36.4 4.6 %all-to-all-start.1 = ((bf16[16,144,128]{2,1,0:T(8,128)(2,1)}), bf16[16,144,128]{2,1,0:T(8,128)(2,1)S(1)}, u32[]{:S(2)}, u32[]{:S(2)}) async-start(bf16[16,144,128]{2,1,0:T(8,128)(2,1)} %get-tuple-element.20.att_ref), calls=%async_computation.1 | async-start | bytes 1179648 | tf_op jit(solution)/shard_map/all_to_all | solution.py:360
  41.0 2.8 %collective-permute-start.2 = (bf16[48,1024]{1,0:T(8,128)(2,1)S(1)}, bf16[48,1024]{1,0:T(8,128)(2,1)S(1)}, u32[]{:S(2)}, u32[]{:S(2)}) collective-permute-start(bf16[48,1024]{1,0:T(8,128)(2,1)S(1)} %get-tuple-element.48), channel_id=1, source_target_pairs={{0,12},{1,13},{2,14},{3,15},{4,0},{5,1},{6,2},{7,3},{8,4},{9,5},{1... | collective-permute-start | bytes 294920 | tf_op jit(solution)/shard_map/ppermute | solution.py:314
  45.6 3.5 %collective-permute-done.2 = bf16[48,1024]{1,0:T(8,128)(2,1)S(1)} collective-permute-done((bf16[48,1024]{1,0:T(8,128)(2,1)S(1)}, bf16[48,1024]{1,0:T(8,128)(2,1)S(1)}, u32[]{:S(2)}, u32[]{:S(2)}) %collective-permute-start.2) | collective-permute-done | bytes 98336 | tf_op jit(solution)/shard_map/ppermute | solution.py:314
  53.3 3.0 %collective-permute-start.8 = (bf16[48,1024]{1,0:T(8,128)(2,1)S(1)}, bf16[48,1024]{1,0:T(8,128)(2,1)S(1)}, u32[]{:S(2)}, u32[]{:S(2)}) collective-permute-start(bf16[48,1024]{1,0:T(8,128)(2,1)S(1)} %get-tuple-element.47), channel_id=1, source_target_pairs={{0,3},{1,0},{2,1},{3,2},{4,7},{5,4},{6,5},{7,6},{8,11},{9,8},{10,9... | collective-permute-start | bytes 294920 | tf_op jit(solution)/shard_map/ppermute | solution.py:319
  59.8 6.2 %collective-permute-done.8 = bf16[48,1024]{1,0:T(8,128)(2,1)S(1)} collective-permute-done((bf16[48,1024]{1,0:T(8,128)(2,1)S(1)}, bf16[48,1024]{1,0:T(8,128)(2,1)S(1)}, u32[]{:S(2)}, u32[]{:S(2)}) %collective-permute-start.8) | collective-permute-done | bytes 98336 | tf_op jit(solution)/shard_map/ppermute | solution.py:319
  72.4 5.2 %collective-permute-done.4.refs_2_ = bf16[192,1024]{1,0:T(8,128)(2,1)S(1)} collective-permute-done((bf16[192,1024]{1,0:T(8,128)(2,1)S(1)}, bf16[192,1024]{1,0:T(8,128)(2,1)S(1)}, u32[]{:S(2)}, u32[]{:S(2)}) %collective-permute-start.4) | collective-permute-done | bytes 393248 | tf_op jit(solution)/shard_map/ppermute | solution.py:319
  77.6 8.4 %collective-permute-done.3.refs_1_ = bf16[192,1024]{1,0:T(8,128)(2,1)} collective-permute-done((bf16[192,1024]{1,0:T(8,128)(2,1)S(1)}, bf16[192,1024]{1,0:T(8,128)(2,1)}, u32[]{:S(2)}, u32[]{:S(2)}) %collective-permute-start.3) | collective-permute-done | bytes 393248 | tf_op jit(solution)/shard_map/ppermute | solution.py:319
  86.0 3.6 %collective-permute-done.9.refs_5_ = bf16[192,1024]{1,0:T(8,128)(2,1)} collective-permute-done((bf16[192,1024]{1,0:T(8,128)(2,1)S(1)}, bf16[192,1024]{1,0:T(8,128)(2,1)}, u32[]{:S(2)}, u32[]{:S(2)}) %collective-permute-start.9) | collective-permute-done | bytes 393248 | tf_op jit(solution)/shard_map/ppermute | solution.py:314
  89.6 4.2 %attention_grads.1 = bf16[16,144,128]{2,1,0:T(8,128)(2,1)} custom-call(s32[16]{0:T(128)S(1)} %get-tuple-element.36.start_ref, s32[16]{0:T(128)S(1)} %get-tuple-element.35.count_ref, s32[1]{0:T(128)} %bitcast.head_ref, bf16[128,2048]{1,0:T(8,128)(2,1)S(1)} %copy-done, bf16[192,1024]{1,0:T(8,128)(2,1)S(1)} %pad_maximum_fusion.refs_0_, ...), custom_call_target="tpu_custom_call" | custom-call | tf_op jit(solution)/shard_map/attention_grads/pallas_call | solution.py:131
  93.8 5.7 %all-to-all-start.2 = ((bf16[16,144,128]{2,1,0:T(8,128)(2,1)}), bf16[16,144,128]{2,1,0:T(8,128)(2,1)S(1)}, u32[]{:S(2)}, u32[]{:S(2)}) async-start(bf16[16,144,128]{2,1,0:T(8,128)(2,1)} %attention_grads.1), calls=%async_computation.2 | async-start | bytes 1179648 | tf_op jit(solution)/shard_map/all_to_all | solution.py:360
  100.4 4.9 %mixed_parts.1 = (bf16[192,1024]{1,0:T(8,128)(2,1)}, bf16[192,1024]{1,0:T(8,128)(2,1)}, bf16[192,1024]{1,0:T(8,128)(2,1)}, bf16[192,1024]{1,0:T(8,128)(2,1)}, bf...) custom-call(s32[16]{0:T(128)S(1)} %get-tuple-element.36.start_ref, ...), custom_call_target="tpu_custom_call" | custom-call | tf_op jit(solution)/shard_map/mixed_parts/pallas_call | solution.py:294
  110.4 6.2 %all-to-all-done.2.g_ref = bf16[16,144,128]{2,1,0:T(8,128)(2,1)S(1)} async-done(((bf16[16,144,128]{2,1,0:T(8,128)(2,1)}), bf16[16,144,128]{2,1,0:T(8,128)(2,1)S(1)}, u32[]{:S(2)}, u32[]{:S(2)}) %all-to-all-start.2) | async-done | bytes 589856 | tf_op jit(solution)/shard_map/all_to_all | solution.py:360
  118.0 5.5 %backward.1 = (bf16[16,144,128]{2,1,0:T(8,128)(2,1)}, bf16[2048,128]{1,0:T(8,128)(2,1)}, bf16[2048,128]{1,0:T(8,128)(2,1)}) custom-call(s32[8]{0:T(128)S(1)} %and_select_fusion.source_ref, s32[8]{0:T(128)S(1)} %get-tuple-element.38.start_ref, s32[8]{0:T(128)S(1)} %get-tuple-element.37.count_ref, bf16[16,144,128]{2,1,0:T(8,128)(2,1)S(1)} %all-to-all-done.q_ref, ...), custom_call_target="tpu_custom_call" | custom-call | tf_op jit(solution)/shard_map/backward/pallas_call | solution.py:232
  123.6 5.1 %all-to-all-start.3 = ((bf16[16,144,128]{2,1,0:T(8,128)(2,1)}), bf16[16,144,128]{2,1,0:T(8,128)(2,1)S(1)}, u32[]{:S(2)}, u32[]{:S(2)}) async-start(bf16[16,144,128]{2,1,0:T(8,128)(2,1)} %get-tuple-element.30), calls=%async_computation.3 | async-start | bytes 1179648 | tf_op jit(solution)/shard_map/all_to_all | solution.py:360
  128.6 6.1 %collective-permute-start.12 = (bf16[192,1024]{1,0:T(8,128)(2,1)}, bf16[192,1024]{1,0:T(8,128)(2,1)S(1)}, u32[]{:S(2)}, u32[]{:S(2)}) collective-permute-start(bf16[192,1024]{1,0:T(8,128)(2,1)} %get-tuple-element.22), channel_id=1, source_target_pairs={{0,3},{1,0},{2,1},{3,2},{4,7},{5,4},{6,5},{7,6},{8,11},{9,8},{10,9... | collective-permute-start | bytes 1179656 | tf_op jit(solution)/shard_map/ppermute | solution.py:319
  134.8 6.9 %collective-permute-start.13 = (bf16[192,1024]{1,0:T(8,128)(2,1)}, bf16[192,1024]{1,0:T(8,128)(2,1)S(1)}, u32[]{:S(2)}, u32[]{:S(2)}) collective-permute-start(bf16[192,1024]{1,0:T(8,128)(2,1)} %get-tuple-element.23), channel_id=1, source_target_pairs={{0,2},{1,3},{2,0},{3,1},{4,6},{5,7},{6,4},{7,5},{8,10},{9,11},{10,... | collective-permute-start | bytes 1179656 | tf_op jit(solution)/shard_map/ppermute | solution.py:319
  143.8 6.4 %collective-permute-done.12 = bf16[192,1024]{1,0:T(8,128)(2,1)S(1)} collective-permute-done((bf16[192,1024]{1,0:T(8,128)(2,1)}, bf16[192,1024]{1,0:T(8,128)(2,1)S(1)}, u32[]{:S(2)}, u32[]{:S(2)}) %collective-permute-start.12) | collective-permute-done | bytes 393248 | tf_op jit(solution)/shard_map/ppermute | solution.py:319
  150.3 9.6 %collective-permute-done.13 = bf16[192,1024]{1,0:T(8,128)(2,1)S(1)} collective-permute-done((bf16[192,1024]{1,0:T(8,128)(2,1)}, bf16[192,1024]{1,0:T(8,128)(2,1)S(1)}, u32[]{:S(2)}, u32[]{:S(2)}) %collective-permute-start.13) | collective-permute-done | bytes 393248 | tf_op jit(solution)/shard_map/ppermute | solution.py:319
  166.2 5.0 %collective-permute-start.27 = (bf16[1,128,128]{2,1,0:T(8,128)(2,1)S(1)}, bf16[1,128,128]{2,1,0:T(8,128)(2,1)S(1)}, u32[]{:S(2)}, u32[]{:S(2)}) collective-permute-start(bf16[1,128,128]{2,1,0:T(8,128)(2,1)S(1)} %fusion.6), channel_id=1, source_target_pairs={{0,128},{16,144},{32,160},{48,176},{64,192},{80,208},{96,224},{112... | collective-permute-start | bytes 98312 | tf_op jit(solution)/shard_map/ppermute | solution.py:324
  171.6 2.5 %collective-permute-done.27 = bf16[1,128,128]{2,1,0:T(8,128)(2,1)S(1)} collective-permute-done((bf16[1,128,128]{2,1,0:T(8,128)(2,1)S(1)}, bf16[1,128,128]{2,1,0:T(8,128)(2,1)S(1)}, u32[]{:S(2)}, u32[]{:S(2)}) %collective-permute-start.27) | collective-permute-done | bytes 32800 | tf_op jit(solution)/shard_map/ppermute | solution.py:324
  174.1 9.4 %collective-permute-start.21 = (bf16[48,1024]{1,0:T(8,128)(2,1)S(1)}, bf16[48,1024]{1,0:T(8,128)(2,1)S(1)}, u32[]{:S(2)}, u32[]{:S(2)}) collective-permute-start(bf16[48,1024]{1,0:T(8,128)(2,1)S(1)} %get-tuple-element.44), channel_id=1, source_target_pairs={{0,2},{1,3},{2,0},{3,1},{4,6},{5,7},{6,4},{7,5},{8,10},{9,11},{10,... | collective-permute-start | bytes 294920 | tf_op jit(solution)/shard_map/ppermute | solution.py:319
  (100 shorter events, 42.4 us)
Async XLA Ops:
  5.0 25.8 %all-to-all-start = ((bf16[16,144,128]{2,1,0:T(8,128)(2,1)}), bf16[16,144,128]{2,1,0:T(8,128)(2,1)S(1)}, u32[]{:S(2)}, u32[]{:S(2)}) async-start(bf16[16,144,128]{2,1,0:T(8,128)(2,1)} %pack_queries.1), calls=%async_computation | async-start | bytes 1179648 | tf_op jit(solution)/shard_map/all_to_all | solution.py:360
  36.4 57.4 %all-to-all-start.1 = ((bf16[16,144,128]{2,1,0:T(8,128)(2,1)}), bf16[16,144,128]{2,1,0:T(8,128)(2,1)S(1)}, u32[]{:S(2)}, u32[]{:S(2)}) async-start(bf16[16,144,128]{2,1,0:T(8,128)(2,1)} %get-tuple-element.20.att_ref), calls=%async_computation.1 | async-start | bytes 1179648 | tf_op jit(solution)/shard_map/all_to_all | solution.py:360
  52.8 18.8 %collective-permute-start.5 = (bf16[192,1024]{1,0:T(8,128)(2,1)S(1)}, bf16[192,1024]{1,0:T(8,128)(2,1)S(1)}, u32[]{:S(2)}, u32[]{:S(2)}) collective-permute-start(bf16[192,1024]{1,0:T(8,128)(2,1)S(1)} %pad_maximum_fusion.refs_0_), channel_id=1, source_target_pairs={{0,3},{1,0},{2,1},{3,2},{4,7},{5,4},{6,5},{7,6},{8,11},{9,8},{10,9... | collective-permute-start | bytes 1179656 | tf_op jit(solution)/shard_map/ppermute | solution.py:319
  53.3 12.7 %collective-permute-start.8 = (bf16[48,1024]{1,0:T(8,128)(2,1)S(1)}, bf16[48,1024]{1,0:T(8,128)(2,1)S(1)}, u32[]{:S(2)}, u32[]{:S(2)}) collective-permute-start(bf16[48,1024]{1,0:T(8,128)(2,1)S(1)} %get-tuple-element.47), channel_id=1, source_target_pairs={{0,3},{1,0},{2,1},{3,2},{4,7},{5,4},{6,5},{7,6},{8,11},{9,8},{10,9... | collective-permute-start | bytes 294920 | tf_op jit(solution)/shard_map/ppermute | solution.py:319
  56.3 13.7 %collective-permute-start.7 = (bf16[48,1024]{1,0:T(8,128)(2,1)S(1)}, bf16[48,1024]{1,0:T(8,128)(2,1)S(1)}, u32[]{:S(2)}, u32[]{:S(2)}) collective-permute-start(bf16[48,1024]{1,0:T(8,128)(2,1)S(1)} %get-tuple-element.47), channel_id=1, source_target_pairs={{0,2},{1,3},{2,0},{3,1},{4,6},{5,7},{6,4},{7,5},{8,10},{9,11},{10,... | collective-permute-start | bytes 294920 | tf_op jit(solution)/shard_map/ppermute | solution.py:319
  56.3 13.7 %collective-permute-start.6 = (bf16[48,1024]{1,0:T(8,128)(2,1)S(1)}, bf16[48,1024]{1,0:T(8,128)(2,1)S(1)}, u32[]{:S(2)}, u32[]{:S(2)}) collective-permute-start(bf16[48,1024]{1,0:T(8,128)(2,1)S(1)} %get-tuple-element.47), channel_id=1, source_target_pairs={{0,1},{1,2},{2,3},{3,0},{4,5},{5,6},{6,7},{7,4},{8,9},{9,10},{10,1... | collective-permute-start | bytes 294920 | tf_op jit(solution)/shard_map/ppermute | solution.py:319
  58.5 19.1 %collective-permute-start.4 = (bf16[192,1024]{1,0:T(8,128)(2,1)S(1)}, bf16[192,1024]{1,0:T(8,128)(2,1)S(1)}, u32[]{:S(2)}, u32[]{:S(2)}) collective-permute-start(bf16[192,1024]{1,0:T(8,128)(2,1)S(1)} %pad_maximum_fusion.refs_0_), channel_id=1, source_target_pairs={{0,2},{1,3},{2,0},{3,1},{4,6},{5,7},{6,4},{7,5},{8,10},{9,11},{10,... | collective-permute-start | bytes 1179656 | tf_op jit(solution)/shard_map/ppermute | solution.py:319
  66.0 20.0 %collective-permute-start.3 = (bf16[192,1024]{1,0:T(8,128)(2,1)S(1)}, bf16[192,1024]{1,0:T(8,128)(2,1)}, u32[]{:S(2)}, u32[]{:S(2)}) collective-permute-start(bf16[192,1024]{1,0:T(8,128)(2,1)S(1)} %pad_maximum_fusion.refs_0_), channel_id=1, source_target_pairs={{0,1},{1,2},{2,3},{3,0},{4,5},{5,6},{6,7},{7,4},{8,9},{9,10},{10,1... | collective-permute-start | bytes 1179656 | tf_op jit(solution)/shard_map/ppermute | solution.py:319
  70.1 15.9 %collective-permute-start.11 = (bf16[192,1024]{1,0:T(8,128)(2,1)S(1)}, bf16[192,1024]{1,0:T(8,128)(2,1)}, u32[]{:S(2)}, u32[]{:S(2)}) collective-permute-start(bf16[192,1024]{1,0:T(8,128)(2,1)S(1)} %pad_maximum_fusion.1.refs_4_), channel_id=1, source_target_pairs={{0,12},{1,13},{2,14},{3,15},{4,0},{5,1},{6,2},{7,3},{8,4},{9,5},{1... | collective-permute-start | bytes 1179656 | tf_op jit(solution)/shard_map/ppermute | solution.py:314
  70.7 15.2 %collective-permute-start.10 = (bf16[192,1024]{1,0:T(8,128)(2,1)S(1)}, bf16[192,1024]{1,0:T(8,128)(2,1)}, u32[]{:S(2)}, u32[]{:S(2)}) collective-permute-start(bf16[192,1024]{1,0:T(8,128)(2,1)S(1)} %pad_maximum_fusion.1.refs_4_), channel_id=1, source_target_pairs={{0,8},{1,9},{2,10},{3,11},{4,12},{5,13},{6,14},{7,15},{8,0},{9,1},... | collective-permute-start | bytes 1179656 | tf_op jit(solution)/shard_map/ppermute | solution.py:314
  71.5 18.1 %collective-permute-start.9 = (bf16[192,1024]{1,0:T(8,128)(2,1)S(1)}, bf16[192,1024]{1,0:T(8,128)(2,1)}, u32[]{:S(2)}, u32[]{:S(2)}) collective-permute-start(bf16[192,1024]{1,0:T(8,128)(2,1)S(1)} %pad_maximum_fusion.1.refs_4_), channel_id=1, source_target_pairs={{0,4},{1,5},{2,6},{3,7},{4,8},{5,9},{6,10},{7,11},{8,12},{9,13},{1... | collective-permute-start | bytes 1179656 | tf_op jit(solution)/shard_map/ppermute | solution.py:314
  93.8 22.8 %all-to-all-start.2 = ((bf16[16,144,128]{2,1,0:T(8,128)(2,1)}), bf16[16,144,128]{2,1,0:T(8,128)(2,1)S(1)}, u32[]{:S(2)}, u32[]{:S(2)}) async-start(bf16[16,144,128]{2,1,0:T(8,128)(2,1)} %attention_grads.1), calls=%async_computation.2 | async-start | bytes 1179648 | tf_op jit(solution)/shard_map/all_to_all | solution.py:360
  108.4 35.2 %collective-permute-start.25 = (bf16[4,128,128]{2,1,0:T(8,128)(2,1)S(1)}, bf16[4,128,128]{2,1,0:T(8,128)(2,1)S(1)}, u32[]{:S(2)}, u32[]{:S(2)}) collective-permute-start(bf16[4,128,128]{2,1,0:T(8,128)(2,1)S(1)} %fusion), channel_id=1, source_target_pairs={{0,32},{16,48},{32,0},{48,16},{64,96},{80,112},{96,64},{112,80},{1... | collective-permute-start | bytes 393224 | tf_op jit(solution)/shard_map/ppermute | solution.py:324
  123.6 60.6 %all-to-all-start.3 = ((bf16[16,144,128]{2,1,0:T(8,128)(2,1)}), bf16[16,144,128]{2,1,0:T(8,128)(2,1)S(1)}, u32[]{:S(2)}, u32[]{:S(2)}) async-start(bf16[16,144,128]{2,1,0:T(8,128)(2,1)} %get-tuple-element.30), calls=%async_computation.3 | async-start | bytes 1179648 | tf_op jit(solution)/shard_map/all_to_all | solution.py:360
  128.6 21.6 %collective-permute-start.12 = (bf16[192,1024]{1,0:T(8,128)(2,1)}, bf16[192,1024]{1,0:T(8,128)(2,1)S(1)}, u32[]{:S(2)}, u32[]{:S(2)}) collective-permute-start(bf16[192,1024]{1,0:T(8,128)(2,1)} %get-tuple-element.22), channel_id=1, source_target_pairs={{0,3},{1,0},{2,1},{3,2},{4,7},{5,4},{6,5},{7,6},{8,11},{9,8},{10,9... | collective-permute-start | bytes 1179656 | tf_op jit(solution)/shard_map/ppermute | solution.py:319
  134.8 25.1 %collective-permute-start.13 = (bf16[192,1024]{1,0:T(8,128)(2,1)}, bf16[192,1024]{1,0:T(8,128)(2,1)S(1)}, u32[]{:S(2)}, u32[]{:S(2)}) collective-permute-start(bf16[192,1024]{1,0:T(8,128)(2,1)} %get-tuple-element.23), channel_id=1, source_target_pairs={{0,2},{1,3},{2,0},{3,1},{4,6},{5,7},{6,4},{7,5},{8,10},{9,11},{10,... | collective-permute-start | bytes 1179656 | tf_op jit(solution)/shard_map/ppermute | solution.py:319
  141.7 20.5 %collective-permute-start.14 = (bf16[192,1024]{1,0:T(8,128)(2,1)}, bf16[192,1024]{1,0:T(8,128)(2,1)S(1)}, u32[]{:S(2)}, u32[]{:S(2)}) collective-permute-start(bf16[192,1024]{1,0:T(8,128)(2,1)} %get-tuple-element.24), channel_id=1, source_target_pairs={{0,1},{1,2},{2,3},{3,0},{4,5},{5,6},{6,7},{7,4},{8,9},{9,10},{10,1... | collective-permute-start | bytes 1179656 | tf_op jit(solution)/shard_map/ppermute | solution.py:319
  142.6 20.0 %collective-permute-start.15 = (bf16[192,1024]{1,0:T(8,128)(2,1)}, bf16[192,1024]{1,0:T(8,128)(2,1)S(1)}, u32[]{:S(2)}, u32[]{:S(2)}) collective-permute-start(bf16[192,1024]{1,0:T(8,128)(2,1)} %get-tuple-element.26), channel_id=1, source_target_pairs={{0,12},{1,13},{2,14},{3,15},{4,0},{5,1},{6,2},{7,3},{8,4},{9,5},{1... | collective-permute-start | bytes 1179656 | tf_op jit(solution)/shard_map/ppermute | solution.py:314
  143.7 21.5 %collective-permute-start.16 = (bf16[192,1024]{1,0:T(8,128)(2,1)S(1)}, bf16[192,1024]{1,0:T(8,128)(2,1)S(1)}, u32[]{:S(2)}, u32[]{:S(2)}) collective-permute-start(bf16[192,1024]{1,0:T(8,128)(2,1)S(1)} %copy-done.14), channel_id=1, source_target_pairs={{0,8},{1,9},{2,10},{3,11},{4,12},{5,13},{6,14},{7,15},{8,0},{9,1},... | collective-permute-start | bytes 1179656 | tf_op jit(solution)/shard_map/ppermute | solution.py:314
  150.3 15.6 %collective-permute-start.17 = (bf16[192,1024]{1,0:T(8,128)(2,1)S(1)}, bf16[192,1024]{1,0:T(8,128)(2,1)S(1)}, u32[]{:S(2)}, u32[]{:S(2)}) collective-permute-start(bf16[192,1024]{1,0:T(8,128)(2,1)S(1)} %copy-done.13), channel_id=1, source_target_pairs={{0,4},{1,5},{2,6},{3,7},{4,8},{5,9},{6,10},{7,11},{8,12},{9,13},{1... | collective-permute-start | bytes 1179656 | tf_op jit(solution)/shard_map/ppermute | solution.py:314
  162.5 21.0 %collective-permute-start.22 = (bf16[48,1024]{1,0:T(8,128)(2,1)S(1)}, bf16[48,1024]{1,0:T(8,128)(2,1)S(1)}, u32[]{:S(2)}, u32[]{:S(2)}) collective-permute-start(bf16[48,1024]{1,0:T(8,128)(2,1)S(1)} %get-tuple-element.39), channel_id=1, source_target_pairs={{0,4},{1,5},{2,6},{3,7},{4,8},{5,9},{6,10},{7,11},{8,12},{9,13},{1... | collective-permute-start | bytes 294920 | tf_op jit(solution)/shard_map/ppermute | solution.py:314
  162.6 23.9 %collective-permute-start.20 = (bf16[48,1024]{1,0:T(8,128)(2,1)S(1)}, bf16[48,1024]{1,0:T(8,128)(2,1)S(1)}, u32[]{:S(2)}, u32[]{:S(2)}) collective-permute-start(bf16[48,1024]{1,0:T(8,128)(2,1)S(1)} %get-tuple-element.40), channel_id=1, source_target_pairs={{0,8},{1,9},{2,10},{3,11},{4,12},{5,13},{6,14},{7,15},{8,0},{9,1},... | collective-permute-start | bytes 294920 | tf_op jit(solution)/shard_map/ppermute | solution.py:314
  165.1 21.4 %collective-permute-start.18 = (bf16[48,1024]{1,0:T(8,128)(2,1)S(1)}, bf16[48,1024]{1,0:T(8,128)(2,1)S(1)}, u32[]{:S(2)}, u32[]{:S(2)}) collective-permute-start(bf16[48,1024]{1,0:T(8,128)(2,1)S(1)} %get-tuple-element.41), channel_id=1, source_target_pairs={{0,12},{1,13},{2,14},{3,15},{4,0},{5,1},{6,2},{7,3},{8,4},{9,5},{1... | collective-permute-start | bytes 294920 | tf_op jit(solution)/shard_map/ppermute | solution.py:314
  171.2 15.3 %collective-permute-start.23 = (bf16[48,1024]{1,0:T(8,128)(2,1)S(1)}, bf16[48,1024]{1,0:T(8,128)(2,1)S(1)}, u32[]{:S(2)}, u32[]{:S(2)}) collective-permute-start(bf16[48,1024]{1,0:T(8,128)(2,1)S(1)} %get-tuple-element.43), channel_id=1, source_target_pairs={{0,1},{1,2},{2,3},{3,0},{4,5},{5,6},{6,7},{7,4},{8,9},{9,10},{10,1... | collective-permute-start | bytes 294920 | tf_op jit(solution)/shard_map/ppermute | solution.py:319
  (24 other events, 383.5 us)
